TPU v7x, 512 devices: a whole 4x4x16 slice. The times are simulated.
512 devices in a mesh: task: 32 (over z, core), tp: 16 (over y, x).
Axes of the slice: x: 4, y: 4, z: 16, core: 2. Of those that a mesh axis runs over, the one named last changes fastest.
Arguments:
- support_x: bfloat16 [32, 384, 3584], P('task'), may hold values from -6 to 6
- adapter_a: bfloat16 [32, 3584, 64], P('task'), may hold values from -0.09375 to 0.09375
- gate_pre: bfloat16 [32, 384, 10240], P('task', None, 'tp'), may hold values from -6 to 6
- lengths: int32 [32], P('task'), may hold values from 128 to 384, as said below
- damping: float32 [32], P('task'), may hold values from 0.03 to 0.3
- down_w: bfloat16 [10240, 3584], P('tp', 'task'), may hold values from -0.0625 to 0.0625
- grad_b: float32 [32, 64, 10240], P('task', None, 'tp'), may hold values from -6 to 6
Outputs:
- solution: float32 [32, 64, 10240], P('task', None, 'tp')
- residual: float32 [32, 64, 10240], P('task', None, 'tp')
Inputs may be any that keep to these rules, and one draw needn't show every extreme that they name: `lengths`: each a multiple of 128; some task has exactly 384.
All inputs are finite; a program needn't handle non-finite values.
Results may differ from a plain program's by a relative error of at most 0.033.
Values may be sent and summed in bfloat16 or wider, within the bound.
No kernel may reach another device: no remote copies, remote signals or barrier semaphores. Data moves between devices by JAX's collectives and lax.ppermute only.
A program may use at most 64 MiB of HBM per device.

v0:
```python
import jax
import jax.numpy as jnp
from jax import lax
from jax.sharding import Mesh
from jax.sharding import PartitionSpec as P

ITERS = 2
TP = ("tp_0", "tp_1")


def cut_along(array, dim, devices):
    before, after = (array.shape[:dim], array.shape[dim + 1 :])
    return jnp.moveaxis(array.reshape(*before, devices, -1, *after), dim, 0)


def sum_at_owner(array, axis, dim):
    pieces = cut_along(array, dim, lax.axis_size(axis))
    arrived = lax.all_to_all(pieces, axis, split_axis=0, concat_axis=0, tiled=True)
    return arrived.astype(jnp.float32).sum(axis=0)


def gathered_by_axis(array, axes, dim):
    for axis in reversed(axes):
        array = lax.all_gather(array, axis, axis=dim, tiled=True)
    return array


def copy_for_each(array, axis):
    copies = jnp.broadcast_to(array, (lax.axis_size(axis), *array.shape))
    return lax.all_to_all(copies, axis, split_axis=0, concat_axis=0, tiled=True)


def over_copies(array, axis):
    everything = copy_for_each(array, axis)
    return jnp.sum(everything, axis=0)


def together(arrays, axis):
    ravelled, at, outs = (jnp.concatenate([a.reshape(-1) for a in arrays]), 0, [])
    total = over_copies(ravelled, axis)
    for a in arrays:
        outs.append(total[at : at + a.size].reshape(a.shape))
        at += a.size
    return tuple(outs)


def shards(support_x, adapter_a, gate_pre, lengths, damping, down_w, grad_b):
    down_full = lax.all_gather(down_w, "task", axis=1, tiled=True)
    features = jnp.dot(support_x[0], adapter_a[0], preferred_element_type=jnp.float32).astype(
        jnp.bfloat16
    )
    positions = lax.broadcasted_iota(jnp.int32, (gate_pre.shape[1], 1), 0)
    gated = jnp.where(
        positions < lengths[0], jax.nn.silu(gate_pre[0].astype(jnp.float32)), 0.0
    ).astype(jnp.bfloat16)
    tokens_live = lengths[0].astype(jnp.float32)
    damping_rate = damping[0]

    def transposed(mixed_rows):
        return lax.dot_general(
            mixed_rows, down_full, (((1,), (1,)), ((), ())), preferred_element_type=jnp.float32
        )

    def apply(vector):
        inner = jnp.dot(features, vector.astype(jnp.bfloat16), preferred_element_type=jnp.float32)
        active = (gated * inner).astype(jnp.bfloat16)
        mixed_share = sum_at_owner(
            jnp.dot(active, down_full, preferred_element_type=jnp.float32).astype(jnp.bfloat16),
            TP,
            0,
        ).astype(jnp.bfloat16)
        second = (gated * transposed(gathered_by_axis(mixed_share, TP, 0))).astype(jnp.bfloat16)
        product = lax.dot_general(
            features, second, (((0,), (0,)), ((), ())), preferred_element_type=jnp.float32
        )
        return product / tokens_live + damping_rate * vector

    def paired_sums(vector, image):
        return together((jnp.sum(vector * vector), jnp.sum(vector * image)), TP)

    target = grad_b[0]
    solution = jnp.zeros_like(target)
    residual = target
    image = apply(residual)
    norm_now, product = paired_sums(residual, image)
    alpha = norm_now / product
    direction, along = (residual, image)
    for step in range(ITERS):
        solution = solution + alpha * direction
        residual = residual - alpha * along
        if step + 1 < ITERS:
            image = apply(residual)
            norm_next, product = paired_sums(residual, image)
            ratio = norm_next / norm_now
            alpha = norm_next / (product - ratio * norm_next / alpha)
            direction = residual + ratio * direction
            along = image + ratio * along
            norm_now = norm_next
    return (solution[None], residual[None])


def solution(mesh):
    split = Mesh(mesh.devices.reshape(mesh.shape["task"], 4, 4), ("task", "tp_0", "tp_1"))
    return jax.shard_map(
        shards,
        mesh=split,
        in_specs=(
            P("task", None, None),
            P("task", None, None),
            P("task", None, TP),
            P("task"),
            P("task"),
            P(TP, "task"),
            P("task", None, TP),
        ),
        out_specs=(P("task", None, TP), P("task", None, TP)),
        check_vma=False,
    )
```

profile of v0, /device:TPU:32, one launch (start us, length us, event | category | flops | bytes accessed | tf_op | source)
XLA Modules:
  0.0 353.3 jit_solution(18380028138753799785)
XLA Ops:
  7.2 0.0 copy-start
  7.2 0.0 copy-start.1
  7.2 0.0 all-gather.4.cloned.1.call-start
  7.2 0.7 all-gather.4.cloned.1.call-update
  7.9 0.0 all-gather.6.cloned.1.call-start
  8.7 0.2 copy-done
  8.9 2.0 fusion.12
  11.0 78.0 %all-gather.4.cloned.1.call-done = bf16[640,3584]{0,1:T(8,128)(2,1)} async-done(((bf16[640,112]{0,1:T(8,128)(2,1)}), bf16[640,3584]{0,1:T(8,128)(2,1)}) %all-gather.4.cloned.1.call-update) | async-done | bytes 4587536 | tf_op jit(solution)/shard_map/all_gather | solution.py:48
  88.9 0.0 copy-done.1
  88.9 6.6 %convolution_convert_fusion.1 = bf16[384,3584]{1,0:T(8,128)(2,1)} fusion(bf16[640,3584]{0,1:T(8,128)(2,1)} %all-gather.4.cloned.1.call-done, bf16[384,64]{0,1:T(8,128)(2,1)S(1)} %fusion.12, f32[1,64,640]{2,1,0:T(8,128)S(1)} %copy-done.1, bf16[1,384,640]{2,1,0:T(8,128)(2,1)} %param.9, pred[384]{0:T(512)(128)(4,1)S(1)} %iota_compare_fusion), kind=kOutput, calls=%fused_computation.1 | convolution fusion | flops 1796898816 | bytes 8044928 | tf_op jit(solution)/shard_map/dot_general | solution.py:68
  95.6 42.7 %all_to_all.22 = bf16[16,24,3584]{2,1,0:T(8,128)(2,1)} all-to-all(bf16[16,24,3584]{2,1,0:T(8,128)(2,1)} %bitcast.83), channel_id=1, replica_groups=mesh['task'=32,'tp_0'=4,'tp_1'=4] {'tp_0','tp_1'}, dimensions={0} | all-to-all | bytes 5505024 | tf_op jit(solution)/shard_map/all_to_all | solution.py:18
  138.3 2.2 reduce_sum.79
  140.5 14.7 %all_gather.16 = bf16[96,3584]{1,0:T(8,128)(2,1)} all-gather(bf16[24,3584]{1,0:T(8,128)(2,1)S(1)} %reduce_sum.79), channel_id=1, replica_groups=mesh['task'=32,'tp_0'=4,'tp_1'=4] {'tp_1'}, dimensions={0}, use_global_device_ids=true | all-gather | bytes 860160 | tf_op jit(solution)/shard_map/all_gather | solution.py:24
  155.2 0.0 all-gather.6.cloned.1.call-update
  155.2 0.0 all-gather.8.cloned.1.call-start
  155.9 36.8 %all-gather.6.cloned.1.call-done = bf16[384,3584]{1,0:T(8,128)(2,1)} async-done(((bf16[96,3584]{1,0:T(8,128)(2,1)}), bf16[384,3584]{1,0:T(8,128)(2,1)}) %all-gather.6.cloned.1.call-update) | async-done | bytes 2752528 | tf_op jit(solution)/shard_map/all_gather | solution.py:24
  192.7 6.4 %fusion.21 = (f32[]{:T(128)}, f32[]{:T(128)}, f32[64,640]{1,0:T(8,128)S(1)}) fusion(f32[1,64,640]{2,1,0:T(8,128)S(1)} %copy-done.1, f32[]{:T(128)} %bitcast.81, f32[]{:T(128)S(6)} %convert_element_type.58, bf16[384,64]{0,1:T(8,128)(2,1)S(1)} %fusion.12, bf16[384,3584]{1,0:T(8,128)(2,1)} %all-gather.6.cloned.1.call-done, ...), kind=kOutput, calls=%fused_computation.34 | convolution fusion | flops 1795809280 | bytes 8208784 | tf_op jit(solution)/shard_map/dot_general | solution.py:73
  199.0 1.4 pad_maximum_fusion
  200.5 13.0 %all_to_all.23 = f32[16,1,2]{2,1,0:T(1,128)S(1)} all-to-all(f32[16,1,2]{2,1,0:T(1,128)S(1)} %broadcast_in_dim.26), channel_id=1, replica_groups=mesh['task'=32,'tp_0'=4,'tp_1'=4] {'tp_0','tp_1'}, dimensions={0} | all-to-all | bytes 256 | tf_op jit(solution)/shard_map/all_to_all | solution.py:30
  213.5 0.6 fusion.36
  215.3 6.6 %convolution_convert_fusion = bf16[384,3584]{1,0:T(8,128)(2,1)} fusion(bf16[640,3584]{0,1:T(8,128)(2,1)} %all-gather.4.cloned.1.call-done, bf16[384,64]{0,1:T(8,128)(2,1)S(1)} %fusion.12, f32[64,640]{1,0:T(8,128)S(1)} %bitcast_subtract_fusion, bf16[1,384,640]{2,1,0:T(8,128)(2,1)} %param.9, pred[384]{0:T(512)(128)(4,1)S(1)} %iota_compare_fusion), kind=kOutput, calls=%fused_computation | convolution fusion | flops 1796939776 | bytes 8044928 | tf_op jit(solution)/shard_map/dot_general | solution.py:68
  222.0 39.7 %all_to_all.24 = bf16[16,24,3584]{2,1,0:T(8,128)(2,1)} all-to-all(bf16[16,24,3584]{2,1,0:T(8,128)(2,1)} %bitcast.84), channel_id=1, replica_groups=mesh['task'=32,'tp_0'=4,'tp_1'=4] {'tp_0','tp_1'}, dimensions={0} | all-to-all | bytes 5505024 | tf_op jit(solution)/shard_map/all_to_all | solution.py:18
  261.7 2.2 reduce_sum.83
  263.9 13.9 %all_gather.18 = bf16[96,3584]{1,0:T(8,128)(2,1)} all-gather(bf16[24,3584]{1,0:T(8,128)(2,1)S(1)} %reduce_sum.83), channel_id=1, replica_groups=mesh['task'=32,'tp_0'=4,'tp_1'=4] {'tp_1'}, dimensions={0}, use_global_device_ids=true | all-gather | bytes 860160 | tf_op jit(solution)/shard_map/all_gather | solution.py:24
  277.7 0.0 all-gather.8.cloned.1.call-update
  277.7 42.3 %all-gather.8.cloned.1.call-done = bf16[384,3584]{1,0:T(8,128)(2,1)} async-done(((bf16[96,3584]{1,0:T(8,128)(2,1)}), bf16[384,3584]{1,0:T(8,128)(2,1)}) %all-gather.8.cloned.1.call-update) | async-done | bytes 2752528 | tf_op jit(solution)/shard_map/all_gather | solution.py:24
  320.1 6.4 %multiply_reduce_fusion.1 = (f32[]{:T(128)}, f32[]{:T(128)}, f32[64,640]{1,0:T(8,128)S(1)}) fusion(f32[64,640]{1,0:T(8,128)S(1)} %bitcast_subtract_fusion, f32[]{:T(128)} %bitcast.82, f32[]{:T(128)S(6)} %convert_element_type.58, bf16[384,64]{0,1:T(8,128)(2,1)S(1)} %fusion.12, bf16[384,3584]{1,0:T(8,128)(2,1)} %all-gather.8.cloned.1.call-done, ...), kind=kOutput, calls=%fused_computation.42 | convolution fusion | flops 1795809280 | bytes 8208784 | tf_op jit(solution)/shard_map/dot_general | solution.py:73
  326.5 1.3 pad_maximum_fusion.1
  327.8 13.0 %all_to_all.25 = f32[16,1,2]{2,1,0:T(1,128)S(1)} all-to-all(f32[16,1,2]{2,1,0:T(1,128)S(1)} %broadcast_in_dim.27), channel_id=1, replica_groups=mesh['task'=32,'tp_0'=4,'tp_1'=4] {'tp_0','tp_1'}, dimensions={0} | all-to-all | bytes 256 | tf_op jit(solution)/shard_map/all_to_all | solution.py:30
  340.8 0.6 fusion.35
  346.0 0.8 subtract_bitcast_fusion
  (6 shorter events, 0.1 us)
Async XLA Ops:
  7.2 1.8 copy-start
  7.2 81.8 %copy-start.1 = (f32[1,64,640]{2,1,0:T(8,128)S(1)}, f32[1,64,640]{2,1,0:T(8,128)}, u32[]{:S(2)}) copy-start(f32[1,64,640]{2,1,0:T(8,128)} %param.13) | copy-start | bytes 491524
  7.2 81.7 %all-gather.4.cloned.1.call-start = ((), (), s32[]{:S(2)}) async-start(), calls=%async_computation.4 | async-start | bytes 4730880 | tf_op jit(solution)/shard_map/all_gather | solution.py:48
  7.9 184.7 %all-gather.6.cloned.1.call-start = ((), (), s32[]{:S(2)}) async-start(), calls=%async_computation.5 | async-start | bytes 3440640 | tf_op jit(solution)/shard_map/all_gather | solution.py:24
  155.2 164.9 %all-gather.8.cloned.1.call-start = ((), (), s32[]{:S(2)}) async-start(), calls=%async_computation.6 | async-start | bytes 3440640 | tf_op jit(solution)/shard_map/all_gather | solution.py:24
Sparse Core Ops, SparseCore 0:
  10.1 78.7 all-gather.3
  155.3 37.2 all-gather.5
  277.9 42.1 all-gather.7
where the time goes:
time: 354 us; the launch traced here: 353 us
  waiting for transfers between devices  158 us (45%)
  blocking collectives  137 us (39%)
  matrix products  28 us (8%)
  between operations  21 us (6%)
  other arithmetic  7.97 us (2%)
    all_to_all x2, blocking collectives, sum_at_owner(): lax.all_to_all(pieces, axis, split_axis=0, concat_axis=0, tiled=True)  82.5 us
    all_gather x2, waiting for transfers between devices, gathered_by_axis(): array = lax.all_gather(array, axis, axis=dim, tiled=True)  79.1 us
    all_gather x1, waiting for transfers between devices, shards(): down_full = lax.all_gather(down_w, 'task', axis=1, tiled=True)  78 us
    all_gather x2, blocking collectives, gathered_by_axis(): array = lax.all_gather(array, axis, axis=dim, tiled=True)  28.6 us
    all_to_all x2, blocking collectives, copy_for_each(): return lax.all_to_all(copies, axis, split_axis=0, concat_axis=0, tiled=True)  26 us
    dot_general x2, matrix products, apply(): jnp.dot(active, down_full, preferred_element_type=jnp.float32)  13.2 us
    dot_general x2, matrix products, apply(): lax.dot_general(features, second, (((0,), (0,)), ((), ())), preferred_ele...  12.8 us
  transfers between devices with their start and end apart: 3, of which 3 were waited for; matrix products, arithmetic and copies ran while one was open for 1% of the time, Pallas kernels for 0%

commit v1 on v0

v1 whole, which is shorter than its diff:
```python
import functools

import jax
import jax.numpy as jnp
from jax import lax
from jax.experimental import pallas as pl
from jax.experimental.pallas import tpu as pltpu
from jax.sharding import Mesh
from jax.sharding import PartitionSpec as P

F32, BF16 = jnp.float32, jnp.bfloat16
HALF = ("y", "xb")
ROW = ("xa", "xb")
ALL = ("y", "xa", "xb")
EXTRA = 8
TAIL = 16
VMEM_LIMIT = 48 << 20


def product(a, b, dims):
    return lax.dot_general(a, b, (dims, ((), ())), preferred_element_type=F32)


def in_pieces(values, shape):
    row = lax.broadcasted_iota(jnp.int32, shape, 0)
    out, at = jnp.zeros(shape, F32), 0
    for value in values:
        rest = jnp.broadcast_to(value, shape)
        for _ in range(3):
            piece = rest.astype(BF16).astype(F32)
            out = jnp.where(row == at, piece, out)
            rest = rest - piece
            at += 1
    return out.astype(BF16)


def from_pieces(rows, at):
    return rows[at : at + 1] + rows[at + 1 : at + 2] + rows[at + 2 : at + 3]


def everywhere(value, shape):
    return jnp.broadcast_to(value[:, :1], shape)


def total(array):
    return jnp.sum(jnp.sum(array, axis=0, keepdims=True), axis=1, keepdims=True)


def post(message, body, scalars, rank):
    pieces = in_pieces(scalars, (EXTRA, body.shape[1]))
    for j in range(message.shape[0]):
        message[j, :rank, :] = body
        message[j, rank:, :] = pieces


def first_message(grad, message):
    g = grad[...]
    post(message, g.astype(BF16), [total(g * g)], g.shape[0])


def forward(rank, features, gated, vectors, weights, partial, acc, scalars):
    step = pl.program_id(0)
    tokens = features.shape[0]

    @pl.when(step == 0)
    def _():
        acc[...] = jnp.zeros_like(acc)
        scalars[...] = jnp.zeros_like(scalars)

    inner = product(features[...], vectors[0, :rank, :], ((1,), (0,)))
    active = (gated[0].astype(F32) * inner).astype(BF16)
    acc[...] += product(active, weights[...], ((1,), (1,)))
    scalars[...] += vectors[0, rank:, : scalars.shape[1]].astype(F32)

    @pl.when(step == pl.num_programs(0) - 1)
    def _():
        partial[:tokens, :] = acc[...].astype(BF16)
        rows = scalars[...]
        partial[tokens:, :] = in_pieces(
            [from_pieces(rows, 0), from_pieces(rows, 3)], (TAIL, rows.shape[1])
        )


def summed(own, other, tokens):
    mixed = own[:tokens, :].astype(F32) + other[:tokens, :].astype(F32)
    return mixed, own[tokens:, :].astype(F32) + other[tokens:, :].astype(F32)


def backward(rank, second_pass, *refs):
    if second_pass:
        features, gated, own, other, own_was, other_was, weights, message, mixed, norm = refs
    else:
        features, gated, own, other, weights, message, mixed, norm = refs
    step = pl.program_id(0)
    tokens = features.shape[0]

    @pl.when(step == 0)
    def _():
        value, rows = summed(own, other, tokens)
        if second_pass:
            before, rows_before = summed(own_was, other_was, tokens)
            ratio = from_pieces(rows, 0) / from_pieces(rows_before, 0)
            value = value + everywhere(ratio, value.shape) * before
        rounded = value.astype(BF16)
        mixed[...] = rounded
        norm[...] = jnp.broadcast_to(total(value * rounded.astype(F32)), norm.shape)

    back = product(mixed[...], weights[...], ((1,), (0,)))
    second = (gated[0].astype(F32) * back).astype(BF16)
    message[0, :rank, :] = product(features[...], second, ((0,), (0,))).astype(BF16)
    message[0, rank:, :] = in_pieces([norm[:1, :1]], (EXTRA, second.shape[1]))


def update(rank, live, rate, arrived, grad, own, other, message, residual, alpha):
    rows = arrived[0].astype(F32)
    for j in range(1, arrived.shape[0]):
        rows = rows + arrived[j].astype(F32)
    g = grad[...]
    tail = own[...].astype(F32) + other[...].astype(F32)
    shape = (1, g.shape[1])
    norm = everywhere(from_pieces(tail, 0), shape)
    step = norm / (from_pieces(rows[rank:], 0) / live[0] + rate[0] * norm)
    h = rows[:rank] / live[0] + rate[0] * g
    r = g - step * h
    residual[...] = r
    alpha[...] = jnp.broadcast_to(step, alpha.shape)
    post(message, r.astype(BF16), [total(r * r), total(r * g)], rank)


def finish(rank, live, rate, arrived, grad, own, other, own_was, other_was, residual, alpha, x, left):
    rows = arrived[0].astype(F32)
    for j in range(1, arrived.shape[0]):
        rows = rows + arrived[j].astype(F32)
    g, r = grad[...], residual[...]
    shape = (1, g.shape[1])
    tail = own[...].astype(F32) + other[...].astype(F32)
    tail_was = own_was[...].astype(F32) + other_was[...].astype(F32)
    norm = everywhere(from_pieces(tail, 0), shape)
    cross = everywhere(from_pieces(tail, 3), shape)
    norm_was = everywhere(from_pieces(tail_was, 0), shape)
    ratio = norm / norm_was
    length = norm + ratio * (2.0 * cross + ratio * norm_was)
    step = norm / (from_pieces(rows[rank:], 0) / live[0] + rate[0] * length)
    d = r + ratio * g
    h = rows[:rank] / live[0] + rate[0] * d
    x[...] = alpha[:1, :] * g + step * d
    left[...] = r - step * h


def whole(array_shape):
    return pl.BlockSpec(array_shape, lambda *_: (0,) * len(array_shape))


SCALAR = pl.BlockSpec(memory_space=pltpu.SMEM)


def params():
    return pltpu.CompilerParams(vmem_limit_bytes=VMEM_LIMIT)


def swapped(array):
    return lax.ppermute(array, ROW, [(0, 3), (3, 0), (1, 2), (2, 1)])


def exchanged(array):
    return lax.all_to_all(array, HALF, split_axis=0, concat_axis=0, tiled=True)


def width_block(down_w):
    members = lax.axis_size(HALF)
    units, columns = down_w.shape
    share = columns // members
    padded = -(-share // 16) * 16
    pieces = down_w.T.reshape(members // 2, 2, share, units)
    pieces = jnp.where(lax.axis_index("xa") == 1, pieces[:, ::-1], pieces)
    pieces = jnp.pad(pieces.reshape(members, share, units), ((0, 0), (0, padded - share), (0, 0)))
    mine = exchanged(pieces)
    mine = jnp.swapaxes(mine, 0, 1).reshape(padded, members * units)
    return lax.all_gather(mine, "task", axis=0, tiled=True)


def shards(support_x, adapter_a, gate_pre, lengths, damping, down_w, grad_b):
    members = lax.axis_size(HALF)
    tokens, units = gate_pre.shape[1:]
    rank = adapter_a.shape[2]
    target = grad_b[0]
    rows = rank + EXTRA
    block_message = pl.BlockSpec((1, rows, units), lambda i: (i, 0, 0))
    block_gated = pl.BlockSpec((1, tokens, units), lambda i: (i, 0, 0))
    message_shape = jax.ShapeDtypeStruct((members, rows, units), BF16)
    state = jax.ShapeDtypeStruct((rank, units), F32)

    weights = width_block(down_w)
    width = weights.shape[0]
    block_weights = pl.BlockSpec((width, units), lambda i: (0, i))

    vectors = exchanged(pl.pallas_call(first_message, out_shape=message_shape)(target))
    positions = lax.broadcasted_iota(jnp.int32, (tokens, 1), 0)
    gated = jnp.where(
        positions < lengths[0], jax.nn.silu(gate_pre[0].astype(F32)), 0.0
    ).astype(BF16)
    gated = exchanged(jnp.broadcast_to(gated, (members, tokens, units)))
    features = jnp.dot(support_x[0], adapter_a[0], preferred_element_type=F32).astype(BF16)
    live = lengths.astype(F32)
    flops = 2 * tokens * units * members * (width + rank)
    moved = 2 * units * members * (tokens + width + rows)

    cost = pl.CostEstimate(flops=flops, bytes_accessed=moved, transcendentals=0)

    partial_shape = (tokens + TAIL, width)

    def mixed_shares(vectors):
        own = pl.pallas_call(
            functools.partial(forward, rank),
            grid=(members,),
            in_specs=[whole((tokens, rank)), block_gated, block_message, block_weights],
            out_specs=whole(partial_shape),
            out_shape=jax.ShapeDtypeStruct(partial_shape, BF16),
            scratch_shapes=[pltpu.VMEM((tokens, width), F32), pltpu.VMEM((EXTRA, width), F32)],
            compiler_params=params(),
            cost_estimate=cost,
        )(features, gated, vectors, weights)
        return own, swapped(own)

    def product_shares(*shares):
        return exchanged(
            pl.pallas_call(
                functools.partial(backward, rank, len(shares) == 4),
                grid=(members,),
                in_specs=[whole((tokens, rank)), block_gated]
                + [whole(partial_shape)] * len(shares)
                + [block_weights],
                out_specs=block_message,
                out_shape=message_shape,
                scratch_shapes=[pltpu.VMEM((tokens, width), BF16), pltpu.VMEM((8, 128), F32)],
                compiler_params=params(),
                cost_estimate=cost,
            )(features, gated, *shares, weights)
        )

    tail = pl.BlockSpec((TAIL, width), lambda i: (tokens // TAIL, 0))
    full_message = whole(message_shape.shape)
    full_state = whole(state.shape)
    full_alpha = whole((8, units))

    first = mixed_shares(vectors)
    arrived = product_shares(*first)
    message, residual, alpha = pl.pallas_call(
        functools.partial(update, rank),
        grid=(1,),
        in_specs=[SCALAR, SCALAR, full_message, full_state, tail, tail],
        out_specs=[full_message, full_state, full_alpha],
        out_shape=[message_shape, state, jax.ShapeDtypeStruct((8, units), F32)],
        compiler_params=params(),
    )(live, damping, arrived, target, *first)
    second = mixed_shares(exchanged(message))
    arrived = product_shares(*second, *first)
    x, left = pl.pallas_call(
        functools.partial(finish, rank),
        grid=(1,),
        in_specs=[SCALAR, SCALAR, full_message, full_state] + [tail] * 4 + [full_state, full_alpha],
        out_specs=[full_state, full_state],
        out_shape=[state, state],
        compiler_params=params(),
    )(live, damping, arrived, target, *second, *first, residual, alpha)
    return (x[None], left[None])


def solution(mesh):
    split = Mesh(mesh.devices.reshape(mesh.shape["task"], 4, 2, 2), ("task", "y", "xa", "xb"))
    return jax.shard_map(
        shards,
        mesh=split,
        in_specs=(
            P("task", None, None),
            P("task", None, None),
            P("task", None, ALL),
            P("task"),
            P("task"),
            P(ALL, "task"),
            P("task", None, ALL),
        ),
        out_specs=(P("task", None, ALL), P("task", None, ALL)),
        check_vma=False,
    )
```

time: 354 us -> 218 us (0.62)
  the two profiles are of different devices: /device:TPU:32 before, /device:TPU:2 now
where the time goes in v1:
time: 218 us; the launch traced here: 217 us
  waiting for transfers between devices  83.5 us (38%)
  blocking collectives  42.3 us (19%)
  Pallas kernels  38.9 us (18%)
  starting transfers between devices  23.6 us (11%)
  between operations  15.5 us (7%)
  local copies, waits for them, and re-layouts  9.17 us (4%)
    all_to_all x3, waiting for transfers between devices, exchanged(): return lax.all_to_all(array, HALF, split_axis=0, concat_axis=0, tiled=True)  55.1 us
    all_to_all x3, blocking collectives, exchanged(): return lax.all_to_all(array, HALF, split_axis=0, concat_axis=0, tiled=True)  42.3 us
    pallas_call x2, Pallas kernels, product_shares(): pl.pallas_call(functools.partial(backward, rank, len(shares) == 4), grid=...  18.1 us
    ppermute x2, waiting for transfers between devices, swapped(): return lax.ppermute(array, ROW, [(0, 3), (3, 0), (1, 2), (2, 1)])  17.3 us
    pallas_call x2, Pallas kernels, mixed_shares(): pl.pallas_call(functools.partial(forward, rank), grid=(members,), in_spec...  16.6 us
    all_to_all x3, starting transfers between devices, exchanged(): return lax.all_to_all(array, HALF, split_axis=0, concat_axis=0, tiled=True)  16.4 us
    all_gather x1, waiting for transfers between devices, width_block(): return lax.all_gather(mine, 'task', axis=0, tiled=True)  11.1 us
    ppermute x2, starting transfers between devices, swapped(): return lax.ppermute(array, ROW, [(0, 3), (3, 0), (1, 2), (2, 1)])  7.19 us
  transfers between devices with their start and end apart: 6, of which 6 were waited for; matrix products, arithmetic and copies ran while one was open for 3% of the time, Pallas kernels for 1%

profile of v1, /device:TPU:2, one launch (start us, length us, event | category | flops | bytes accessed | tf_op | source)
XLA Modules:
  0.0 216.9 jit_solution(10626019808495556953)
XLA Ops:
  7.2 0.0 copy-start
  7.2 0.0 all-gather.2.cloned.1.call-start
  7.2 1.1 reshape.20
  8.4 13.9 %all_to_all.30 = bf16[8,16,640]{2,1,0:T(8,128)(2,1)S(1)} all-to-all(bf16[8,16,640]{2,1,0:T(8,128)(2,1)S(1)} %pad.4), channel_id=1, replica_groups=mesh['task'=32,'y'=4,'xa'=2,'xb'=2] {'y','xb'}, dimensions={0} | all-to-all | bytes 327680 | tf_op jit(solution)/shard_map/all_to_all | solution.py:166
  22.3 0.7 copy.16
  23.0 0.0 all-gather.2.cloned.1.call-update
  23.0 1.9 shard_map.86
  24.9 4.7 %all-to-all-start.1 = ((bf16[8,72,640]{2,1,0:T(8,128)(2,1)}), bf16[8,72,640]{2,1,0:T(8,128)(2,1)S(1)}, u32[]{:S(2)}, u32[]{:S(2)}) async-start(bf16[8,72,640]{2,1,0:T(8,128)(2,1)} %shard_map.86), calls=%async_computation.1 | async-start | bytes 1474560 | tf_op jit(solution)/shard_map/all_to_all | solution.py:166
  30.3 2.1 fusion.9
  32.4 5.9 %all-to-all-done.1.vectors = bf16[8,72,640]{2,1,0:T(8,128)(2,1)S(1)} async-done(((bf16[8,72,640]{2,1,0:T(8,128)(2,1)}), bf16[8,72,640]{2,1,0:T(8,128)(2,1)S(1)}, u32[]{:S(2)}, u32[]{:S(2)}) %all-to-all-start.1) | async-done | bytes 737312 | tf_op jit(solution)/shard_map/all_to_all | solution.py:166
  38.3 0.0 copy-start.4
  38.3 3.6 %broadcast_in_dim.23 = bf16[8,384,640]{2,1,0:T(8,128)(2,1)} broadcast(bf16[384,640]{1,0:T(8,128)(2,1)} %fusion.9), dimensions={1,2} | broadcast | bytes 4423680 | tf_op jit(solution)/shard_map/broadcast_in_dim | solution.py:202
  41.9 0.0 copy-done.4
  41.9 5.6 %all-to-all-start = ((bf16[8,384,640]{2,1,0:T(8,128)(2,1)}), bf16[8,384,640]{2,1,0:T(8,128)(2,1)}, u32[]{:S(2)}, u32[]{:S(2)}) async-start(bf16[8,384,640]{2,1,0:T(8,128)(2,1)} %broadcast_in_dim.23), calls=%async_computation | async-start | bytes 7864320 | tf_op jit(solution)/shard_map/all_to_all | solution.py:166
  47.5 0.0 copy-done
  47.5 1.9 fusion.2.features.refs_0_
  49.4 38.9 %all-to-all-done.gated.refs_1_ = bf16[8,384,640]{2,1,0:T(8,128)(2,1)} async-done(((bf16[8,384,640]{2,1,0:T(8,128)(2,1)}), bf16[8,384,640]{2,1,0:T(8,128)(2,1)}, u32[]{:S(2)}, u32[]{:S(2)}) %all-to-all-start) | async-done | bytes 3932192 | tf_op jit(solution)/shard_map/all_to_all | solution.py:166
  88.2 11.1 %all-gather.2.cloned.1.call-done.weights.refs_4_.refs_6_ = bf16[512,5120]{1,0:T(8,128)(2,1)} async-done(((bf16[16,5120]{1,0:T(8,128)(2,1)}), bf16[512,5120]{1,0:T(8,128)(2,1)}) %all-gather.2.cloned.1.call-update) | async-done | bytes 5242896 | tf_op jit(solution)/shard_map/all_gather | solution.py:179
  99.3 0.0 copy-start.5
  99.3 1.1 copy-done.5
  100.4 8.3 %shard_map.87.refs_2_.own.refs_4_.own_was = bf16[400,512]{1,0:T(8,128)(2,1)S(1)} custom-call(bf16[384,64]{1,0:T(8,128)(2,1)S(1)} %fusion.2.features.refs_0_, bf16[8,384,640]{2,1,0:T(8,128)(2,1)} %all-to-all-done.gated.refs_1_, bf16[8,72,640]{2,1,0:T(8,128)(2,1)S(1)} %copy-done.5, bf16[512,5120]{1,0:T(8,128)(2,1)} %all-gather.2.cloned.1.call-done.weights.refs_4_.refs_6_), custom_call_target="tpu_custom_call" | custom-call | flops 2264924160 | bytes 9912320 | tf_op jit(solution)/shard_map/pallas_call | solution.py:213
  108.7 0.0 copy-start.7
  108.7 3.5 %collective-permute-start = (bf16[400,512]{1,0:T(8,128)(2,1)S(1)}, bf16[400,512]{1,0:T(8,128)(2,1)S(1)}, u32[]{:S(2)}, u32[]{:S(2)}) collective-permute-start(bf16[400,512]{1,0:T(8,128)(2,1)S(1)} %shard_map.87.refs_2_.own.refs_4_.own_was), channel_id=1, source_target_pairs={{0,3},{3,0},{1,2},{2,1},{4,7},{7,4},{5,6},{6,5},{8,11},{11,8},{9,1... | collective-permute-start | bytes 1228808 | tf_op jit(solution)/shard_map/ppermute | solution.py:162
  112.2 10.1 %collective-permute-done.refs_3_.other.refs_5_.other_was = bf16[400,512]{1,0:T(8,128)(2,1)S(1)} collective-permute-done((bf16[400,512]{1,0:T(8,128)(2,1)S(1)}, bf16[400,512]{1,0:T(8,128)(2,1)S(1)}, u32[]{:S(2)}, u32[]{:S(2)}) %collective-permute-start) | collective-permute-done | bytes 409632 | tf_op jit(solution)/shard_map/ppermute | solution.py:162
  122.3 8.9 %shard_map.88 = bf16[8,72,640]{2,1,0:T(8,128)(2,1)S(1)} custom-call(bf16[384,64]{1,0:T(8,128)(2,1)S(1)} %fusion.2.features.refs_0_, bf16[8,384,640]{2,1,0:T(8,128)(2,1)} %all-to-all-done.gated.refs_1_, bf16[400,512]{1,0:T(8,128)(2,1)S(1)} %shard_map.87.refs_2_.own.refs_4_.own_was, bf16[400,512]{1,0:T(8,128)(2,1)S(1)} %collective-permute-done.refs_3_.other.refs_5_.other_was, ...), custom_call_target="tpu_custom_call" | custom-call | flops 2264924160 | bytes 9912320 | tf_op jit(solution)/shard_map/pallas_call | solution.py:227
  131.3 0.0 copy-start.1
  131.3 0.8 copy-done.1
  132.0 0.0 copy-start.6
  132.0 0.9 copy-done.6
  132.9 6.0 %all-to-all-start.3 = ((bf16[8,72,640]{2,1,0:T(8,128)(2,1)}), bf16[8,72,640]{2,1,0:T(8,128)(2,1)}, u32[]{:S(2)}, u32[]{:S(2)}) async-start(bf16[8,72,640]{2,1,0:T(8,128)(2,1)} %copy-done.6), calls=%async_computation.3 | async-start | bytes 1474560 | tf_op jit(solution)/shard_map/all_to_all | solution.py:166
  139.6 10.3 %all-to-all-done.3.arrived = bf16[8,72,640]{2,1,0:T(8,128)(2,1)} async-done(((bf16[8,72,640]{2,1,0:T(8,128)(2,1)}), bf16[8,72,640]{2,1,0:T(8,128)(2,1)}, u32[]{:S(2)}, u32[]{:S(2)}) %all-to-all-start.3) | async-done | bytes 737312 | tf_op jit(solution)/shard_map/all_to_all | solution.py:166
  150.0 0.0 copy-done.7
  150.0 0.0 copy-start.2
  150.0 1.0 copy-done.2
  151.0 1.4 shard_map.89
  152.4 14.3 %all_to_all.31.vectors = bf16[8,72,640]{2,1,0:T(8,128)(2,1)S(1)} all-to-all(bf16[8,72,640]{2,1,0:T(8,128)(2,1)S(1)} %get-tuple-element.7), channel_id=1, replica_groups=mesh['task'=32,'y'=4,'xa'=2,'xb'=2] {'y','xb'}, dimensions={0} | all-to-all | bytes 1474560 | tf_op jit(solution)/shard_map/all_to_all | solution.py:166
  166.7 0.0 copy-start.3
  166.7 8.3 %shard_map.90.refs_2_.own = bf16[400,512]{1,0:T(8,128)(2,1)S(1)} custom-call(bf16[384,64]{1,0:T(8,128)(2,1)S(1)} %fusion.2.features.refs_0_, bf16[8,384,640]{2,1,0:T(8,128)(2,1)} %all-to-all-done.gated.refs_1_, bf16[8,72,640]{2,1,0:T(8,128)(2,1)S(1)} %all_to_all.31.vectors, bf16[512,5120]{1,0:T(8,128)(2,1)} %all-gather.2.cloned.1.call-done.weights.refs_4_.refs_6_), custom_call_target="tpu_custom_call" | custom-call | flops 2264924160 | bytes 9912320 | tf_op jit(solution)/shard_map/pallas_call | solution.py:213
  175.0 3.6 %collective-permute-start.1 = (bf16[400,512]{1,0:T(8,128)(2,1)S(1)}, bf16[400,512]{1,0:T(8,128)(2,1)S(1)}, u32[]{:S(2)}, u32[]{:S(2)}) collective-permute-start(bf16[400,512]{1,0:T(8,128)(2,1)S(1)} %shard_map.90.refs_2_.own), channel_id=1, source_target_pairs={{0,3},{3,0},{1,2},{2,1},{4,7},{7,4},{5,6},{6,5},{8,11},{11,8},{9,1... | collective-permute-start | bytes 1228808 | tf_op jit(solution)/shard_map/ppermute | solution.py:162
  178.7 7.3 %collective-permute-done.1.refs_3_.other = bf16[400,512]{1,0:T(8,128)(2,1)S(1)} collective-permute-done((bf16[400,512]{1,0:T(8,128)(2,1)S(1)}, bf16[400,512]{1,0:T(8,128)(2,1)S(1)}, u32[]{:S(2)}, u32[]{:S(2)}) %collective-permute-start.1) | collective-permute-done | bytes 409632 | tf_op jit(solution)/shard_map/ppermute | solution.py:162
  185.9 0.0 copy-done.3
  186.0 9.2 %shard_map.91 = bf16[8,72,640]{2,1,0:T(8,128)(2,1)S(1)} custom-call(bf16[384,64]{1,0:T(8,128)(2,1)S(1)} %fusion.2.features.refs_0_, bf16[8,384,640]{2,1,0:T(8,128)(2,1)} %all-to-all-done.gated.refs_1_, bf16[400,512]{1,0:T(8,128)(2,1)S(1)} %shard_map.90.refs_2_.own, bf16[400,512]{1,0:T(8,128)(2,1)S(1)} %collective-permute-done.1.refs_3_.other, ...), custom_call_target="tpu_custom_call" | custom-call | flops 2264924160 | bytes 9912320 | tf_op jit(solution)/shard_map/pallas_call | solution.py:227
  195.1 14.0 %all_to_all.32.arrived = bf16[8,72,640]{2,1,0:T(8,128)(2,1)S(1)} all-to-all(bf16[8,72,640]{2,1,0:T(8,128)(2,1)S(1)} %shard_map.91), channel_id=1, replica_groups=mesh['task'=32,'y'=4,'xa'=2,'xb'=2] {'y','xb'}, dimensions={0} | all-to-all | bytes 1474560 | tf_op jit(solution)/shard_map/all_to_all | solution.py:166
  209.2 0.9 shard_map.92
  (3 shorter events, 0.1 us)
Async XLA Ops:
  7.2 40.3 %copy-start = (bf16[1,384,3584]{2,1,0:T(8,128)(2,1)S(1)}, bf16[1,384,3584]{2,1,0:T(8,128)(2,1)}, u32[]{:S(2)}) copy-start(bf16[1,384,3584]{2,1,0:T(8,128)(2,1)} %param.7) | copy-start | bytes 8257540
  7.2 92.1 %all-gather.2.cloned.1.call-start = ((), (), s32[]{:S(2)}) async-start(), calls=%async_computation.6 | async-start | bytes 5406720 | tf_op jit(solution)/shard_map/all_gather | solution.py:179
  24.9 13.4 %all-to-all-start.1 = ((bf16[8,72,640]{2,1,0:T(8,128)(2,1)}), bf16[8,72,640]{2,1,0:T(8,128)(2,1)S(1)}, u32[]{:S(2)}, u32[]{:S(2)}) async-start(bf16[8,72,640]{2,1,0:T(8,128)(2,1)} %shard_map.86), calls=%async_computation.1 | async-start | bytes 1474560 | tf_op jit(solution)/shard_map/all_to_all | solution.py:166
  38.3 3.6 %copy-start.4 = (bf16[8,72,640]{2,1,0:T(8,128)(2,1)}, bf16[8,72,640]{2,1,0:T(8,128)(2,1)S(1)}, u32[]{:S(2)}) copy-start(bf16[8,72,640]{2,1,0:T(8,128)(2,1)S(1)} %all-to-all-done.1.vectors) | copy-start | bytes 2211844
  41.9 46.4 %all-to-all-start = ((bf16[8,384,640]{2,1,0:T(8,128)(2,1)}), bf16[8,384,640]{2,1,0:T(8,128)(2,1)}, u32[]{:S(2)}, u32[]{:S(2)}) async-start(bf16[8,384,640]{2,1,0:T(8,128)(2,1)} %broadcast_in_dim.23), calls=%async_computation | async-start | bytes 7864320 | tf_op jit(solution)/shard_map/all_to_all | solution.py:166
  99.3 1.1 copy-start.5
  108.7 41.3 %copy-start.7 = (f32[1,64,640]{2,1,0:T(8,128)S(1)}, f32[1,64,640]{2,1,0:T(8,128)}, u32[]{:S(2)}) copy-start(f32[1,64,640]{2,1,0:T(8,128)} %param.13) | copy-start | bytes 491524
  108.7 13.6 %collective-permute-start = (bf16[400,512]{1,0:T(8,128)(2,1)S(1)}, bf16[400,512]{1,0:T(8,128)(2,1)S(1)}, u32[]{:S(2)}, u32[]{:S(2)}) collective-permute-start(bf16[400,512]{1,0:T(8,128)(2,1)S(1)} %shard_map.87.refs_2_.own.refs_4_.own_was), channel_id=1, source_target_pairs={{0,3},{3,0},{1,2},{2,1},{4,7},{7,4},{5,6},{6,5},{8,11},{11,8},{9,1... | collective-permute-start | bytes 1228808 | tf_op jit(solution)/shard_map/ppermute | solution.py:162
  131.3 0.8 copy-start.1
  132.0 0.9 copy-start.6
  132.9 17.0 %all-to-all-start.3 = ((bf16[8,72,640]{2,1,0:T(8,128)(2,1)}), bf16[8,72,640]{2,1,0:T(8,128)(2,1)}, u32[]{:S(2)}, u32[]{:S(2)}) async-start(bf16[8,72,640]{2,1,0:T(8,128)(2,1)} %copy-done.6), calls=%async_computation.3 | async-start | bytes 1474560 | tf_op jit(solution)/shard_map/all_to_all | solution.py:166
  150.0 1.0 copy-start.2
  166.7 19.2 %copy-start.3 = (bf16[400,512]{1,0:T(8,128)(2,1)S(1)}, bf16[400,512]{1,0:T(8,128)(2,1)}, u32[]{:S(2)}) copy-start(bf16[400,512]{1,0:T(8,128)(2,1)} %copy-done.1) | copy-start | bytes 1228804
  175.0 10.9 %collective-permute-start.1 = (bf16[400,512]{1,0:T(8,128)(2,1)S(1)}, bf16[400,512]{1,0:T(8,128)(2,1)S(1)}, u32[]{:S(2)}, u32[]{:S(2)}) collective-permute-start(bf16[400,512]{1,0:T(8,128)(2,1)S(1)} %shard_map.90.refs_2_.own), channel_id=1, source_target_pairs={{0,3},{3,0},{1,2},{2,1},{4,7},{7,4},{5,6},{6,5},{8,11},{11,8},{9,1... | collective-permute-start | bytes 1228808 | tf_op jit(solution)/shard_map/ppermute | solution.py:162
Sparse Core Ops, SparseCore 0:
  23.1 76.1 all-gather.1

commit v2 on v1

--- a/solution.py
+++ b/solution.py
@@ -14,7 +14,8 @@
 ALL = ("y", "xa", "xb")
 EXTRA = 8
 TAIL = 16
-VMEM_LIMIT = 48 << 20
+VMEM_LIMIT = 56 << 20
+TOGETHER = 2
 
 
 def product(a, b, dims):
@@ -58,19 +59,31 @@
     post(message, g.astype(BF16), [total(g * g)], g.shape[0])
 
 
-def forward(rank, features, gated, vectors, weights, partial, acc, scalars):
+def forward(rank, count, features, gated, vectors, *refs):
+    pieces, (partial, *outs) = refs[:count], refs[count:]
+    if count > 1:
+        weights, active, acc, scalars = outs
+        at = 0
+        for piece in pieces:
+            weights[at : at + piece.shape[0], :] = piece[...]
+            at += piece.shape[0]
+    else:
+        (weights,), (active, acc, scalars) = pieces, outs
     step = pl.program_id(0)
     tokens = features.shape[0]
+    units = gated.shape[2]
 
     @pl.when(step == 0)
     def _():
         acc[...] = jnp.zeros_like(acc)
         scalars[...] = jnp.zeros_like(scalars)
 
-    inner = product(features[...], vectors[0, :rank, :], ((1,), (0,)))
-    active = (gated[0].astype(F32) * inner).astype(BF16)
-    acc[...] += product(active, weights[...], ((1,), (1,)))
-    scalars[...] += vectors[0, rank:, : scalars.shape[1]].astype(F32)
+    for j in range(gated.shape[0]):
+        inner = product(features[...], vectors[j, :rank, :], ((1,), (0,)))
+        at = slice(j * units, (j + 1) * units)
+        active[:, at] = (gated[j].astype(F32) * inner).astype(BF16)
+        scalars[...] += vectors[j, rank:, : scalars.shape[1]].astype(F32)
+    acc[...] += product(active[...], weights[...], ((1,), (1,)))
 
     @pl.when(step == pl.num_programs(0) - 1)
     def _():
@@ -105,10 +118,13 @@
         mixed[...] = rounded
         norm[...] = jnp.broadcast_to(total(value * rounded.astype(F32)), norm.shape)
 
-    back = product(mixed[...], weights[...], ((1,), (0,)))
-    second = (gated[0].astype(F32) * back).astype(BF16)
-    message[0, :rank, :] = product(features[...], second, ((0,), (0,))).astype(BF16)
-    message[0, rank:, :] = in_pieces([norm[:1, :1]], (EXTRA, second.shape[1]))
+    units = gated.shape[2]
+    pieces = in_pieces([norm[:1, :1]], (EXTRA, units))
+    for j in range(gated.shape[0]):
+        back = product(mixed[...], weights[:, j * units : (j + 1) * units], ((1,), (0,)))
+        second = (gated[j].astype(F32) * back).astype(BF16)
+        message[j, :rank, :] = product(features[...], second, ((0,), (0,))).astype(BF16)
+        message[j, rank:, :] = pieces
 
 
 def update(rank, live, rate, arrived, grad, own, other, message, residual, alpha):
@@ -166,6 +182,15 @@
     return lax.all_to_all(array, HALF, split_axis=0, concat_axis=0, tiled=True)
 
 
+def shifted(array, by):
+    size = lax.axis_size("z")
+    return lax.ppermute(array, "z", [(i, (i + by) % size) for i in range(size)])
+
+
+def other_core(array):
+    return lax.ppermute(array, "c", [(0, 1), (1, 0)])
+
+
 def width_block(down_w):
     members = lax.axis_size(HALF)
     units, columns = down_w.shape
@@ -175,8 +200,18 @@
     pieces = jnp.where(lax.axis_index("xa") == 1, pieces[:, ::-1], pieces)
     pieces = jnp.pad(pieces.reshape(members, share, units), ((0, 0), (0, padded - share), (0, 0)))
     mine = exchanged(pieces)
-    mine = jnp.swapaxes(mine, 0, 1).reshape(padded, members * units)
-    return lax.all_gather(mine, "task", axis=0, tiled=True)
+    return jnp.swapaxes(mine, 0, 1).reshape(padded, members * units)
+
+
+def all_blocks(mine):
+    rows = mine.shape[0]
+    near = jnp.concatenate([mine, shifted(mine, 5), shifted(mine, -5)], axis=0)
+    up, down = shifted(near, 1), shifted(near, -1)
+    up2, down2 = shifted(up, 1), shifted(down, -1)
+    half = rows // 2
+    last = [shifted(up2[rows : rows + half], 1), shifted(down2[2 * rows + half :], -1)]
+    pieces = [near, up, down, up2, down2, *last]
+    return pieces + [other_core(piece) for piece in pieces]
 
 
 def shards(support_x, adapter_a, gate_pre, lengths, damping, down_w, grad_b):
@@ -185,14 +220,18 @@
     rank = adapter_a.shape[2]
     target = grad_b[0]
     rows = rank + EXTRA
-    block_message = pl.BlockSpec((1, rows, units), lambda i: (i, 0, 0))
-    block_gated = pl.BlockSpec((1, tokens, units), lambda i: (i, 0, 0))
+    block_message = pl.BlockSpec((TOGETHER, rows, units), lambda i: (i, 0, 0))
+    block_gated = pl.BlockSpec((TOGETHER, tokens, units), lambda i: (i, 0, 0))
+    span = TOGETHER * units
+    steps = members // TOGETHER
     message_shape = jax.ShapeDtypeStruct((members, rows, units), BF16)
     state = jax.ShapeDtypeStruct((rank, units), F32)
 
-    weights = width_block(down_w)
-    width = weights.shape[0]
-    block_weights = pl.BlockSpec((width, units), lambda i: (0, i))
+    pieces = all_blocks(width_block(down_w))
+    width = sum(piece.shape[0] for piece in pieces)
+
+    def block_weights(array):
+        return pl.BlockSpec((array.shape[0], span), lambda i: (0, i))
 
     vectors = exchanged(pl.pallas_call(first_message, out_shape=message_shape)(target))
     positions = lax.broadcasted_iota(jnp.int32, (tokens, 1), 0)
@@ -209,27 +248,37 @@
 
     partial_shape = (tokens + TAIL, width)
 
-    def mixed_shares(vectors):
-        own = pl.pallas_call(
-            functools.partial(forward, rank),
-            grid=(members,),
-            in_specs=[whole((tokens, rank)), block_gated, block_message, block_weights],
-            out_specs=whole(partial_shape),
-            out_shape=jax.ShapeDtypeStruct(partial_shape, BF16),
-            scratch_shapes=[pltpu.VMEM((tokens, width), F32), pltpu.VMEM((EXTRA, width), F32)],
+    def mixed_shares(vectors, pieces):
+        shapes = [jax.ShapeDtypeStruct(partial_shape, BF16)]
+        specs = [whole(partial_shape)]
+        if len(pieces) > 1:
+            shapes.append(jax.ShapeDtypeStruct((width, units * members), BF16))
+            specs.append(block_weights(shapes[1]))
+        own, *weights = pl.pallas_call(
+            functools.partial(forward, rank, len(pieces)),
+            grid=(steps,),
+            in_specs=[whole((tokens, rank)), block_gated, block_message]
+            + [block_weights(piece) for piece in pieces],
+            out_specs=specs,
+            out_shape=shapes,
+            scratch_shapes=[
+                pltpu.VMEM((tokens, span), BF16),
+                pltpu.VMEM((tokens, width), F32),
+                pltpu.VMEM((EXTRA, width), F32),
+            ],
             compiler_params=params(),
             cost_estimate=cost,
-        )(features, gated, vectors, weights)
-        return own, swapped(own)
-
-    def product_shares(*shares):
+        )(features, gated, vectors, *pieces)
+        return (own, swapped(own)), weights
+
+    def product_shares(weights, *shares):
         return exchanged(
             pl.pallas_call(
                 functools.partial(backward, rank, len(shares) == 4),
-                grid=(members,),
+                grid=(steps,),
                 in_specs=[whole((tokens, rank)), block_gated]
                 + [whole(partial_shape)] * len(shares)
-                + [block_weights],
+                + [block_weights(weights)],
                 out_specs=block_message,
                 out_shape=message_shape,
                 scratch_shapes=[pltpu.VMEM((tokens, width), BF16), pltpu.VMEM((8, 128), F32)],
@@ -243,8 +292,8 @@
     full_state = whole(state.shape)
     full_alpha = whole((8, units))
 
-    first = mixed_shares(vectors)
-    arrived = product_shares(*first)
+    first, (weights,) = mixed_shares(vectors, pieces)
+    arrived = product_shares(weights, *first)
     message, residual, alpha = pl.pallas_call(
         functools.partial(update, rank),
         grid=(1,),
@@ -253,8 +302,8 @@
         out_shape=[message_shape, state, jax.ShapeDtypeStruct((8, units), F32)],
         compiler_params=params(),
     )(live, damping, arrived, target, *first)
-    second = mixed_shares(exchanged(message))
-    arrived = product_shares(*second, *first)
+    second, _ = mixed_shares(exchanged(message), [weights])
+    arrived = product_shares(weights, *second, *first)
     x, left = pl.pallas_call(
         functools.partial(finish, rank),
         grid=(1,),
@@ -267,19 +316,21 @@
 
 
 def solution(mesh):
-    split = Mesh(mesh.devices.reshape(mesh.shape["task"], 4, 2, 2), ("task", "y", "xa", "xb"))
+    tasks = mesh.shape["task"]
+    split = Mesh(mesh.devices.reshape(tasks // 2, 2, 4, 2, 2), ("z", "c", "y", "xa", "xb"))
+    task = ("z", "c")
     return jax.shard_map(
         shards,
         mesh=split,
         in_specs=(
-            P("task", None, None),
-            P("task", None, None),
-            P("task", None, ALL),
-            P("task"),
-            P("task"),
-            P(ALL, "task"),
-            P("task", None, ALL),
+            P(task, None, None),
+            P(task, None, None),
+            P(task, None, ALL),
+            P(task),
+            P(task),
+            P(ALL, task),
+            P(task, None, ALL),
         ),
-        out_specs=(P("task", None, ALL), P("task", None, ALL)),
+        out_specs=(P(task, None, ALL), P(task, None, ALL)),
         check_vma=False,
     )

time: 218 us -> 241 us (1.11)
  the two profiles are of different devices: /device:TPU:2 before, /device:TPU:32 now
where the time goes in v2:
time: 241 us; the launch traced here: 240 us
  starting transfers between devices  84.8 us (35%)
  waiting for transfers between devices  67.4 us (28%)
  Pallas kernels  40.4 us (17%)
  blocking collectives  29.3 us (12%)
  local copies, waits for them, and re-layouts  10.9 us (5%)
  matrix products  2.51 us (1%)
    ppermute x8, starting transfers between devices, shifted(): return lax.ppermute(array, 'z', [(i, (i + by) % size) for i in range(size)])  43.9 us
    all_to_all x2, blocking collectives, exchanged(): return lax.all_to_all(array, HALF, split_axis=0, concat_axis=0, tiled=True)  29.3 us
    all_to_all x4, waiting for transfers between devices, exchanged(): return lax.all_to_all(array, HALF, split_axis=0, concat_axis=0, tiled=True)  24.9 us
    ppermute x8, waiting for transfers between devices, shifted(): return lax.ppermute(array, 'z', [(i, (i + by) % size) for i in range(size)])  24.5 us
    ppermute x2, waiting for transfers between devices, swapped(): return lax.ppermute(array, ROW, [(0, 3), (3, 0), (1, 2), (2, 1)])  18 us
    pallas_call x2, Pallas kernels, product_shares(): pl.pallas_call(functools.partial(backward, rank, len(shares) == 4), grid=...  17.8 us
    all_to_all x4, starting transfers between devices, exchanged(): return lax.all_to_all(array, HALF, split_axis=0, concat_axis=0, tiled=True)  17.6 us
    pallas_call x2, Pallas kernels, mixed_shares(): pl.pallas_call(functools.partial(forward, rank, len(pieces)), grid=(steps...  16.1 us
  transfers between devices with their start and end apart: 21, of which 13 were waited for; matrix products, arithmetic and copies ran while one was open for 2% of the time, Pallas kernels for 1%

profile of v2, /device:TPU:32, one launch (start us, length us, event | category | flops | bytes accessed | tf_op | source)
XLA Modules:
  0.0 239.8 jit_solution(13756011744864788942)
XLA Ops:
  0.6 1.1 reshape.20
  2.5 5.4 %all-to-all-start.2 = ((bf16[8,16,640]{2,1,0:T(8,128)(2,1)}), bf16[8,16,640]{2,1,0:T(8,128)(2,1)S(1)}, u32[]{:S(2)}, u32[]{:S(2)}) async-start(bf16[8,16,640]{2,1,0:T(8,128)(2,1)} %pad.4), calls=%async_computation.2 | async-start | bytes 327680 | tf_op jit(solution)/shard_map/all_to_all | solution.py:182
  7.9 1.9 shard_map.86
  9.8 4.9 %all-to-all-done.2 = bf16[8,16,640]{2,1,0:T(8,128)(2,1)S(1)} async-done(((bf16[8,16,640]{2,1,0:T(8,128)(2,1)}), bf16[8,16,640]{2,1,0:T(8,128)(2,1)S(1)}, u32[]{:S(2)}, u32[]{:S(2)}) %all-to-all-start.2) | async-done | bytes 163872 | tf_op jit(solution)/shard_map/all_to_all | solution.py:182
  15.4 3.5 %all-to-all-start.1 = ((bf16[8,72,640]{2,1,0:T(8,128)(2,1)}), bf16[8,72,640]{2,1,0:T(8,128)(2,1)S(1)}, u32[]{:S(2)}, u32[]{:S(2)}) async-start(bf16[8,72,640]{2,1,0:T(8,128)(2,1)} %shard_map.86), calls=%async_computation.1 | async-start | bytes 1474560 | tf_op jit(solution)/shard_map/all_to_all | solution.py:182
  19.6 2.1 fusion.9
  21.7 8.4 %all-to-all-done.1.vectors = bf16[8,72,640]{2,1,0:T(8,128)(2,1)S(1)} async-done(((bf16[8,72,640]{2,1,0:T(8,128)(2,1)}), bf16[8,72,640]{2,1,0:T(8,128)(2,1)S(1)}, u32[]{:S(2)}, u32[]{:S(2)}) %all-to-all-start.1) | async-done | bytes 737312 | tf_op jit(solution)/shard_map/all_to_all | solution.py:182
  30.2 3.5 %broadcast_in_dim.23 = bf16[8,384,640]{2,1,0:T(8,128)(2,1)} broadcast(bf16[384,640]{1,0:T(8,128)(2,1)} %fusion.9), dimensions={1,2} | broadcast | bytes 4423680 | tf_op jit(solution)/shard_map/broadcast_in_dim | solution.py:241
  33.6 4.5 %all-to-all-start = ((bf16[8,384,640]{2,1,0:T(8,128)(2,1)}), bf16[8,384,640]{2,1,0:T(8,128)(2,1)}, u32[]{:S(2)}, u32[]{:S(2)}) async-start(bf16[8,384,640]{2,1,0:T(8,128)(2,1)} %broadcast_in_dim.23), calls=%async_computation | async-start | bytes 7864320 | tf_op jit(solution)/shard_map/all_to_all | solution.py:182
  38.2 0.9 copy.16
  39.1 10.5 %collective-permute-start = (bf16[16,5120]{1,0:T(8,128)(2,1)S(1)}, bf16[16,5120]{1,0:T(8,128)(2,1)S(1)}, u32[]{:S(2)}, u32[]{:S(2)}) collective-permute-start(bf16[16,5120]{1,0:T(8,128)(2,1)S(1)} %bitcast.25), channel_id=1, source_target_pairs={{0,160},{32,192},{64,224},{96,256},{128,288},{160,320},{192,352},{... | collective-permute-start | bytes 491528 | tf_op jit(solution)/shard_map/ppermute | solution.py:187
  49.6 3.8 %collective-permute-start.1 = (bf16[16,5120]{1,0:T(8,128)(2,1)S(1)}, bf16[16,5120]{1,0:T(8,128)(2,1)S(1)}, u32[]{:S(2)}, u32[]{:S(2)}) collective-permute-start(bf16[16,5120]{1,0:T(8,128)(2,1)S(1)} %bitcast.27), channel_id=1, source_target_pairs={{0,352},{32,384},{64,416},{96,448},{128,480},{160,0},{192,32},{224... | collective-permute-start | bytes 491528 | tf_op jit(solution)/shard_map/ppermute | solution.py:187
  53.3 6.8 %collective-permute-done = bf16[16,5120]{1,0:T(8,128)(2,1)S(1)} collective-permute-done((bf16[16,5120]{1,0:T(8,128)(2,1)S(1)}, bf16[16,5120]{1,0:T(8,128)(2,1)S(1)}, u32[]{:S(2)}, u32[]{:S(2)}) %collective-permute-start) | collective-permute-done | bytes 163872 | tf_op jit(solution)/shard_map/ppermute | solution.py:187
  60.2 5.4 %collective-permute-done.1 = bf16[16,5120]{1,0:T(8,128)(2,1)S(1)} collective-permute-done((bf16[16,5120]{1,0:T(8,128)(2,1)S(1)}, bf16[16,5120]{1,0:T(8,128)(2,1)S(1)}, u32[]{:S(2)}, u32[]{:S(2)}) %collective-permute-start.1) | collective-permute-done | bytes 163872 | tf_op jit(solution)/shard_map/ppermute | solution.py:187
  65.6 7.1 %collective-permute-start.2 = (bf16[48,5120]{1,0:T(8,128)(2,1)S(1)}, bf16[48,5120]{1,0:T(8,128)(2,1)S(1)}, u32[]{:S(2)}, u32[]{:S(2)}) collective-permute-start(bf16[48,5120]{1,0:T(8,128)(2,1)S(1)} %constant_dynamic-update-slice_fusion.refs_0_), channel_id=1, source_target_pairs={{0,32},{32,64},{64,96},{96,128},{128,160},{160,192},{192,224},{224... | collective-permute-start | bytes 1474568 | tf_op jit(solution)/shard_map/ppermute | solution.py:187
  72.7 3.0 %collective-permute-start.3 = (bf16[48,5120]{1,0:T(8,128)(2,1)S(1)}, bf16[48,5120]{1,0:T(8,128)(2,1)S(1)}, u32[]{:S(2)}, u32[]{:S(2)}) collective-permute-start(bf16[48,5120]{1,0:T(8,128)(2,1)S(1)} %constant_dynamic-update-slice_fusion.refs_0_), channel_id=1, source_target_pairs={{0,480},{32,0},{64,32},{96,64},{128,96},{160,128},{192,160},{224,1... | collective-permute-start | bytes 1474568 | tf_op jit(solution)/shard_map/ppermute | solution.py:187
  75.7 4.9 %collective-permute-done.2.refs_1_ = bf16[48,5120]{1,0:T(8,128)(2,1)S(1)} collective-permute-done((bf16[48,5120]{1,0:T(8,128)(2,1)S(1)}, bf16[48,5120]{1,0:T(8,128)(2,1)S(1)}, u32[]{:S(2)}, u32[]{:S(2)}) %collective-permute-start.2) | collective-permute-done | bytes 491552 | tf_op jit(solution)/shard_map/ppermute | solution.py:187
  80.6 8.3 %collective-permute-start.4 = (bf16[48,5120]{1,0:T(8,128)(2,1)S(1)}, bf16[48,5120]{1,0:T(8,128)(2,1)S(1)}, u32[]{:S(2)}, u32[]{:S(2)}) collective-permute-start(bf16[48,5120]{1,0:T(8,128)(2,1)S(1)} %collective-permute-done.2.refs_1_), channel_id=1, source_target_pairs={{0,32},{32,64},{64,96},{96,128},{128,160},{160,192},{192,224},{224... | collective-permute-start | bytes 1474568 | tf_op jit(solution)/shard_map/ppermute | solution.py:187
  89.4 3.8 %collective-permute-start.5 = (bf16[48,5120]{1,0:T(8,128)(2,1)S(1)}, bf16[48,5120]{1,0:T(8,128)(2,1)S(1)}, u32[]{:S(2)}, u32[]{:S(2)}) collective-permute-start(bf16[48,5120]{1,0:T(8,128)(2,1)S(1)} %collective-permute-done.3.refs_2_), channel_id=1, source_target_pairs={{0,480},{32,0},{64,32},{96,64},{128,96},{160,128},{192,160},{224,1... | collective-permute-start | bytes 1474568 | tf_op jit(solution)/shard_map/ppermute | solution.py:187
  93.2 1.9 collective-permute-start.8
  95.1 2.4 %collective-permute-start.10 = (bf16[48,5120]{1,0:T(8,128)(2,1)S(1)}, bf16[48,5120]{1,0:T(8,128)(2,1)S(1)}, u32[]{:S(2)}, u32[]{:S(2)}) collective-permute-start(bf16[48,5120]{1,0:T(8,128)(2,1)S(1)} %collective-permute-done.3.refs_2_), channel_id=1, source_target_pairs={{0,16},{16,0},{1,17},{17,1},{2,18},{18,2},{3,19},{19,3},{4,20},{20... | collective-permute-start | bytes 1474568 | tf_op jit(solution)/shard_map/ppermute | solution.py:191
  97.5 1.9 collective-permute-start.9
  99.4 2.2 collective-permute-done.4.refs_3_
  101.6 1.9 collective-permute-start.11
  103.5 1.0 collective-permute-done.5.refs_4_
  104.5 1.9 collective-permute-start.12
  106.5 5.6 %collective-permute-start.6 = (bf16[8,5120]{1,0:T(8,128)(2,1)S(1)}, bf16[8,5120]{1,0:T(8,128)(2,1)S(1)}, u32[]{:S(2)}, u32[]{:S(2)}) collective-permute-start(bf16[8,5120]{1,0:T(8,128)(2,1)S(1)} %slice.8), channel_id=1, source_target_pairs={{0,32},{32,64},{64,96},{96,128},{128,160},{160,192},{192,224},{224... | collective-permute-start | bytes 245768 | tf_op jit(solution)/shard_map/ppermute | solution.py:187
  112.1 1.9 collective-permute-start.7
  114.5 1.9 collective-permute-start.13
  116.4 3.4 %collective-permute-done.7.refs_6_ = bf16[8,5120]{1,0:T(8,128)(2,1)S(1)} collective-permute-done((bf16[8,5120]{1,0:T(8,128)(2,1)S(1)}, bf16[8,5120]{1,0:T(8,128)(2,1)S(1)}, u32[]{:S(2)}, u32[]{:S(2)}) %collective-permute-start.7) | collective-permute-done | bytes 81952 | tf_op jit(solution)/shard_map/ppermute | solution.py:187
  119.8 1.9 collective-permute-start.14
  121.7 2.5 %fusion.2.features.refs_0_ = bf16[384,64]{1,0:T(8,128)(2,1)} fusion(bf16[1,384,3584]{2,1,0:T(8,128)(2,1)S(1)} %copy-done, bf16[1,3584,64]{1,2,0:T(8,128)(2,1)} %param.8), kind=kOutput, calls=%fused_computation.4 | convolution fusion | flops 176185344 | bytes 3260416 | tf_op jit(solution)/shard_map/dot_general | solution.py:242
  125.1 0.8 copy-done.14
  125.9 8.9 %shard_map.87 = (bf16[400,512]{1,0:T(8,128)(2,1)}, bf16[512,5120]{1,0:T(8,128)(2,1)}) custom-call(bf16[384,64]{1,0:T(8,128)(2,1)} %fusion.2.features.refs_0_, bf16[8,384,640]{2,1,0:T(8,128)(2,1)} %all-to-all-done.gated.refs_1_, bf16[8,72,640]{2,1,0:T(8,128)(2,1)} %copy-done.2, bf16[48,5120]{1,0:T(8,128)(2,1)} %copy-done.5, bf16[48,5120]{1,0:T(8,128)(2,1)} %copy-done.9, ...), custom_call_target="tpu_custom_call" | custom-call | flops 2264924160 | bytes 9912320 | tf_op jit(solution)/shard_map/pallas_call | solution.py:257
  134.8 4.5 %collective-permute-start.15 = (bf16[400,512]{1,0:T(8,128)(2,1)}, bf16[400,512]{1,0:T(8,128)(2,1)S(1)}, u32[]{:S(2)}, u32[]{:S(2)}) collective-permute-start(bf16[400,512]{1,0:T(8,128)(2,1)} %get-tuple-element.9.refs_2_.own.refs_4_.own_was), channel_id=1, source_target_pairs={{0,3},{3,0},{1,2},{2,1},{4,7},{7,4},{5,6},{6,5},{8,11},{11,8},{9,1... | collective-permute-start | bytes 1228808 | tf_op jit(solution)/shard_map/ppermute | solution.py:178
  139.3 10.7 %collective-permute-done.15.refs_3_.other.refs_5_.other_was = bf16[400,512]{1,0:T(8,128)(2,1)S(1)} collective-permute-done((bf16[400,512]{1,0:T(8,128)(2,1)}, bf16[400,512]{1,0:T(8,128)(2,1)S(1)}, u32[]{:S(2)}, u32[]{:S(2)}) %collective-permute-start.15) | collective-permute-done | bytes 409632 | tf_op jit(solution)/shard_map/ppermute | solution.py:178
  150.7 8.7 %shard_map.88 = bf16[8,72,640]{2,1,0:T(8,128)(2,1)} custom-call(bf16[384,64]{1,0:T(8,128)(2,1)} %fusion.2.features.refs_0_, bf16[8,384,640]{2,1,0:T(8,128)(2,1)} %all-to-all-done.gated.refs_1_, bf16[400,512]{1,0:T(8,128)(2,1)} %get-tuple-element.9.refs_2_.own.refs_4_.own_was, bf16[400,512]{1,0:T(8,128)(2,1)} %copy-done.1, ...), custom_call_target="tpu_custom_call" | custom-call | flops 2264924160 | bytes 9912320 | tf_op jit(solution)/shard_map/pallas_call | solution.py:276
  159.4 4.1 %all-to-all-start.3 = ((bf16[8,72,640]{2,1,0:T(8,128)(2,1)}), bf16[8,72,640]{2,1,0:T(8,128)(2,1)S(1)}, u32[]{:S(2)}, u32[]{:S(2)}) async-start(bf16[8,72,640]{2,1,0:T(8,128)(2,1)} %shard_map.88), calls=%async_computation.3 | async-start | bytes 1474560 | tf_op jit(solution)/shard_map/all_to_all | solution.py:182
  164.2 11.6 %all-to-all-done.3.arrived = bf16[8,72,640]{2,1,0:T(8,128)(2,1)S(1)} async-done(((bf16[8,72,640]{2,1,0:T(8,128)(2,1)}), bf16[8,72,640]{2,1,0:T(8,128)(2,1)S(1)}, u32[]{:S(2)}, u32[]{:S(2)}) %all-to-all-start.3) | async-done | bytes 737312 | tf_op jit(solution)/shard_map/all_to_all | solution.py:182
  175.7 0.9 copy-done.3
  176.6 2.4 shard_map.89
  179.0 15.3 %all_to_all.30.vectors = bf16[8,72,640]{2,1,0:T(8,128)(2,1)} all-to-all(bf16[8,72,640]{2,1,0:T(8,128)(2,1)} %get-tuple-element.11), channel_id=1, replica_groups=mesh['z'=16,'c'=2,'y'=4,'xa'=2,'xb'=2] {'y','xb'}, dimensions={0} | all-to-all | bytes 1474560 | tf_op jit(solution)/shard_map/all_to_all | solution.py:182
  194.2 7.2 %shard_map.90.refs_2_.own = bf16[400,512]{1,0:T(8,128)(2,1)} custom-call(bf16[384,64]{1,0:T(8,128)(2,1)} %fusion.2.features.refs_0_, bf16[8,384,640]{2,1,0:T(8,128)(2,1)} %all-to-all-done.gated.refs_1_, bf16[8,72,640]{2,1,0:T(8,128)(2,1)} %all_to_all.30.vectors, bf16[512,5120]{1,0:T(8,128)(2,1)} %get-tuple-element.10.refs_4_.refs_0_.refs_6_), custom_call_target="tpu_custom_call" | custom-call | flops 2264924160 | bytes 9912320 | tf_op jit(solution)/shard_map/pallas_call | solution.py:257
  201.4 4.9 %collective-permute-start.16 = (bf16[400,512]{1,0:T(8,128)(2,1)}, bf16[400,512]{1,0:T(8,128)(2,1)S(1)}, u32[]{:S(2)}, u32[]{:S(2)}) collective-permute-start(bf16[400,512]{1,0:T(8,128)(2,1)} %shard_map.90.refs_2_.own), channel_id=1, source_target_pairs={{0,3},{3,0},{1,2},{2,1},{4,7},{7,4},{5,6},{6,5},{8,11},{11,8},{9,1... | collective-permute-start | bytes 1228808 | tf_op jit(solution)/shard_map/ppermute | solution.py:178
  206.4 7.3 %collective-permute-done.16.refs_3_.other = bf16[400,512]{1,0:T(8,128)(2,1)S(1)} collective-permute-done((bf16[400,512]{1,0:T(8,128)(2,1)}, bf16[400,512]{1,0:T(8,128)(2,1)S(1)}, u32[]{:S(2)}, u32[]{:S(2)}) %collective-permute-start.16) | collective-permute-done | bytes 409632 | tf_op jit(solution)/shard_map/ppermute | solution.py:178
  214.4 9.1 %shard_map.91 = bf16[8,72,640]{2,1,0:T(8,128)(2,1)} custom-call(bf16[384,64]{1,0:T(8,128)(2,1)} %fusion.2.features.refs_0_, bf16[8,384,640]{2,1,0:T(8,128)(2,1)} %all-to-all-done.gated.refs_1_, bf16[400,512]{1,0:T(8,128)(2,1)} %shard_map.90.refs_2_.own, bf16[400,512]{1,0:T(8,128)(2,1)} %copy-done.4, ...), custom_call_target="tpu_custom_call" | custom-call | flops 2264924160 | bytes 9912320 | tf_op jit(solution)/shard_map/pallas_call | solution.py:276
  223.5 14.0 %all_to_all.31.arrived = bf16[8,72,640]{2,1,0:T(8,128)(2,1)} all-to-all(bf16[8,72,640]{2,1,0:T(8,128)(2,1)} %shard_map.91), channel_id=1, replica_groups=mesh['z'=16,'c'=2,'y'=4,'xa'=2,'xb'=2] {'y','xb'}, dimensions={0} | all-to-all | bytes 1474560 | tf_op jit(solution)/shard_map/all_to_all | solution.py:182
  237.6 2.2 shard_map.92
  (54 shorter events, 4.6 us)
Async XLA Ops:
  0.6 121.1 %copy-start = (bf16[1,384,3584]{2,1,0:T(8,128)(2,1)S(1)}, bf16[1,384,3584]{2,1,0:T(8,128)(2,1)}, u32[]{:S(2)}) copy-start(bf16[1,384,3584]{2,1,0:T(8,128)(2,1)} %param.7) | copy-start | bytes 8257540
  2.5 12.2 %all-to-all-start.2 = ((bf16[8,16,640]{2,1,0:T(8,128)(2,1)}), bf16[8,16,640]{2,1,0:T(8,128)(2,1)S(1)}, u32[]{:S(2)}, u32[]{:S(2)}) async-start(bf16[8,16,640]{2,1,0:T(8,128)(2,1)} %pad.4), calls=%async_computation.2 | async-start | bytes 327680 | tf_op jit(solution)/shard_map/all_to_all | solution.py:182
  14.7 0.7 copy-start.8
  15.4 14.8 %all-to-all-start.1 = ((bf16[8,72,640]{2,1,0:T(8,128)(2,1)}), bf16[8,72,640]{2,1,0:T(8,128)(2,1)S(1)}, u32[]{:S(2)}, u32[]{:S(2)}) async-start(bf16[8,72,640]{2,1,0:T(8,128)(2,1)} %shard_map.86), calls=%async_computation.1 | async-start | bytes 1474560 | tf_op jit(solution)/shard_map/all_to_all | solution.py:182
  30.2 3.5 %copy-start.2 = (bf16[8,72,640]{2,1,0:T(8,128)(2,1)}, bf16[8,72,640]{2,1,0:T(8,128)(2,1)S(1)}, u32[]{:S(2)}) copy-start(bf16[8,72,640]{2,1,0:T(8,128)(2,1)S(1)} %all-to-all-done.1.vectors) | copy-start | bytes 2211844
  33.6 92.2 %all-to-all-start = ((bf16[8,384,640]{2,1,0:T(8,128)(2,1)}), bf16[8,384,640]{2,1,0:T(8,128)(2,1)}, u32[]{:S(2)}, u32[]{:S(2)}) async-start(bf16[8,384,640]{2,1,0:T(8,128)(2,1)} %broadcast_in_dim.23), calls=%async_computation | async-start | bytes 7864320 | tf_op jit(solution)/shard_map/all_to_all | solution.py:182
  39.1 21.1 %collective-permute-start = (bf16[16,5120]{1,0:T(8,128)(2,1)S(1)}, bf16[16,5120]{1,0:T(8,128)(2,1)S(1)}, u32[]{:S(2)}, u32[]{:S(2)}) collective-permute-start(bf16[16,5120]{1,0:T(8,128)(2,1)S(1)} %bitcast.25), channel_id=1, source_target_pairs={{0,160},{32,192},{64,224},{96,256},{128,288},{160,320},{192,352},{... | collective-permute-start | bytes 491528 | tf_op jit(solution)/shard_map/ppermute | solution.py:187
  49.6 16.0 %collective-permute-start.1 = (bf16[16,5120]{1,0:T(8,128)(2,1)S(1)}, bf16[16,5120]{1,0:T(8,128)(2,1)S(1)}, u32[]{:S(2)}, u32[]{:S(2)}) collective-permute-start(bf16[16,5120]{1,0:T(8,128)(2,1)S(1)} %bitcast.27), channel_id=1, source_target_pairs={{0,352},{32,384},{64,416},{96,448},{128,480},{160,0},{192,32},{224... | collective-permute-start | bytes 491528 | tf_op jit(solution)/shard_map/ppermute | solution.py:187
  65.6 60.3 %copy-start.5 = (bf16[48,5120]{1,0:T(8,128)(2,1)}, bf16[48,5120]{1,0:T(8,128)(2,1)S(1)}, u32[]{:S(2)}) copy-start(bf16[48,5120]{1,0:T(8,128)(2,1)S(1)} %constant_dynamic-update-slice_fusion.refs_0_) | copy-start | bytes 1474564
  65.6 15.0 %collective-permute-start.2 = (bf16[48,5120]{1,0:T(8,128)(2,1)S(1)}, bf16[48,5120]{1,0:T(8,128)(2,1)S(1)}, u32[]{:S(2)}, u32[]{:S(2)}) collective-permute-start(bf16[48,5120]{1,0:T(8,128)(2,1)S(1)} %constant_dynamic-update-slice_fusion.refs_0_), channel_id=1, source_target_pairs={{0,32},{32,64},{64,96},{96,128},{128,160},{160,192},{192,224},{224... | collective-permute-start | bytes 1474568 | tf_op jit(solution)/shard_map/ppermute | solution.py:187
  72.7 16.6 %collective-permute-start.3 = (bf16[48,5120]{1,0:T(8,128)(2,1)S(1)}, bf16[48,5120]{1,0:T(8,128)(2,1)S(1)}, u32[]{:S(2)}, u32[]{:S(2)}) collective-permute-start(bf16[48,5120]{1,0:T(8,128)(2,1)S(1)} %constant_dynamic-update-slice_fusion.refs_0_), channel_id=1, source_target_pairs={{0,480},{32,0},{64,32},{96,64},{128,96},{160,128},{192,160},{224,1... | collective-permute-start | bytes 1474568 | tf_op jit(solution)/shard_map/ppermute | solution.py:187
  80.6 43.7 %copy-start.9 = (bf16[48,5120]{1,0:T(8,128)(2,1)}, bf16[48,5120]{1,0:T(8,128)(2,1)S(1)}, u32[]{:S(2)}) copy-start(bf16[48,5120]{1,0:T(8,128)(2,1)S(1)} %collective-permute-done.2.refs_1_) | copy-start | bytes 1474564
  80.6 21.0 %collective-permute-start.4 = (bf16[48,5120]{1,0:T(8,128)(2,1)S(1)}, bf16[48,5120]{1,0:T(8,128)(2,1)S(1)}, u32[]{:S(2)}, u32[]{:S(2)}) collective-permute-start(bf16[48,5120]{1,0:T(8,128)(2,1)S(1)} %collective-permute-done.2.refs_1_), channel_id=1, source_target_pairs={{0,32},{32,64},{64,96},{96,128},{128,160},{160,192},{192,224},{224... | collective-permute-start | bytes 1474568 | tf_op jit(solution)/shard_map/ppermute | solution.py:187
  89.3 22.8 %copy-start.10 = (bf16[48,5120]{1,0:T(8,128)(2,1)}, bf16[48,5120]{1,0:T(8,128)(2,1)S(1)}, u32[]{:S(2)}) copy-start(bf16[48,5120]{1,0:T(8,128)(2,1)S(1)} %collective-permute-done.3.refs_2_) | copy-start | bytes 1474564
  89.4 15.2 %collective-permute-start.5 = (bf16[48,5120]{1,0:T(8,128)(2,1)S(1)}, bf16[48,5120]{1,0:T(8,128)(2,1)S(1)}, u32[]{:S(2)}, u32[]{:S(2)}) collective-permute-start(bf16[48,5120]{1,0:T(8,128)(2,1)S(1)} %collective-permute-done.3.refs_2_), channel_id=1, source_target_pairs={{0,480},{32,0},{64,32},{96,64},{128,96},{160,128},{192,160},{224,1... | collective-permute-start | bytes 1474568 | tf_op jit(solution)/shard_map/ppermute | solution.py:187
  93.2 13.3 %collective-permute-start.8 = (bf16[48,5120]{1,0:T(8,128)(2,1)S(1)}, bf16[48,5120]{1,0:T(8,128)(2,1)S(1)}, u32[]{:S(2)}, u32[]{:S(2)}) collective-permute-start(bf16[48,5120]{1,0:T(8,128)(2,1)S(1)} %constant_dynamic-update-slice_fusion.refs_0_), channel_id=1, source_target_pairs={{0,16},{16,0},{1,17},{17,1},{2,18},{18,2},{3,19},{19,3},{4,20},{20... | collective-permute-start | bytes 1474568 | tf_op jit(solution)/shard_map/ppermute | solution.py:191
  95.1 17.0 %collective-permute-start.10 = (bf16[48,5120]{1,0:T(8,128)(2,1)S(1)}, bf16[48,5120]{1,0:T(8,128)(2,1)S(1)}, u32[]{:S(2)}, u32[]{:S(2)}) collective-permute-start(bf16[48,5120]{1,0:T(8,128)(2,1)S(1)} %collective-permute-done.3.refs_2_), channel_id=1, source_target_pairs={{0,16},{16,0},{1,17},{17,1},{2,18},{18,2},{3,19},{19,3},{4,20},{20... | collective-permute-start | bytes 1474568 | tf_op jit(solution)/shard_map/ppermute | solution.py:191
  97.5 26.8 %collective-permute-start.9 = (bf16[48,5120]{1,0:T(8,128)(2,1)S(1)}, bf16[48,5120]{1,0:T(8,128)(2,1)S(1)}, u32[]{:S(2)}, u32[]{:S(2)}) collective-permute-start(bf16[48,5120]{1,0:T(8,128)(2,1)S(1)} %collective-permute-done.2.refs_1_), channel_id=1, source_target_pairs={{0,16},{16,0},{1,17},{17,1},{2,18},{18,2},{3,19},{19,3},{4,20},{20... | collective-permute-start | bytes 1474568 | tf_op jit(solution)/shard_map/ppermute | solution.py:191
  101.6 4.9 %copy-start.6 = (bf16[48,5120]{1,0:T(8,128)(2,1)}, bf16[48,5120]{1,0:T(8,128)(2,1)S(1)}, u32[]{:S(2)}) copy-start(bf16[48,5120]{1,0:T(8,128)(2,1)S(1)} %collective-permute-done.4.refs_3_) | copy-start | bytes 1474564
  101.6 22.7 %collective-permute-start.11 = (bf16[48,5120]{1,0:T(8,128)(2,1)S(1)}, bf16[48,5120]{1,0:T(8,128)(2,1)S(1)}, u32[]{:S(2)}, u32[]{:S(2)}) collective-permute-start(bf16[48,5120]{1,0:T(8,128)(2,1)S(1)} %collective-permute-done.4.refs_3_), channel_id=1, source_target_pairs={{0,16},{16,0},{1,17},{17,1},{2,18},{18,2},{3,19},{19,3},{4,20},{20... | collective-permute-start | bytes 1474568 | tf_op jit(solution)/shard_map/ppermute | solution.py:191
  104.5 19.8 %copy-start.7 = (bf16[48,5120]{1,0:T(8,128)(2,1)}, bf16[48,5120]{1,0:T(8,128)(2,1)S(1)}, u32[]{:S(2)}) copy-start(bf16[48,5120]{1,0:T(8,128)(2,1)S(1)} %collective-permute-done.5.refs_4_) | copy-start | bytes 1474564
  104.5 21.4 %collective-permute-start.12 = (bf16[48,5120]{1,0:T(8,128)(2,1)S(1)}, bf16[48,5120]{1,0:T(8,128)(2,1)}, u32[]{:S(2)}, u32[]{:S(2)}) collective-permute-start(bf16[48,5120]{1,0:T(8,128)(2,1)S(1)} %collective-permute-done.5.refs_4_), channel_id=1, source_target_pairs={{0,16},{16,0},{1,17},{17,1},{2,18},{18,2},{3,19},{19,3},{4,20},{20... | collective-permute-start | bytes 1474568 | tf_op jit(solution)/shard_map/ppermute | solution.py:191
  106.5 5.6 %copy-start.11 = (bf16[48,5120]{1,0:T(8,128)(2,1)}, bf16[48,5120]{1,0:T(8,128)(2,1)S(1)}, u32[]{:S(2)}) copy-start(bf16[48,5120]{1,0:T(8,128)(2,1)S(1)} %collective-permute-done.8.refs_7_) | copy-start | bytes 1474564
  106.5 8.0 %collective-permute-start.6 = (bf16[8,5120]{1,0:T(8,128)(2,1)S(1)}, bf16[8,5120]{1,0:T(8,128)(2,1)S(1)}, u32[]{:S(2)}, u32[]{:S(2)}) collective-permute-start(bf16[8,5120]{1,0:T(8,128)(2,1)S(1)} %slice.8), channel_id=1, source_target_pairs={{0,32},{32,64},{64,96},{96,128},{128,160},{160,192},{192,224},{224... | collective-permute-start | bytes 245768 | tf_op jit(solution)/shard_map/ppermute | solution.py:187
  112.1 1.9 copy-start.12
  112.1 7.7 %collective-permute-start.7 = (bf16[8,5120]{1,0:T(8,128)(2,1)S(1)}, bf16[8,5120]{1,0:T(8,128)(2,1)S(1)}, u32[]{:S(2)}, u32[]{:S(2)}) collective-permute-start(bf16[8,5120]{1,0:T(8,128)(2,1)S(1)} %slice.9), channel_id=1, source_target_pairs={{0,480},{32,0},{64,32},{96,64},{128,96},{160,128},{192,160},{224,1... | collective-permute-start | bytes 245768 | tf_op jit(solution)/shard_map/ppermute | solution.py:187
  114.4 11.4 %copy-start.15 = (bf16[8,5120]{1,0:T(8,128)(2,1)}, bf16[8,5120]{1,0:T(8,128)(2,1)S(1)}, u32[]{:S(2)}) copy-start(bf16[8,5120]{1,0:T(8,128)(2,1)S(1)} %collective-permute-done.6.refs_5_) | copy-start | bytes 245764
  114.5 9.8 %collective-permute-start.13 = (bf16[8,5120]{1,0:T(8,128)(2,1)S(1)}, bf16[8,5120]{1,0:T(8,128)(2,1)S(1)}, u32[]{:S(2)}, u32[]{:S(2)}) collective-permute-start(bf16[8,5120]{1,0:T(8,128)(2,1)S(1)} %collective-permute-done.6.refs_5_), channel_id=1, source_target_pairs={{0,16},{16,0},{1,17},{17,1},{2,18},{18,2},{3,19},{19,3},{4,20},{20... | collective-permute-start | bytes 245768 | tf_op jit(solution)/shard_map/ppermute | solution.py:191
  119.8 6.1 %copy-start.16 = (bf16[8,5120]{1,0:T(8,128)(2,1)}, bf16[8,5120]{1,0:T(8,128)(2,1)S(1)}, u32[]{:S(2)}) copy-start(bf16[8,5120]{1,0:T(8,128)(2,1)S(1)} %collective-permute-done.7.refs_6_) | copy-start | bytes 245764
  119.8 4.5 %collective-permute-start.14 = (bf16[8,5120]{1,0:T(8,128)(2,1)S(1)}, bf16[8,5120]{1,0:T(8,128)(2,1)S(1)}, u32[]{:S(2)}, u32[]{:S(2)}) collective-permute-start(bf16[8,5120]{1,0:T(8,128)(2,1)S(1)} %collective-permute-done.7.refs_6_), channel_id=1, source_target_pairs={{0,16},{16,0},{1,17},{17,1},{2,18},{18,2},{3,19},{19,3},{4,20},{20... | collective-permute-start | bytes 245768 | tf_op jit(solution)/shard_map/ppermute | solution.py:191
  124.3 0.8 copy-start.13
  124.3 1.6 copy-start.17
  124.3 0.8 copy-start.18
  125.1 0.8 copy-start.14
  134.8 15.2 %collective-permute-start.15 = (bf16[400,512]{1,0:T(8,128)(2,1)}, bf16[400,512]{1,0:T(8,128)(2,1)S(1)}, u32[]{:S(2)}, u32[]{:S(2)}) collective-permute-start(bf16[400,512]{1,0:T(8,128)(2,1)} %get-tuple-element.9.refs_2_.own.refs_4_.own_was), channel_id=1, source_target_pairs={{0,3},{3,0},{1,2},{2,1},{4,7},{7,4},{5,6},{6,5},{8,11},{11,8},{9,1... | collective-permute-start | bytes 1228808 | tf_op jit(solution)/shard_map/ppermute | solution.py:178
  150.0 0.7 copy-start.1
  159.4 16.3 %all-to-all-start.3 = ((bf16[8,72,640]{2,1,0:T(8,128)(2,1)}), bf16[8,72,640]{2,1,0:T(8,128)(2,1)S(1)}, u32[]{:S(2)}, u32[]{:S(2)}) async-start(bf16[8,72,640]{2,1,0:T(8,128)(2,1)} %shard_map.88), calls=%async_computation.3 | async-start | bytes 1474560 | tf_op jit(solution)/shard_map/all_to_all | solution.py:182
  175.7 0.9 copy-start.3
  201.4 12.2 %collective-permute-start.16 = (bf16[400,512]{1,0:T(8,128)(2,1)}, bf16[400,512]{1,0:T(8,128)(2,1)S(1)}, u32[]{:S(2)}, u32[]{:S(2)}) collective-permute-start(bf16[400,512]{1,0:T(8,128)(2,1)} %shard_map.90.refs_2_.own), channel_id=1, source_target_pairs={{0,3},{3,0},{1,2},{2,1},{4,7},{7,4},{5,6},{6,5},{8,11},{11,8},{9,1... | collective-permute-start | bytes 1228808 | tf_op jit(solution)/shard_map/ppermute | solution.py:178
  213.6 0.8 copy-start.4

commit v3 on v2

--- a/solution.py
+++ b/solution.py
@@ -54,9 +54,20 @@
         message[j, rank:, :] = pieces
 
 
-def first_message(grad, message):
-    g = grad[...]
-    post(message, g.astype(BF16), [total(g * g)], g.shape[0])
+def pack(live, gate, grad, message, held):
+    tokens = gate.shape[0]
+    rank = grad.shape[0]
+
+    @pl.when(pl.program_id(0) == 0)
+    def _():
+        v = gate[...].astype(F32)
+        row = lax.broadcasted_iota(jnp.int32, v.shape, 0)
+        held[:tokens, :] = jnp.where(row < live[0], v / (1.0 + jnp.exp(-v)), 0.0).astype(BF16)
+        g = grad[...]
+        held[tokens : tokens + rank, :] = g.astype(BF16)
+        held[tokens + rank :, :] = in_pieces([total(g * g)], (held.shape[0] - tokens - rank, g.shape[1]))
+
+    message[0] = held[...]
 
 
 def forward(rank, count, features, gated, vectors, *refs):
@@ -82,7 +93,7 @@
         inner = product(features[...], vectors[j, :rank, :], ((1,), (0,)))
         at = slice(j * units, (j + 1) * units)
         active[:, at] = (gated[j].astype(F32) * inner).astype(BF16)
-        scalars[...] += vectors[j, rank:, : scalars.shape[1]].astype(F32)
+        scalars[...] += vectors[j, rank : rank + EXTRA, : scalars.shape[1]].astype(F32)
     acc[...] += product(active[...], weights[...], ((1,), (1,)))
 
     @pl.when(step == pl.num_programs(0) - 1)
@@ -203,14 +214,20 @@
     return jnp.swapaxes(mine, 0, 1).reshape(padded, members * units)
 
 
-def all_blocks(mine):
-    rows = mine.shape[0]
-    near = jnp.concatenate([mine, shifted(mine, 5), shifted(mine, -5)], axis=0)
+def start_blocks(mine):
+    return jnp.concatenate([mine, shifted(mine, 5), shifted(mine, -5)], axis=0)
+
+
+def all_blocks(near):
+    rows = near.shape[0] // 3
     up, down = shifted(near, 1), shifted(near, -1)
     up2, down2 = shifted(up, 1), shifted(down, -1)
-    half = rows // 2
-    last = [shifted(up2[rows : rows + half], 1), shifted(down2[2 * rows + half :], -1)]
-    pieces = [near, up, down, up2, down2, *last]
+    far = jnp.where(lax.axis_index("c") == 0, up2[rows : 2 * rows], down2[2 * rows :])
+    size = lax.axis_size("z")
+    both_ways = [(2 * i, 2 * ((i + 1) % size)) for i in range(size)]
+    both_ways += [(2 * i + 1, 2 * ((i - 1) % size) + 1) for i in range(size)]
+    last = lax.ppermute(far, ("z", "c"), both_ways)
+    pieces = [near, up, down, up2, down2, last]
     return pieces + [other_core(piece) for piece in pieces]
 
 
@@ -227,19 +244,34 @@
     message_shape = jax.ShapeDtypeStruct((members, rows, units), BF16)
     state = jax.ShapeDtypeStruct((rank, units), F32)
 
-    pieces = all_blocks(width_block(down_w))
+    first_rows = rank + 4 * EXTRA
+    packed_shape = (tokens + first_rows, units)
+    packed = pl.pallas_call(
+        pack,
+        grid=(members,),
+        in_specs=[SCALAR, whole((tokens, units)), whole((rank, units))],
+        out_specs=pl.BlockSpec((1, *packed_shape), lambda i: (i, 0, 0)),
+        out_shape=jax.ShapeDtypeStruct((members, *packed_shape), BF16),
+        scratch_shapes=[pltpu.VMEM(packed_shape, BF16)],
+        compiler_params=params(),
+        cost_estimate=pl.CostEstimate(
+            flops=8 * tokens * units,
+            bytes_accessed=2 * members * packed_shape[0] * units,
+            transcendentals=tokens * units,
+        ),
+    )(lengths, gate_pre[0], target)
+    block_first = pl.BlockSpec((TOGETHER, first_rows, units), lambda i: (i, tokens // first_rows, 0))
+    mine = width_block(down_w)
+    mine, packed = lax.optimization_barrier((mine, packed))
+    gated = exchanged(packed)
+    features = jnp.dot(support_x[0], adapter_a[0], preferred_element_type=F32).astype(BF16)
+    near, features = lax.optimization_barrier((start_blocks(mine), features))
+    pieces = all_blocks(near)
     width = sum(piece.shape[0] for piece in pieces)
 
     def block_weights(array):
         return pl.BlockSpec((array.shape[0], span), lambda i: (0, i))
 
-    vectors = exchanged(pl.pallas_call(first_message, out_shape=message_shape)(target))
-    positions = lax.broadcasted_iota(jnp.int32, (tokens, 1), 0)
-    gated = jnp.where(
-        positions < lengths[0], jax.nn.silu(gate_pre[0].astype(F32)), 0.0
-    ).astype(BF16)
-    gated = exchanged(jnp.broadcast_to(gated, (members, tokens, units)))
-    features = jnp.dot(support_x[0], adapter_a[0], preferred_element_type=F32).astype(BF16)
     live = lengths.astype(F32)
     flops = 2 * tokens * units * members * (width + rank)
     moved = 2 * units * members * (tokens + width + rows)
@@ -257,7 +289,11 @@
         own, *weights = pl.pallas_call(
             functools.partial(forward, rank, len(pieces)),
             grid=(steps,),
-            in_specs=[whole((tokens, rank)), block_gated, block_message]
+            in_specs=[
+                whole((tokens, rank)),
+                block_gated,
+                block_message if vectors is not gated else block_first,
+            ]
             + [block_weights(piece) for piece in pieces],
             out_specs=specs,
             out_shape=shapes,
@@ -292,7 +328,7 @@
     full_state = whole(state.shape)
     full_alpha = whole((8, units))
 
-    first, (weights,) = mixed_shares(vectors, pieces)
+    first, (weights,) = mixed_shares(gated, pieces)
     arrived = product_shares(weights, *first)
     message, residual, alpha = pl.pallas_call(
         functools.partial(update, rank),

time: 241 us -> 220 us (0.913)
  the two profiles are of different devices: /device:TPU:32 before, /device:TPU:96 now
where the time goes in v3:
time: 220 us; the launch traced here: 218 us
  waiting for transfers between devices  68.5 us (31%)
  starting transfers between devices  66.8 us (30%)
  Pallas kernels  43.4 us (20%)
  blocking collectives  29.3 us (13%)
  local copies, waits for them, and re-layouts  5.66 us (3%)
  between operations  2.2 us (1%)
    ppermute x6, waiting for transfers between devices, shifted(): return lax.ppermute(array, 'z', [(i, (i + by) % size) for i in range(size)])  33.2 us
    all_to_all x2, blocking collectives, exchanged(): return lax.all_to_all(array, HALF, split_axis=0, concat_axis=0, tiled=True)  29.3 us
    ppermute x6, starting transfers between devices, shifted(): return lax.ppermute(array, 'z', [(i, (i + by) % size) for i in range(size)])  27 us
    pallas_call x2, Pallas kernels, product_shares(): pl.pallas_call(functools.partial(backward, rank, len(shares) == 4), grid=...  17.8 us
    ppermute x2, waiting for transfers between devices, swapped(): return lax.ppermute(array, ROW, [(0, 3), (3, 0), (1, 2), (2, 1)])  17.5 us
    pallas_call x2, Pallas kernels, mixed_shares(): pl.pallas_call(functools.partial(forward, rank, len(pieces)), grid=(steps...  15.7 us
    all_to_all x3, starting transfers between devices, exchanged(): return lax.all_to_all(array, HALF, split_axis=0, concat_axis=0, tiled=True)  14.8 us
    ppermute x6, starting transfers between devices, other_core(): return lax.ppermute(array, 'c', [(0, 1), (1, 0)])  12.5 us
  transfers between devices with their start and end apart: 18, of which 11 were waited for; matrix products, arithmetic and copies ran while one was open for 1% of the time, Pallas kernels for 2%

profile of v3, /device:TPU:96, one launch (start us, length us, event | category | flops | bytes accessed | tf_op | source)
XLA Modules:
  0.0 218.5 jit_solution(2455470001388184387)
XLA Ops:
  0.6 0.0 copy-start
  0.7 1.1 reshape.13
  1.8 0.7 pad.4
  2.5 5.4 %all-to-all-start = ((bf16[8,16,640]{2,1,0:T(8,128)(2,1)}), bf16[8,16,640]{2,1,0:T(8,128)(2,1)S(1)}, u32[]{:S(2)}, u32[]{:S(2)}) async-start(bf16[8,16,640]{2,1,0:T(8,128)(2,1)} %pad.4), calls=%async_computation | async-start | bytes 327680 | tf_op jit(solution)/shard_map/all_to_all | solution.py:193
  8.5 5.3 %shard_map.86 = bf16[8,480,640]{2,1,0:T(8,128)(2,1)} custom-call(s32[1]{0:T(128)S(6)} %copy.17.live, bf16[384,640]{1,0:T(8,128)(2,1)} %bitcast.25, f32[64,640]{1,0:T(8,128)} %bitcast.17), custom_call_target="tpu_custom_call" | custom-call | flops 1966080 | bytes 4915200 | tf_op jit(solution)/shard_map/pallas_call | solution.py:249
  13.8 0.9 all-to-all-done
  14.7 4.9 %all-to-all-start.1 = ((bf16[8,480,640]{2,1,0:T(8,128)(2,1)}), bf16[8,480,640]{2,1,0:T(8,128)(2,1)}, u32[]{:S(2)}, u32[]{:S(2)}) async-start(bf16[8,480,640]{2,1,0:T(8,128)(2,1)} %shard_map.86), calls=%async_computation.1 | async-start | bytes 9830400 | tf_op jit(solution)/shard_map/all_to_all | solution.py:193
  19.7 11.6 %collective-permute-start = (bf16[16,5120]{1,0:T(8,128)(2,1)S(1)}, bf16[16,5120]{1,0:T(8,128)(2,1)S(1)}, u32[]{:S(2)}, u32[]{:S(2)}) collective-permute-start(bf16[16,5120]{1,0:T(8,128)(2,1)S(1)} %bitcast.22), channel_id=1, source_target_pairs={{0,160},{32,192},{64,224},{96,256},{128,288},{160,320},{192,352},{... | collective-permute-start | bytes 491528 | tf_op jit(solution)/shard_map/ppermute | solution.py:198
  31.3 1.9 collective-permute-start.1
  33.3 1.5 fusion.2.features.refs_0_
  34.8 12.8 %collective-permute-done = bf16[16,5120]{1,0:T(8,128)(2,1)S(1)} collective-permute-done((bf16[16,5120]{1,0:T(8,128)(2,1)S(1)}, bf16[16,5120]{1,0:T(8,128)(2,1)S(1)}, u32[]{:S(2)}, u32[]{:S(2)}) %collective-permute-start) | collective-permute-done | bytes 163872 | tf_op jit(solution)/shard_map/ppermute | solution.py:198
  47.6 9.2 %collective-permute-done.1 = bf16[16,5120]{1,0:T(8,128)(2,1)S(1)} collective-permute-done((bf16[16,5120]{1,0:T(8,128)(2,1)S(1)}, bf16[16,5120]{1,0:T(8,128)(2,1)S(1)}, u32[]{:S(2)}, u32[]{:S(2)}) %collective-permute-start.1) | collective-permute-done | bytes 163872 | tf_op jit(solution)/shard_map/ppermute | solution.py:198
  56.9 2.3 %collective-permute-start.2 = (bf16[48,5120]{1,0:T(8,128)(2,1)S(1)}, bf16[48,5120]{1,0:T(8,128)(2,1)}, u32[]{:S(2)}, u32[]{:S(2)}) collective-permute-start(bf16[48,5120]{1,0:T(8,128)(2,1)S(1)} %pad_maximum_fusion.refs_0_), channel_id=1, source_target_pairs={{0,32},{32,64},{64,96},{96,128},{128,160},{160,192},{192,224},{224... | collective-permute-start | bytes 1474568 | tf_op jit(solution)/shard_map/ppermute | solution.py:198
  59.2 3.5 %collective-permute-start.3 = (bf16[48,5120]{1,0:T(8,128)(2,1)S(1)}, bf16[48,5120]{1,0:T(8,128)(2,1)}, u32[]{:S(2)}, u32[]{:S(2)}) collective-permute-start(bf16[48,5120]{1,0:T(8,128)(2,1)S(1)} %pad_maximum_fusion.refs_0_), channel_id=1, source_target_pairs={{0,480},{32,0},{64,32},{96,64},{128,96},{160,128},{192,160},{224,1... | collective-permute-start | bytes 1474568 | tf_op jit(solution)/shard_map/ppermute | solution.py:198
  62.7 6.5 %collective-permute-done.2.refs_1_ = bf16[48,5120]{1,0:T(8,128)(2,1)} collective-permute-done((bf16[48,5120]{1,0:T(8,128)(2,1)S(1)}, bf16[48,5120]{1,0:T(8,128)(2,1)}, u32[]{:S(2)}, u32[]{:S(2)}) %collective-permute-start.2) | collective-permute-done | bytes 491552 | tf_op jit(solution)/shard_map/ppermute | solution.py:198
  69.3 5.7 %collective-permute-start.4 = (bf16[48,5120]{1,0:T(8,128)(2,1)}, bf16[48,5120]{1,0:T(8,128)(2,1)}, u32[]{:S(2)}, u32[]{:S(2)}) collective-permute-start(bf16[48,5120]{1,0:T(8,128)(2,1)} %collective-permute-done.2.refs_1_), channel_id=1, source_target_pairs={{0,32},{32,64},{64,96},{96,128},{128,160},{160,192},{192,224},{224... | collective-permute-start | bytes 1474568 | tf_op jit(solution)/shard_map/ppermute | solution.py:198
  75.0 1.9 collective-permute-start.5
  76.9 1.9 collective-permute-start.7
  78.8 2.4 %collective-permute-start.8 = (bf16[48,5120]{1,0:T(8,128)(2,1)}, bf16[48,5120]{1,0:T(8,128)(2,1)}, u32[]{:S(2)}, u32[]{:S(2)}) collective-permute-start(bf16[48,5120]{1,0:T(8,128)(2,1)} %collective-permute-done.2.refs_1_), channel_id=1, source_target_pairs={{0,16},{16,0},{1,17},{17,1},{2,18},{18,2},{3,19},{19,3},{4,20},{20... | collective-permute-start | bytes 1474568 | tf_op jit(solution)/shard_map/ppermute | solution.py:202
  81.3 1.9 collective-permute-start.9
  83.2 1.2 collective-permute-done.4.refs_3_
  84.4 1.9 collective-permute-start.10
  86.3 3.4 %collective-permute-done.5.refs_4_ = bf16[48,5120]{1,0:T(8,128)(2,1)} collective-permute-done((bf16[48,5120]{1,0:T(8,128)(2,1)}, bf16[48,5120]{1,0:T(8,128)(2,1)}, u32[]{:S(2)}, u32[]{:S(2)}) %collective-permute-start.5) | collective-permute-done | bytes 491552 | tf_op jit(solution)/shard_map/ppermute | solution.py:198
  89.7 1.9 collective-permute-start.11
  91.6 1.0 slice_select_fusion
  92.7 0.8 copy-done.5
  93.5 2.7 %collective-permute-start.6 = (bf16[16,5120]{1,0:T(8,128)(2,1)S(1)}, bf16[16,5120]{1,0:T(8,128)(2,1)S(1)}, u32[]{:S(2)}, u32[]{:S(2)}) collective-permute-start(bf16[16,5120]{1,0:T(8,128)(2,1)S(1)} %slice_select_fusion), channel_id=1, source_target_pairs={{0,32},{32,64},{64,96},{96,128},{128,160},{160,192},{192,224},{224... | collective-permute-start | bytes 491528 | tf_op jit(solution)/shard_map/ppermute | solution.py:229
  96.2 4.5 %collective-permute-done.6.refs_5_ = bf16[16,5120]{1,0:T(8,128)(2,1)S(1)} collective-permute-done((bf16[16,5120]{1,0:T(8,128)(2,1)S(1)}, bf16[16,5120]{1,0:T(8,128)(2,1)S(1)}, u32[]{:S(2)}, u32[]{:S(2)}) %collective-permute-start.6) | collective-permute-done | bytes 163872 | tf_op jit(solution)/shard_map/ppermute | solution.py:229
  100.7 2.5 %collective-permute-start.12 = (bf16[16,5120]{1,0:T(8,128)(2,1)S(1)}, bf16[16,5120]{1,0:T(8,128)(2,1)S(1)}, u32[]{:S(2)}, u32[]{:S(2)}) collective-permute-start(bf16[16,5120]{1,0:T(8,128)(2,1)S(1)} %collective-permute-done.6.refs_5_), channel_id=1, source_target_pairs={{0,16},{16,0},{1,17},{17,1},{2,18},{18,2},{3,19},{19,3},{4,20},{20... | collective-permute-start | bytes 491528 | tf_op jit(solution)/shard_map/ppermute | solution.py:202
  103.2 1.0 collective-permute-done.12.refs_11_
  104.2 0.7 copy-done.7
  104.9 8.6 %shard_map.87 = (bf16[400,512]{1,0:T(8,128)(2,1)}, bf16[512,5120]{1,0:T(8,128)(2,1)}) custom-call(bf16[384,64]{1,0:T(8,128)(2,1)} %fusion.2.features.refs_0_, bf16[8,480,640]{2,1,0:T(8,128)(2,1)} %all-to-all-done.1.gated.vectors.refs_1_, bf16[8,480,640]{2,1,0:T(8,128)(2,1)} %all-to-all-done.1.gated.vectors.refs_1_, bf16[48,5120]{1,0:T(8,128)(2,1)} %copy-done.3, ...), custom_call_target="tpu_custom_call" | custom-call | flops 2264924160 | bytes 9912320 | tf_op jit(solution)/shard_map/pallas_call | solution.py:289
  113.4 4.9 %collective-permute-start.13 = (bf16[400,512]{1,0:T(8,128)(2,1)}, bf16[400,512]{1,0:T(8,128)(2,1)S(1)}, u32[]{:S(2)}, u32[]{:S(2)}) collective-permute-start(bf16[400,512]{1,0:T(8,128)(2,1)} %get-tuple-element.17.refs_2_.own.refs_4_.own_was), channel_id=1, source_target_pairs={{0,3},{3,0},{1,2},{2,1},{4,7},{7,4},{5,6},{6,5},{8,11},{11,8},{9,1... | collective-permute-start | bytes 1228808 | tf_op jit(solution)/shard_map/ppermute | solution.py:189
  118.4 10.2 %collective-permute-done.13.refs_3_.other.refs_5_.other_was = bf16[400,512]{1,0:T(8,128)(2,1)S(1)} collective-permute-done((bf16[400,512]{1,0:T(8,128)(2,1)}, bf16[400,512]{1,0:T(8,128)(2,1)S(1)}, u32[]{:S(2)}, u32[]{:S(2)}) %collective-permute-start.13) | collective-permute-done | bytes 409632 | tf_op jit(solution)/shard_map/ppermute | solution.py:189
  128.6 0.8 copy-done.1
  129.3 8.6 %shard_map.88 = bf16[8,72,640]{2,1,0:T(8,128)(2,1)} custom-call(bf16[384,64]{1,0:T(8,128)(2,1)} %fusion.2.features.refs_0_, bf16[8,480,640]{2,1,0:T(8,128)(2,1)} %all-to-all-done.1.gated.vectors.refs_1_, bf16[400,512]{1,0:T(8,128)(2,1)} %get-tuple-element.17.refs_2_.own.refs_4_.own_was, bf16[400,512]{1,0:T(8,128)(2,1)} %copy-done.1, ...), custom_call_target="tpu_custom_call" | custom-call | flops 2264924160 | bytes 9912320 | tf_op jit(solution)/shard_map/pallas_call | solution.py:312
  138.0 4.5 %all-to-all-start.2 = ((bf16[8,72,640]{2,1,0:T(8,128)(2,1)}), bf16[8,72,640]{2,1,0:T(8,128)(2,1)S(1)}, u32[]{:S(2)}, u32[]{:S(2)}) async-start(bf16[8,72,640]{2,1,0:T(8,128)(2,1)} %shard_map.88), calls=%async_computation.2 | async-start | bytes 1474560 | tf_op jit(solution)/shard_map/all_to_all | solution.py:193
  143.1 11.4 %all-to-all-done.2.arrived = bf16[8,72,640]{2,1,0:T(8,128)(2,1)S(1)} async-done(((bf16[8,72,640]{2,1,0:T(8,128)(2,1)}), bf16[8,72,640]{2,1,0:T(8,128)(2,1)S(1)}, u32[]{:S(2)}, u32[]{:S(2)}) %all-to-all-start.2) | async-done | bytes 737312 | tf_op jit(solution)/shard_map/all_to_all | solution.py:193
  154.5 0.8 copy-done.2
  155.4 2.4 %shard_map.89 = (bf16[8,72,640]{2,1,0:T(8,128)(2,1)}, f32[64,640]{1,0:T(8,128)}, f32[8,640]{1,0:T(8,128)}) custom-call(f32[1]{0:T(128)S(6)} %convert_element_type.8.live, f32[1]{0:T(128)S(6)} %copy.18.rate, bf16[8,72,640]{2,1,0:T(8,128)(2,1)} %copy-done.2, f32[64,640]{1,0:T(8,128)} %bitcast.18, ...), custom_call_target="tpu_custom_call" | custom-call | tf_op jit(solution)/shard_map/pallas_call | solution.py:333
  157.7 15.3 %all_to_all.25.vectors = bf16[8,72,640]{2,1,0:T(8,128)(2,1)} all-to-all(bf16[8,72,640]{2,1,0:T(8,128)(2,1)} %get-tuple-element.19), channel_id=1, replica_groups=mesh['z'=16,'c'=2,'y'=4,'xa'=2,'xb'=2] {'y','xb'}, dimensions={0} | all-to-all | bytes 1474560 | tf_op jit(solution)/shard_map/all_to_all | solution.py:193
  173.0 7.2 %shard_map.90.refs_2_.own = bf16[400,512]{1,0:T(8,128)(2,1)} custom-call(bf16[384,64]{1,0:T(8,128)(2,1)} %fusion.2.features.refs_0_, bf16[8,480,640]{2,1,0:T(8,128)(2,1)} %all-to-all-done.1.gated.vectors.refs_1_, bf16[8,72,640]{2,1,0:T(8,128)(2,1)} %all_to_all.25.vectors, bf16[512,5120]{1,0:T(8,128)(2,1)} %get-tuple-element.18.refs_4_.refs_0_.refs_6_), custom_call_target="tpu_custom_call" | custom-call | flops 2264924160 | bytes 9912320 | tf_op jit(solution)/shard_map/pallas_call | solution.py:289
  180.2 4.9 %collective-permute-start.14 = (bf16[400,512]{1,0:T(8,128)(2,1)}, bf16[400,512]{1,0:T(8,128)(2,1)S(1)}, u32[]{:S(2)}, u32[]{:S(2)}) collective-permute-start(bf16[400,512]{1,0:T(8,128)(2,1)} %shard_map.90.refs_2_.own), channel_id=1, source_target_pairs={{0,3},{3,0},{1,2},{2,1},{4,7},{7,4},{5,6},{6,5},{8,11},{11,8},{9,1... | collective-permute-start | bytes 1228808 | tf_op jit(solution)/shard_map/ppermute | solution.py:189
  185.1 7.3 %collective-permute-done.14.refs_3_.other = bf16[400,512]{1,0:T(8,128)(2,1)S(1)} collective-permute-done((bf16[400,512]{1,0:T(8,128)(2,1)}, bf16[400,512]{1,0:T(8,128)(2,1)S(1)}, u32[]{:S(2)}, u32[]{:S(2)}) %collective-permute-start.14) | collective-permute-done | bytes 409632 | tf_op jit(solution)/shard_map/ppermute | solution.py:189
  192.4 0.7 copy-done.4
  193.1 9.1 %shard_map.91 = bf16[8,72,640]{2,1,0:T(8,128)(2,1)} custom-call(bf16[384,64]{1,0:T(8,128)(2,1)} %fusion.2.features.refs_0_, bf16[8,480,640]{2,1,0:T(8,128)(2,1)} %all-to-all-done.1.gated.vectors.refs_1_, bf16[400,512]{1,0:T(8,128)(2,1)} %shard_map.90.refs_2_.own, bf16[400,512]{1,0:T(8,128)(2,1)} %copy-done.4, ...), custom_call_target="tpu_custom_call" | custom-call | flops 2264924160 | bytes 9912320 | tf_op jit(solution)/shard_map/pallas_call | solution.py:312
  202.3 14.0 %all_to_all.26.arrived = bf16[8,72,640]{2,1,0:T(8,128)(2,1)} all-to-all(bf16[8,72,640]{2,1,0:T(8,128)(2,1)} %shard_map.91), channel_id=1, replica_groups=mesh['z'=16,'c'=2,'y'=4,'xa'=2,'xb'=2] {'y','xb'}, dimensions={0} | all-to-all | bytes 1474560 | tf_op jit(solution)/shard_map/all_to_all | solution.py:193
  216.3 2.2 %shard_map.92 = (f32[64,640]{1,0:T(8,128)}, f32[64,640]{1,0:T(8,128)}) custom-call(f32[1]{0:T(128)S(6)} %convert_element_type.8.live, f32[1]{0:T(128)S(6)} %copy.18.rate, bf16[8,72,640]{2,1,0:T(8,128)(2,1)} %all_to_all.26.arrived, f32[64,640]{1,0:T(8,128)} %bitcast.19, bf16[400,512]{1,0:T(8,128)(2,1)} %shard_map.90.refs_2_.own, bf16[400,512]{1,0:T(8,128)(2,1)} %copy-done.4, ...), custom_call_target="tpu_custom_call" | custom-call | tf_op jit(solution)/shard_map/pallas_call | solution.py:343
  (22 shorter events, 0.1 us)
Async XLA Ops:
  0.6 32.6 %copy-start = (bf16[1,384,3584]{2,1,0:T(8,128)(2,1)S(1)}, bf16[1,384,3584]{2,1,0:T(8,128)(2,1)}, u32[]{:S(2)}) copy-start(bf16[1,384,3584]{2,1,0:T(8,128)(2,1)} %param.7) | copy-start | bytes 8257540
  2.5 12.2 %all-to-all-start = ((bf16[8,16,640]{2,1,0:T(8,128)(2,1)}), bf16[8,16,640]{2,1,0:T(8,128)(2,1)S(1)}, u32[]{:S(2)}, u32[]{:S(2)}) async-start(bf16[8,16,640]{2,1,0:T(8,128)(2,1)} %pad.4), calls=%async_computation | async-start | bytes 327680 | tf_op jit(solution)/shard_map/all_to_all | solution.py:193
  14.7 18.5 %copy-start.8 = (bf16[1,3584,64]{1,2,0:T(8,128)(2,1)S(1)}, bf16[1,3584,64]{1,2,0:T(8,128)(2,1)}, u32[]{:S(2)}) copy-start(bf16[1,3584,64]{1,2,0:T(8,128)(2,1)} %param.8) | copy-start | bytes 1376260
  14.7 90.1 %all-to-all-start.1 = ((bf16[8,480,640]{2,1,0:T(8,128)(2,1)}), bf16[8,480,640]{2,1,0:T(8,128)(2,1)}, u32[]{:S(2)}, u32[]{:S(2)}) async-start(bf16[8,480,640]{2,1,0:T(8,128)(2,1)} %shard_map.86), calls=%async_computation.1 | async-start | bytes 9830400 | tf_op jit(solution)/shard_map/all_to_all | solution.py:193
  19.7 28.0 %collective-permute-start = (bf16[16,5120]{1,0:T(8,128)(2,1)S(1)}, bf16[16,5120]{1,0:T(8,128)(2,1)S(1)}, u32[]{:S(2)}, u32[]{:S(2)}) collective-permute-start(bf16[16,5120]{1,0:T(8,128)(2,1)S(1)} %bitcast.22), channel_id=1, source_target_pairs={{0,160},{32,192},{64,224},{96,256},{128,288},{160,320},{192,352},{... | collective-permute-start | bytes 491528 | tf_op jit(solution)/shard_map/ppermute | solution.py:198
  31.3 25.5 %collective-permute-start.1 = (bf16[16,5120]{1,0:T(8,128)(2,1)S(1)}, bf16[16,5120]{1,0:T(8,128)(2,1)S(1)}, u32[]{:S(2)}, u32[]{:S(2)}) collective-permute-start(bf16[16,5120]{1,0:T(8,128)(2,1)S(1)} %bitcast.23), channel_id=1, source_target_pairs={{0,352},{32,384},{64,416},{96,448},{128,480},{160,0},{192,32},{224... | collective-permute-start | bytes 491528 | tf_op jit(solution)/shard_map/ppermute | solution.py:198
  56.9 48.0 %copy-start.3 = (bf16[48,5120]{1,0:T(8,128)(2,1)}, bf16[48,5120]{1,0:T(8,128)(2,1)S(1)}, u32[]{:S(2)}) copy-start(bf16[48,5120]{1,0:T(8,128)(2,1)S(1)} %pad_maximum_fusion.refs_0_) | copy-start | bytes 1474564
  56.9 12.4 %collective-permute-start.2 = (bf16[48,5120]{1,0:T(8,128)(2,1)S(1)}, bf16[48,5120]{1,0:T(8,128)(2,1)}, u32[]{:S(2)}, u32[]{:S(2)}) collective-permute-start(bf16[48,5120]{1,0:T(8,128)(2,1)S(1)} %pad_maximum_fusion.refs_0_), channel_id=1, source_target_pairs={{0,32},{32,64},{64,96},{96,128},{128,160},{160,192},{192,224},{224... | collective-permute-start | bytes 1474568 | tf_op jit(solution)/shard_map/ppermute | solution.py:198
  59.2 15.7 %collective-permute-start.3 = (bf16[48,5120]{1,0:T(8,128)(2,1)S(1)}, bf16[48,5120]{1,0:T(8,128)(2,1)}, u32[]{:S(2)}, u32[]{:S(2)}) collective-permute-start(bf16[48,5120]{1,0:T(8,128)(2,1)S(1)} %pad_maximum_fusion.refs_0_), channel_id=1, source_target_pairs={{0,480},{32,0},{64,32},{96,64},{128,96},{160,128},{192,160},{224,1... | collective-permute-start | bytes 1474568 | tf_op jit(solution)/shard_map/ppermute | solution.py:198
  69.3 15.1 %collective-permute-start.4 = (bf16[48,5120]{1,0:T(8,128)(2,1)}, bf16[48,5120]{1,0:T(8,128)(2,1)}, u32[]{:S(2)}, u32[]{:S(2)}) collective-permute-start(bf16[48,5120]{1,0:T(8,128)(2,1)} %collective-permute-done.2.refs_1_), channel_id=1, source_target_pairs={{0,32},{32,64},{64,96},{96,128},{128,160},{160,192},{192,224},{224... | collective-permute-start | bytes 1474568 | tf_op jit(solution)/shard_map/ppermute | solution.py:198
  75.0 14.8 %collective-permute-start.5 = (bf16[48,5120]{1,0:T(8,128)(2,1)}, bf16[48,5120]{1,0:T(8,128)(2,1)}, u32[]{:S(2)}, u32[]{:S(2)}) collective-permute-start(bf16[48,5120]{1,0:T(8,128)(2,1)} %collective-permute-done.3.refs_2_), channel_id=1, source_target_pairs={{0,480},{32,0},{64,32},{96,64},{128,96},{160,128},{192,160},{224,1... | collective-permute-start | bytes 1474568 | tf_op jit(solution)/shard_map/ppermute | solution.py:198
  76.9 15.8 %collective-permute-start.7 = (bf16[48,5120]{1,0:T(8,128)(2,1)S(1)}, bf16[48,5120]{1,0:T(8,128)(2,1)S(1)}, u32[]{:S(2)}, u32[]{:S(2)}) collective-permute-start(bf16[48,5120]{1,0:T(8,128)(2,1)S(1)} %pad_maximum_fusion.refs_0_), channel_id=1, source_target_pairs={{0,16},{16,0},{1,17},{17,1},{2,18},{18,2},{3,19},{19,3},{4,20},{20... | collective-permute-start | bytes 1474568 | tf_op jit(solution)/shard_map/ppermute | solution.py:202
  78.8 24.3 %collective-permute-start.8 = (bf16[48,5120]{1,0:T(8,128)(2,1)}, bf16[48,5120]{1,0:T(8,128)(2,1)}, u32[]{:S(2)}, u32[]{:S(2)}) collective-permute-start(bf16[48,5120]{1,0:T(8,128)(2,1)} %collective-permute-done.2.refs_1_), channel_id=1, source_target_pairs={{0,16},{16,0},{1,17},{17,1},{2,18},{18,2},{3,19},{19,3},{4,20},{20... | collective-permute-start | bytes 1474568 | tf_op jit(solution)/shard_map/ppermute | solution.py:202
  81.3 21.9 %collective-permute-start.9 = (bf16[48,5120]{1,0:T(8,128)(2,1)}, bf16[48,5120]{1,0:T(8,128)(2,1)}, u32[]{:S(2)}, u32[]{:S(2)}) collective-permute-start(bf16[48,5120]{1,0:T(8,128)(2,1)} %collective-permute-done.3.refs_2_), channel_id=1, source_target_pairs={{0,16},{16,0},{1,17},{17,1},{2,18},{18,2},{3,19},{19,3},{4,20},{20... | collective-permute-start | bytes 1474568 | tf_op jit(solution)/shard_map/ppermute | solution.py:202
  84.4 20.5 %collective-permute-start.10 = (bf16[48,5120]{1,0:T(8,128)(2,1)}, bf16[48,5120]{1,0:T(8,128)(2,1)}, u32[]{:S(2)}, u32[]{:S(2)}) collective-permute-start(bf16[48,5120]{1,0:T(8,128)(2,1)} %collective-permute-done.4.refs_3_), channel_id=1, source_target_pairs={{0,16},{16,0},{1,17},{17,1},{2,18},{18,2},{3,19},{19,3},{4,20},{20... | collective-permute-start | bytes 1474568 | tf_op jit(solution)/shard_map/ppermute | solution.py:202
  89.7 15.1 %collective-permute-start.11 = (bf16[48,5120]{1,0:T(8,128)(2,1)}, bf16[48,5120]{1,0:T(8,128)(2,1)}, u32[]{:S(2)}, u32[]{:S(2)}) collective-permute-start(bf16[48,5120]{1,0:T(8,128)(2,1)} %collective-permute-done.5.refs_4_), channel_id=1, source_target_pairs={{0,16},{16,0},{1,17},{17,1},{2,18},{18,2},{3,19},{19,3},{4,20},{20... | collective-permute-start | bytes 1474568 | tf_op jit(solution)/shard_map/ppermute | solution.py:202
  92.7 0.8 copy-start.5
  93.5 7.2 %collective-permute-start.6 = (bf16[16,5120]{1,0:T(8,128)(2,1)S(1)}, bf16[16,5120]{1,0:T(8,128)(2,1)S(1)}, u32[]{:S(2)}, u32[]{:S(2)}) collective-permute-start(bf16[16,5120]{1,0:T(8,128)(2,1)S(1)} %slice_select_fusion), channel_id=1, source_target_pairs={{0,32},{32,64},{64,96},{96,128},{128,160},{160,192},{192,224},{224... | collective-permute-start | bytes 491528 | tf_op jit(solution)/shard_map/ppermute | solution.py:229
  100.7 4.2 %copy-start.6 = (bf16[16,5120]{1,0:T(8,128)(2,1)}, bf16[16,5120]{1,0:T(8,128)(2,1)S(1)}, u32[]{:S(2)}) copy-start(bf16[16,5120]{1,0:T(8,128)(2,1)S(1)} %collective-permute-done.6.refs_5_) | copy-start | bytes 491524
  100.7 3.5 %collective-permute-start.12 = (bf16[16,5120]{1,0:T(8,128)(2,1)S(1)}, bf16[16,5120]{1,0:T(8,128)(2,1)S(1)}, u32[]{:S(2)}, u32[]{:S(2)}) collective-permute-start(bf16[16,5120]{1,0:T(8,128)(2,1)S(1)} %collective-permute-done.6.refs_5_), channel_id=1, source_target_pairs={{0,16},{16,0},{1,17},{17,1},{2,18},{18,2},{3,19},{19,3},{4,20},{20... | collective-permute-start | bytes 491528 | tf_op jit(solution)/shard_map/ppermute | solution.py:202
  104.2 0.7 copy-start.7
  113.4 15.1 %collective-permute-start.13 = (bf16[400,512]{1,0:T(8,128)(2,1)}, bf16[400,512]{1,0:T(8,128)(2,1)S(1)}, u32[]{:S(2)}, u32[]{:S(2)}) collective-permute-start(bf16[400,512]{1,0:T(8,128)(2,1)} %get-tuple-element.17.refs_2_.own.refs_4_.own_was), channel_id=1, source_target_pairs={{0,3},{3,0},{1,2},{2,1},{4,7},{7,4},{5,6},{6,5},{8,11},{11,8},{9,1... | collective-permute-start | bytes 1228808 | tf_op jit(solution)/shard_map/ppermute | solution.py:189
  128.6 0.8 copy-start.1
  138.0 16.5 %all-to-all-start.2 = ((bf16[8,72,640]{2,1,0:T(8,128)(2,1)}), bf16[8,72,640]{2,1,0:T(8,128)(2,1)S(1)}, u32[]{:S(2)}, u32[]{:S(2)}) async-start(bf16[8,72,640]{2,1,0:T(8,128)(2,1)} %shard_map.88), calls=%async_computation.2 | async-start | bytes 1474560 | tf_op jit(solution)/shard_map/all_to_all | solution.py:193
  154.5 0.8 copy-start.2
  180.2 12.1 %collective-permute-start.14 = (bf16[400,512]{1,0:T(8,128)(2,1)}, bf16[400,512]{1,0:T(8,128)(2,1)S(1)}, u32[]{:S(2)}, u32[]{:S(2)}) collective-permute-start(bf16[400,512]{1,0:T(8,128)(2,1)} %shard_map.90.refs_2_.own), channel_id=1, source_target_pairs={{0,3},{3,0},{1,2},{2,1},{4,7},{7,4},{5,6},{6,5},{8,11},{11,8},{9,1... | collective-permute-start | bytes 1228808 | tf_op jit(solution)/shard_map/ppermute | solution.py:189
  192.4 0.8 copy-start.4

commit v4 on v3

--- a/solution.py
+++ b/solution.py
@@ -14,7 +14,7 @@
 ALL = ("y", "xa", "xb")
 EXTRA = 8
 TAIL = 16
-VMEM_LIMIT = 56 << 20
+LATER = 56
 TOGETHER = 2
 
 
@@ -105,26 +105,23 @@
         )
 
 
-def summed(own, other, tokens):
-    mixed = own[:tokens, :].astype(F32) + other[:tokens, :].astype(F32)
-    return mixed, own[tokens:, :].astype(F32) + other[tokens:, :].astype(F32)
-
-
-def backward(rank, second_pass, *refs):
-    if second_pass:
-        features, gated, own, other, own_was, other_was, weights, message, mixed, norm = refs
-    else:
-        features, gated, own, other, weights, message, mixed, norm = refs
+def backward(rank, second_pass, features, gated, own, other, *refs):
+    before, refs = (refs[0], refs[1:]) if second_pass else (None, refs)
+    weights, message, kept, mixed, norm = refs
     step = pl.program_id(0)
     tokens = features.shape[0]
 
     @pl.when(step == 0)
     def _():
-        value, rows = summed(own, other, tokens)
+        value = own[:tokens, :].astype(F32) + other[:tokens, :].astype(F32)
+        rows = own[tokens:, :].astype(F32) + other[tokens:, :].astype(F32)
         if second_pass:
-            before, rows_before = summed(own_was, other_was, tokens)
-            ratio = from_pieces(rows, 0) / from_pieces(rows_before, 0)
-            value = value + everywhere(ratio, value.shape) * before
+            kept[...] = rows
+            ratio = from_pieces(rows, 0)[:, :1] / from_pieces(before[tokens:, :], 0)[:, :1]
+            value = value + everywhere(ratio, value.shape) * before[:tokens, :]
+        else:
+            kept[:tokens, :] = value
+            kept[tokens:, :] = rows
         rounded = value.astype(BF16)
         mixed[...] = rounded
         norm[...] = jnp.broadcast_to(total(value * rounded.astype(F32)), norm.shape)
@@ -138,14 +135,13 @@
         message[j, rank:, :] = pieces
 
 
-def update(rank, live, rate, arrived, grad, own, other, message, residual, alpha):
+def update(rank, live, rate, arrived, grad, tail, message, residual, alpha):
     rows = arrived[0].astype(F32)
     for j in range(1, arrived.shape[0]):
         rows = rows + arrived[j].astype(F32)
     g = grad[...]
-    tail = own[...].astype(F32) + other[...].astype(F32)
     shape = (1, g.shape[1])
-    norm = everywhere(from_pieces(tail, 0), shape)
+    norm = everywhere(from_pieces(tail[...], 0), shape)
     step = norm / (from_pieces(rows[rank:], 0) / live[0] + rate[0] * norm)
     h = rows[:rank] / live[0] + rate[0] * g
     r = g - step * h
@@ -154,17 +150,15 @@
     post(message, r.astype(BF16), [total(r * r), total(r * g)], rank)
 
 
-def finish(rank, live, rate, arrived, grad, own, other, own_was, other_was, residual, alpha, x, left):
+def finish(rank, live, rate, arrived, grad, tail, tail_was, residual, alpha, x, left):
     rows = arrived[0].astype(F32)
     for j in range(1, arrived.shape[0]):
         rows = rows + arrived[j].astype(F32)
     g, r = grad[...], residual[...]
     shape = (1, g.shape[1])
-    tail = own[...].astype(F32) + other[...].astype(F32)
-    tail_was = own_was[...].astype(F32) + other_was[...].astype(F32)
-    norm = everywhere(from_pieces(tail, 0), shape)
-    cross = everywhere(from_pieces(tail, 3), shape)
-    norm_was = everywhere(from_pieces(tail_was, 0), shape)
+    norm = everywhere(from_pieces(tail[...], 0), shape)
+    cross = everywhere(from_pieces(tail[...], 3), shape)
+    norm_was = everywhere(from_pieces(tail_was[...], 0), shape)
     ratio = norm / norm_was
     length = norm + ratio * (2.0 * cross + ratio * norm_was)
     step = norm / (from_pieces(rows[rank:], 0) / live[0] + rate[0] * length)
@@ -181,8 +175,8 @@
 SCALAR = pl.BlockSpec(memory_space=pltpu.SMEM)
 
 
-def params():
-    return pltpu.CompilerParams(vmem_limit_bytes=VMEM_LIMIT)
+def params(mebibytes=56):
+    return pltpu.CompilerParams(vmem_limit_bytes=mebibytes << 20)
 
 
 def swapped(array):
@@ -221,12 +215,12 @@
 def all_blocks(near):
     rows = near.shape[0] // 3
     up, down = shifted(near, 1), shifted(near, -1)
-    up2, down2 = shifted(up, 1), shifted(down, -1)
-    far = jnp.where(lax.axis_index("c") == 0, up2[rows : 2 * rows], down2[2 * rows :])
+    far = jnp.where(lax.axis_index("c") == 0, up[rows : 2 * rows], down[2 * rows :])
     size = lax.axis_size("z")
-    both_ways = [(2 * i, 2 * ((i + 1) % size)) for i in range(size)]
-    both_ways += [(2 * i + 1, 2 * ((i - 1) % size) + 1) for i in range(size)]
+    both_ways = [(2 * i, 2 * ((i + 2) % size)) for i in range(size)]
+    both_ways += [(2 * i + 1, 2 * ((i - 2) % size) + 1) for i in range(size)]
     last = lax.ppermute(far, ("z", "c"), both_ways)
+    up2, down2, last = lax.optimization_barrier((shifted(up, 1), shifted(down, -1), last))
     pieces = [near, up, down, up2, down2, last]
     return pieces + [other_core(piece) for piece in pieces]
 
@@ -302,52 +296,53 @@
                 pltpu.VMEM((tokens, width), F32),
                 pltpu.VMEM((EXTRA, width), F32),
             ],
-            compiler_params=params(),
+            compiler_params=params(56 if len(pieces) > 1 else LATER),
             cost_estimate=cost,
         )(features, gated, vectors, *pieces)
         return (own, swapped(own)), weights
 
-    def product_shares(weights, *shares):
-        return exchanged(
-            pl.pallas_call(
-                functools.partial(backward, rank, len(shares) == 4),
-                grid=(steps,),
-                in_specs=[whole((tokens, rank)), block_gated]
-                + [whole(partial_shape)] * len(shares)
-                + [block_weights(weights)],
-                out_specs=block_message,
-                out_shape=message_shape,
-                scratch_shapes=[pltpu.VMEM((tokens, width), BF16), pltpu.VMEM((8, 128), F32)],
-                compiler_params=params(),
-                cost_estimate=cost,
-            )(features, gated, *shares, weights)
-        )
+    def product_shares(weights, own, other, *before):
+        kept_shape = (TAIL, width) if before else partial_shape
+        message, kept = pl.pallas_call(
+            functools.partial(backward, rank, bool(before)),
+            grid=(steps,),
+            in_specs=[whole((tokens, rank)), block_gated]
+            + [whole(partial_shape)] * (2 + len(before))
+            + [block_weights(weights)],
+            out_specs=[block_message, whole(kept_shape)],
+            out_shape=[message_shape, jax.ShapeDtypeStruct(kept_shape, F32)],
+            scratch_shapes=[pltpu.VMEM((tokens, width), BF16), pltpu.VMEM((8, 128), F32)],
+            compiler_params=params(LATER),
+            cost_estimate=cost,
+        )(features, gated, own, other, *before, weights)
+        return exchanged(message), kept
 
     tail = pl.BlockSpec((TAIL, width), lambda i: (tokens // TAIL, 0))
     full_message = whole(message_shape.shape)
     full_state = whole(state.shape)
     full_alpha = whole((8, units))
 
-    first, (weights,) = mixed_shares(gated, pieces)
-    arrived = product_shares(weights, *first)
+    shares, (weights,) = mixed_shares(gated, pieces)
+    arrived, first = product_shares(weights, *shares)
     message, residual, alpha = pl.pallas_call(
         functools.partial(update, rank),
         grid=(1,),
-        in_specs=[SCALAR, SCALAR, full_message, full_state, tail, tail],
+        in_specs=[SCALAR, SCALAR, full_message, full_state, tail],
         out_specs=[full_message, full_state, full_alpha],
         out_shape=[message_shape, state, jax.ShapeDtypeStruct((8, units), F32)],
-        compiler_params=params(),
-    )(live, damping, arrived, target, *first)
-    second, _ = mixed_shares(exchanged(message), [weights])
-    arrived = product_shares(weights, *second, *first)
+        compiler_params=params(8),
+    )(live, damping, arrived, target, first)
+    shares, _ = mixed_shares(exchanged(message), [weights])
+    arrived, second = product_shares(weights, *shares, first)
     x, left = pl.pallas_call(
         functools.partial(finish, rank),
         grid=(1,),
-        in_specs=[SCALAR, SCALAR, full_message, full_state] + [tail] * 4 + [full_state, full_alpha],
+        in_specs=[SCALAR, SCALAR, full_message, full_state, whole((TAIL, width)), tail]
+        + [full_state, full_alpha],
         out_specs=[full_state, full_state],
         out_shape=[state, state],
-        compiler_params=params(),
-    )(live, damping, arrived, target, *second, *first, residual, alpha)
+        compiler_params=params(8),
+    )(live, damping, arrived, target, second, first, residual, alpha)
     return (x[None], left[None])
 
 

time: 220 us -> 215 us (0.977)
  the two profiles are of different devices: /device:TPU:96 before, /device:TPU:64 now
where the time goes in v4:
time: 215 us; the launch traced here: 214 us
  starting transfers between devices  85 us (40%)
  waiting for transfers between devices  49.4 us (23%)
  Pallas kernels  39.9 us (19%)
  blocking collectives  27.3 us (13%)
  local copies, waits for them, and re-layouts  7.64 us (4%)
  between operations  2.29 us (1%)
    ppermute x6, starting transfers between devices, shifted(): return lax.ppermute(array, 'z', [(i, (i + by) % size) for i in range(size)])  35.5 us
    all_to_all x2, blocking collectives, exchanged(): return lax.all_to_all(array, HALF, split_axis=0, concat_axis=0, tiled=True)  27.3 us
    ppermute x6, waiting for transfers between devices, shifted(): return lax.ppermute(array, 'z', [(i, (i + by) % size) for i in range(size)])  18.8 us
    pallas_call x2, Pallas kernels, product_shares(): pl.pallas_call(functools.partial(backward, rank, bool(before)), grid=(ste...  17.7 us
    ppermute x2, waiting for transfers between devices, swapped(): return lax.ppermute(array, ROW, [(0, 3), (3, 0), (1, 2), (2, 1)])  17.1 us
    ppermute x6, starting transfers between devices, other_core(): return lax.ppermute(array, 'c', [(0, 1), (1, 0)])  16.9 us
    pallas_call x2, Pallas kernels, mixed_shares(): pl.pallas_call(functools.partial(forward, rank, len(pieces)), grid=(steps...  15.7 us
    all_to_all x3, starting transfers between devices, exchanged(): return lax.all_to_all(array, HALF, split_axis=0, concat_axis=0, tiled=True)  14.8 us
  transfers between devices with their start and end apart: 18, of which 9 were waited for; matrix products, arithmetic and copies ran while one was open for 1% of the time, Pallas kernels for 2%

profile of v4, /device:TPU:64, one launch (start us, length us, event | category | flops | bytes accessed | tf_op | source)
XLA Modules:
  0.0 214.1 jit_solution(7290411835862838608)
XLA Ops:
  0.6 0.0 copy-start
  0.7 1.1 reshape.13
  1.8 0.7 pad.4
  2.5 5.4 %all-to-all-start = ((bf16[8,16,640]{2,1,0:T(8,128)(2,1)}), bf16[8,16,640]{2,1,0:T(8,128)(2,1)S(1)}, u32[]{:S(2)}, u32[]{:S(2)}) async-start(bf16[8,16,640]{2,1,0:T(8,128)(2,1)} %pad.4), calls=%async_computation | async-start | bytes 327680 | tf_op jit(solution)/shard_map/all_to_all | solution.py:187
  8.5 5.2 %shard_map.86 = bf16[8,480,640]{2,1,0:T(8,128)(2,1)} custom-call(s32[1]{0:T(128)S(6)} %copy.17.live, bf16[384,640]{1,0:T(8,128)(2,1)} %bitcast.25, f32[64,640]{1,0:T(8,128)} %bitcast.17), custom_call_target="tpu_custom_call" | custom-call | flops 1966080 | bytes 4915200 | tf_op jit(solution)/shard_map/pallas_call | solution.py:243
  13.8 0.9 all-to-all-done
  14.7 4.9 %all-to-all-start.1 = ((bf16[8,480,640]{2,1,0:T(8,128)(2,1)}), bf16[8,480,640]{2,1,0:T(8,128)(2,1)}, u32[]{:S(2)}, u32[]{:S(2)}) async-start(bf16[8,480,640]{2,1,0:T(8,128)(2,1)} %shard_map.86), calls=%async_computation.1 | async-start | bytes 9830400 | tf_op jit(solution)/shard_map/all_to_all | solution.py:187
  19.7 10.4 %collective-permute-start = (bf16[16,5120]{1,0:T(8,128)(2,1)S(1)}, bf16[16,5120]{1,0:T(8,128)(2,1)S(1)}, u32[]{:S(2)}, u32[]{:S(2)}) collective-permute-start(bf16[16,5120]{1,0:T(8,128)(2,1)S(1)} %bitcast.22), channel_id=1, source_target_pairs={{0,160},{32,192},{64,224},{96,256},{128,288},{160,320},{192,352},{... | collective-permute-start | bytes 491528 | tf_op jit(solution)/shard_map/ppermute | solution.py:192
  30.1 2.9 %collective-permute-start.1 = (bf16[16,5120]{1,0:T(8,128)(2,1)S(1)}, bf16[16,5120]{1,0:T(8,128)(2,1)S(1)}, u32[]{:S(2)}, u32[]{:S(2)}) collective-permute-start(bf16[16,5120]{1,0:T(8,128)(2,1)S(1)} %bitcast.23), channel_id=1, source_target_pairs={{0,352},{32,384},{64,416},{96,448},{128,480},{160,0},{192,32},{224... | collective-permute-start | bytes 491528 | tf_op jit(solution)/shard_map/ppermute | solution.py:192
  33.0 1.5 fusion.2.features
  34.5 12.1 %collective-permute-done = bf16[16,5120]{1,0:T(8,128)(2,1)S(1)} collective-permute-done((bf16[16,5120]{1,0:T(8,128)(2,1)S(1)}, bf16[16,5120]{1,0:T(8,128)(2,1)S(1)}, u32[]{:S(2)}, u32[]{:S(2)}) %collective-permute-start) | collective-permute-done | bytes 163872 | tf_op jit(solution)/shard_map/ppermute | solution.py:192
  46.6 1.7 collective-permute-done.1
  48.3 12.4 %collective-permute-start.2 = (bf16[48,5120]{1,0:T(8,128)(2,1)S(1)}, bf16[48,5120]{1,0:T(8,128)(2,1)}, u32[]{:S(2)}, u32[]{:S(2)}) collective-permute-start(bf16[48,5120]{1,0:T(8,128)(2,1)S(1)} %pad_maximum_fusion.refs_0_), channel_id=1, source_target_pairs={{0,32},{32,64},{64,96},{96,128},{128,160},{160,192},{192,224},{224... | collective-permute-start | bytes 1474568 | tf_op jit(solution)/shard_map/ppermute | solution.py:192
  60.7 1.9 collective-permute-start.3
  62.6 4.4 %collective-permute-done.2.refs_1_ = bf16[48,5120]{1,0:T(8,128)(2,1)} collective-permute-done((bf16[48,5120]{1,0:T(8,128)(2,1)S(1)}, bf16[48,5120]{1,0:T(8,128)(2,1)}, u32[]{:S(2)}, u32[]{:S(2)}) %collective-permute-start.2) | collective-permute-done | bytes 491552 | tf_op jit(solution)/shard_map/ppermute | solution.py:192
  67.0 6.0 %collective-permute-start.4 = (bf16[48,5120]{1,0:T(8,128)(2,1)}, bf16[48,5120]{1,0:T(8,128)(2,1)S(1)}, u32[]{:S(2)}, u32[]{:S(2)}) collective-permute-start(bf16[48,5120]{1,0:T(8,128)(2,1)} %collective-permute-done.2.refs_1_), channel_id=1, source_target_pairs={{0,32},{32,64},{64,96},{96,128},{128,160},{160,192},{192,224},{224... | collective-permute-start | bytes 1474568 | tf_op jit(solution)/shard_map/ppermute | solution.py:192
  73.1 0.6 collective-permute-done.3.refs_2_
  73.7 1.9 collective-permute-start.5
  75.6 1.0 slice_select_fusion
  76.6 7.8 %collective-permute-start.6 = (bf16[16,5120]{1,0:T(8,128)(2,1)S(1)}, bf16[16,5120]{1,0:T(8,128)(2,1)S(1)}, u32[]{:S(2)}, u32[]{:S(2)}) collective-permute-start(bf16[16,5120]{1,0:T(8,128)(2,1)S(1)} %slice_select_fusion), channel_id=1, source_target_pairs={{0,64},{32,96},{64,128},{96,160},{128,192},{160,224},{192,256},{22... | collective-permute-start | bytes 491528 | tf_op jit(solution)/shard_map/ppermute | solution.py:222
  84.4 1.9 collective-permute-start.7
  86.3 2.4 %collective-permute-start.8 = (bf16[48,5120]{1,0:T(8,128)(2,1)}, bf16[48,5120]{1,0:T(8,128)(2,1)S(1)}, u32[]{:S(2)}, u32[]{:S(2)}) collective-permute-start(bf16[48,5120]{1,0:T(8,128)(2,1)} %collective-permute-done.2.refs_1_), channel_id=1, source_target_pairs={{0,16},{16,0},{1,17},{17,1},{2,18},{18,2},{3,19},{19,3},{4,20},{20... | collective-permute-start | bytes 1474568 | tf_op jit(solution)/shard_map/ppermute | solution.py:196
  88.8 6.3 %collective-permute-start.9 = (bf16[48,5120]{1,0:T(8,128)(2,1)}, bf16[48,5120]{1,0:T(8,128)(2,1)S(1)}, u32[]{:S(2)}, u32[]{:S(2)}) collective-permute-start(bf16[48,5120]{1,0:T(8,128)(2,1)} %collective-permute-done.3.refs_2_), channel_id=1, source_target_pairs={{0,16},{16,0},{1,17},{17,1},{2,18},{18,2},{3,19},{19,3},{4,20},{20... | collective-permute-start | bytes 1474568 | tf_op jit(solution)/shard_map/ppermute | solution.py:196
  95.2 1.9 collective-permute-start.10
  97.1 2.4 %collective-permute-start.11 = (bf16[48,5120]{1,0:T(8,128)(2,1)S(1)}, bf16[48,5120]{1,0:T(8,128)(2,1)}, u32[]{:S(2)}, u32[]{:S(2)}) collective-permute-start(bf16[48,5120]{1,0:T(8,128)(2,1)S(1)} %collective-permute-done.5.refs_4_), channel_id=1, source_target_pairs={{0,16},{16,0},{1,17},{17,1},{2,18},{18,2},{3,19},{19,3},{4,20},{20... | collective-permute-start | bytes 1474568 | tf_op jit(solution)/shard_map/ppermute | solution.py:196
  99.5 1.9 collective-permute-start.12
  101.5 1.3 collective-permute-done.12.refs_11_
  102.9 0.6 copy-done.16
  103.5 0.8 copy-done.12
  104.3 8.6 %shard_map.87 = (bf16[400,512]{1,0:T(8,128)(2,1)}, bf16[512,5120]{1,0:T(8,128)(2,1)}) custom-call(bf16[384,64]{1,0:T(8,128)(2,1)} %fusion.2.features, bf16[8,480,640]{2,1,0:T(8,128)(2,1)} %all-to-all-done.1.gated.vectors, bf16[8,480,640]{2,1,0:T(8,128)(2,1)} %all-to-all-done.1.gated.vectors, bf16[48,5120]{1,0:T(8,128)(2,1)} %copy-done.6, ...), custom_call_target="tpu_custom_call" | custom-call | flops 2264924160 | bytes 9912320 | tf_op jit(solution)/shard_map/pallas_call | solution.py:283
  112.9 4.9 %collective-permute-start.13 = (bf16[400,512]{1,0:T(8,128)(2,1)}, bf16[400,512]{1,0:T(8,128)(2,1)S(1)}, u32[]{:S(2)}, u32[]{:S(2)}) collective-permute-start(bf16[400,512]{1,0:T(8,128)(2,1)} %get-tuple-element.27.own), channel_id=1, source_target_pairs={{0,3},{3,0},{1,2},{2,1},{4,7},{7,4},{5,6},{6,5},{8,11},{11,8},{9,1... | collective-permute-start | bytes 1228808 | tf_op jit(solution)/shard_map/ppermute | solution.py:183
  117.8 10.0 %collective-permute-done.13.other = bf16[400,512]{1,0:T(8,128)(2,1)S(1)} collective-permute-done((bf16[400,512]{1,0:T(8,128)(2,1)}, bf16[400,512]{1,0:T(8,128)(2,1)S(1)}, u32[]{:S(2)}, u32[]{:S(2)}) %collective-permute-start.13) | collective-permute-done | bytes 409632 | tf_op jit(solution)/shard_map/ppermute | solution.py:183
  127.8 0.8 copy-done.14
  128.5 8.6 %shard_map.88 = (bf16[8,72,640]{2,1,0:T(8,128)(2,1)}, f32[400,512]{1,0:T(8,128)}) custom-call(bf16[384,64]{1,0:T(8,128)(2,1)} %fusion.2.features, bf16[8,480,640]{2,1,0:T(8,128)(2,1)} %all-to-all-done.1.gated.vectors, bf16[400,512]{1,0:T(8,128)(2,1)} %get-tuple-element.27.own, bf16[400,512]{1,0:T(8,128)(2,1)} %copy-done.14, ...), custom_call_target="tpu_custom_call" | custom-call | flops 2264924160 | bytes 9912320 | tf_op jit(solution)/shard_map/pallas_call | solution.py:306
  137.2 4.4 %all-to-all-start.2 = ((bf16[8,72,640]{2,1,0:T(8,128)(2,1)}), bf16[8,72,640]{2,1,0:T(8,128)(2,1)S(1)}, u32[]{:S(2)}, u32[]{:S(2)}) async-start(bf16[8,72,640]{2,1,0:T(8,128)(2,1)} %get-tuple-element.29), calls=%async_computation.2 | async-start | bytes 1474560 | tf_op jit(solution)/shard_map/all_to_all | solution.py:187
  142.3 11.2 %all-to-all-done.2.arrived = bf16[8,72,640]{2,1,0:T(8,128)(2,1)S(1)} async-done(((bf16[8,72,640]{2,1,0:T(8,128)(2,1)}), bf16[8,72,640]{2,1,0:T(8,128)(2,1)S(1)}, u32[]{:S(2)}, u32[]{:S(2)}) %all-to-all-start.2) | async-done | bytes 737312 | tf_op jit(solution)/shard_map/all_to_all | solution.py:187
  153.5 1.1 copy-done.1
  154.6 0.9 copy-done.3
  155.6 0.3 shard_map.89
  155.9 14.0 %all_to_all.25.vectors = bf16[8,72,640]{2,1,0:T(8,128)(2,1)} all-to-all(bf16[8,72,640]{2,1,0:T(8,128)(2,1)S(1)} %get-tuple-element.31), channel_id=1, replica_groups=mesh['z'=16,'c'=2,'y'=4,'xa'=2,'xb'=2] {'y','xb'}, dimensions={0} | all-to-all | bytes 1474560 | tf_op jit(solution)/shard_map/all_to_all | solution.py:187
  169.9 7.2 %shard_map.90.own = bf16[400,512]{1,0:T(8,128)(2,1)} custom-call(bf16[384,64]{1,0:T(8,128)(2,1)} %fusion.2.features, bf16[8,480,640]{2,1,0:T(8,128)(2,1)} %all-to-all-done.1.gated.vectors, bf16[8,72,640]{2,1,0:T(8,128)(2,1)} %all_to_all.25.vectors, bf16[512,5120]{1,0:T(8,128)(2,1)} %get-tuple-element.28.refs_0_.refs_1_), custom_call_target="tpu_custom_call" | custom-call | flops 2264924160 | bytes 9912320 | tf_op jit(solution)/shard_map/pallas_call | solution.py:283
  177.0 5.1 %collective-permute-start.14 = (bf16[400,512]{1,0:T(8,128)(2,1)}, bf16[400,512]{1,0:T(8,128)(2,1)S(1)}, u32[]{:S(2)}, u32[]{:S(2)}) collective-permute-start(bf16[400,512]{1,0:T(8,128)(2,1)} %shard_map.90.own), channel_id=1, source_target_pairs={{0,3},{3,0},{1,2},{2,1},{4,7},{7,4},{5,6},{6,5},{8,11},{11,8},{9,1... | collective-permute-start | bytes 1228808 | tf_op jit(solution)/shard_map/ppermute | solution.py:183
  182.1 7.1 %collective-permute-done.14.other = bf16[400,512]{1,0:T(8,128)(2,1)S(1)} collective-permute-done((bf16[400,512]{1,0:T(8,128)(2,1)}, bf16[400,512]{1,0:T(8,128)(2,1)S(1)}, u32[]{:S(2)}, u32[]{:S(2)}) %collective-permute-start.14) | collective-permute-done | bytes 409632 | tf_op jit(solution)/shard_map/ppermute | solution.py:183
  189.3 0.8 copy-done.13
  190.1 9.0 %shard_map.91 = (bf16[8,72,640]{2,1,0:T(8,128)(2,1)}, f32[16,512]{1,0:T(8,128)}) custom-call(bf16[384,64]{1,0:T(8,128)(2,1)} %fusion.2.features, bf16[8,480,640]{2,1,0:T(8,128)(2,1)} %all-to-all-done.1.gated.vectors, bf16[400,512]{1,0:T(8,128)(2,1)} %shard_map.90.own, bf16[400,512]{1,0:T(8,128)(2,1)} %copy-done.13, ...), custom_call_target="tpu_custom_call" | custom-call | flops 2264924160 | bytes 9912320 | tf_op jit(solution)/shard_map/pallas_call | solution.py:306
  199.1 13.3 %all_to_all.26.arrived = bf16[8,72,640]{2,1,0:T(8,128)(2,1)S(1)} all-to-all(bf16[8,72,640]{2,1,0:T(8,128)(2,1)} %get-tuple-element.32), channel_id=1, replica_groups=mesh['z'=16,'c'=2,'y'=4,'xa'=2,'xb'=2] {'y','xb'}, dimensions={0} | all-to-all | bytes 1474560 | tf_op jit(solution)/shard_map/all_to_all | solution.py:187
  212.4 0.8 copy-done.5
  213.2 0.9 shard_map.92
  (40 shorter events, 0.2 us)
Async XLA Ops:
  0.6 32.3 %copy-start = (bf16[1,384,3584]{2,1,0:T(8,128)(2,1)S(1)}, bf16[1,384,3584]{2,1,0:T(8,128)(2,1)}, u32[]{:S(2)}) copy-start(bf16[1,384,3584]{2,1,0:T(8,128)(2,1)} %param.7) | copy-start | bytes 8257540
  2.5 12.2 %all-to-all-start = ((bf16[8,16,640]{2,1,0:T(8,128)(2,1)}), bf16[8,16,640]{2,1,0:T(8,128)(2,1)S(1)}, u32[]{:S(2)}, u32[]{:S(2)}) async-start(bf16[8,16,640]{2,1,0:T(8,128)(2,1)} %pad.4), calls=%async_computation | async-start | bytes 327680 | tf_op jit(solution)/shard_map/all_to_all | solution.py:187
  14.7 18.3 %copy-start.17 = (bf16[1,3584,64]{1,2,0:T(8,128)(2,1)S(1)}, bf16[1,3584,64]{1,2,0:T(8,128)(2,1)}, u32[]{:S(2)}) copy-start(bf16[1,3584,64]{1,2,0:T(8,128)(2,1)} %param.8) | copy-start | bytes 1376260
  14.7 89.6 %all-to-all-start.1 = ((bf16[8,480,640]{2,1,0:T(8,128)(2,1)}), bf16[8,480,640]{2,1,0:T(8,128)(2,1)}, u32[]{:S(2)}, u32[]{:S(2)}) async-start(bf16[8,480,640]{2,1,0:T(8,128)(2,1)} %shard_map.86), calls=%async_computation.1 | async-start | bytes 9830400 | tf_op jit(solution)/shard_map/all_to_all | solution.py:187
  19.7 26.9 %collective-permute-start = (bf16[16,5120]{1,0:T(8,128)(2,1)S(1)}, bf16[16,5120]{1,0:T(8,128)(2,1)S(1)}, u32[]{:S(2)}, u32[]{:S(2)}) collective-permute-start(bf16[16,5120]{1,0:T(8,128)(2,1)S(1)} %bitcast.22), channel_id=1, source_target_pairs={{0,160},{32,192},{64,224},{96,256},{128,288},{160,320},{192,352},{... | collective-permute-start | bytes 491528 | tf_op jit(solution)/shard_map/ppermute | solution.py:192
  30.1 18.2 %collective-permute-start.1 = (bf16[16,5120]{1,0:T(8,128)(2,1)S(1)}, bf16[16,5120]{1,0:T(8,128)(2,1)S(1)}, u32[]{:S(2)}, u32[]{:S(2)}) collective-permute-start(bf16[16,5120]{1,0:T(8,128)(2,1)S(1)} %bitcast.23), channel_id=1, source_target_pairs={{0,352},{32,384},{64,416},{96,448},{128,480},{160,0},{192,32},{224... | collective-permute-start | bytes 491528 | tf_op jit(solution)/shard_map/ppermute | solution.py:192
  48.3 56.0 %copy-start.6 = (bf16[48,5120]{1,0:T(8,128)(2,1)}, bf16[48,5120]{1,0:T(8,128)(2,1)S(1)}, u32[]{:S(2)}) copy-start(bf16[48,5120]{1,0:T(8,128)(2,1)S(1)} %pad_maximum_fusion.refs_0_) | copy-start | bytes 1474564
  48.3 18.7 %collective-permute-start.2 = (bf16[48,5120]{1,0:T(8,128)(2,1)S(1)}, bf16[48,5120]{1,0:T(8,128)(2,1)}, u32[]{:S(2)}, u32[]{:S(2)}) collective-permute-start(bf16[48,5120]{1,0:T(8,128)(2,1)S(1)} %pad_maximum_fusion.refs_0_), channel_id=1, source_target_pairs={{0,32},{32,64},{64,96},{96,128},{128,160},{160,192},{192,224},{224... | collective-permute-start | bytes 1474568 | tf_op jit(solution)/shard_map/ppermute | solution.py:192
  60.7 12.9 %collective-permute-start.3 = (bf16[48,5120]{1,0:T(8,128)(2,1)S(1)}, bf16[48,5120]{1,0:T(8,128)(2,1)}, u32[]{:S(2)}, u32[]{:S(2)}) collective-permute-start(bf16[48,5120]{1,0:T(8,128)(2,1)S(1)} %pad_maximum_fusion.refs_0_), channel_id=1, source_target_pairs={{0,480},{32,0},{64,32},{96,64},{128,96},{160,128},{192,160},{224,1... | collective-permute-start | bytes 1474568 | tf_op jit(solution)/shard_map/ppermute | solution.py:192
  67.0 28.1 %collective-permute-start.4 = (bf16[48,5120]{1,0:T(8,128)(2,1)}, bf16[48,5120]{1,0:T(8,128)(2,1)S(1)}, u32[]{:S(2)}, u32[]{:S(2)}) collective-permute-start(bf16[48,5120]{1,0:T(8,128)(2,1)} %collective-permute-done.2.refs_1_), channel_id=1, source_target_pairs={{0,32},{32,64},{64,96},{96,128},{128,160},{160,192},{192,224},{224... | collective-permute-start | bytes 1474568 | tf_op jit(solution)/shard_map/ppermute | solution.py:192
  73.7 21.5 %collective-permute-start.5 = (bf16[48,5120]{1,0:T(8,128)(2,1)}, bf16[48,5120]{1,0:T(8,128)(2,1)S(1)}, u32[]{:S(2)}, u32[]{:S(2)}) collective-permute-start(bf16[48,5120]{1,0:T(8,128)(2,1)} %collective-permute-done.3.refs_2_), channel_id=1, source_target_pairs={{0,480},{32,0},{64,32},{96,64},{128,96},{160,128},{192,160},{224,1... | collective-permute-start | bytes 1474568 | tf_op jit(solution)/shard_map/ppermute | solution.py:192
  76.6 12.2 %collective-permute-start.6 = (bf16[16,5120]{1,0:T(8,128)(2,1)S(1)}, bf16[16,5120]{1,0:T(8,128)(2,1)S(1)}, u32[]{:S(2)}, u32[]{:S(2)}) collective-permute-start(bf16[16,5120]{1,0:T(8,128)(2,1)S(1)} %slice_select_fusion), channel_id=1, source_target_pairs={{0,64},{32,96},{64,128},{96,160},{128,192},{160,224},{192,256},{22... | collective-permute-start | bytes 491528 | tf_op jit(solution)/shard_map/ppermute | solution.py:222
  84.4 15.1 %collective-permute-start.7 = (bf16[48,5120]{1,0:T(8,128)(2,1)S(1)}, bf16[48,5120]{1,0:T(8,128)(2,1)S(1)}, u32[]{:S(2)}, u32[]{:S(2)}) collective-permute-start(bf16[48,5120]{1,0:T(8,128)(2,1)S(1)} %pad_maximum_fusion.refs_0_), channel_id=1, source_target_pairs={{0,16},{16,0},{1,17},{17,1},{2,18},{18,2},{3,19},{19,3},{4,20},{20... | collective-permute-start | bytes 1474568 | tf_op jit(solution)/shard_map/ppermute | solution.py:196
  86.3 15.1 %collective-permute-start.8 = (bf16[48,5120]{1,0:T(8,128)(2,1)}, bf16[48,5120]{1,0:T(8,128)(2,1)S(1)}, u32[]{:S(2)}, u32[]{:S(2)}) collective-permute-start(bf16[48,5120]{1,0:T(8,128)(2,1)} %collective-permute-done.2.refs_1_), channel_id=1, source_target_pairs={{0,16},{16,0},{1,17},{17,1},{2,18},{18,2},{3,19},{19,3},{4,20},{20... | collective-permute-start | bytes 1474568 | tf_op jit(solution)/shard_map/ppermute | solution.py:196
  88.8 15.6 %copy-start.15 = (bf16[16,5120]{1,0:T(8,128)(2,1)}, bf16[16,5120]{1,0:T(8,128)(2,1)S(1)}, u32[]{:S(2)}) copy-start(bf16[16,5120]{1,0:T(8,128)(2,1)S(1)} %collective-permute-done.6.refs_5_) | copy-start | bytes 491524
  88.8 12.7 %collective-permute-start.9 = (bf16[48,5120]{1,0:T(8,128)(2,1)}, bf16[48,5120]{1,0:T(8,128)(2,1)S(1)}, u32[]{:S(2)}, u32[]{:S(2)}) collective-permute-start(bf16[48,5120]{1,0:T(8,128)(2,1)} %collective-permute-done.3.refs_2_), channel_id=1, source_target_pairs={{0,16},{16,0},{1,17},{17,1},{2,18},{18,2},{3,19},{19,3},{4,20},{20... | collective-permute-start | bytes 1474568 | tf_op jit(solution)/shard_map/ppermute | solution.py:196
  95.1 4.4 %copy-start.7 = (bf16[48,5120]{1,0:T(8,128)(2,1)}, bf16[48,5120]{1,0:T(8,128)(2,1)S(1)}, u32[]{:S(2)}) copy-start(bf16[48,5120]{1,0:T(8,128)(2,1)S(1)} %collective-permute-done.4.refs_3_) | copy-start | bytes 1474564
  95.2 7.7 %copy-start.8 = (bf16[48,5120]{1,0:T(8,128)(2,1)}, bf16[48,5120]{1,0:T(8,128)(2,1)S(1)}, u32[]{:S(2)}) copy-start(bf16[48,5120]{1,0:T(8,128)(2,1)S(1)} %collective-permute-done.5.refs_4_) | copy-start | bytes 1474564
  95.2 7.7 %collective-permute-start.10 = (bf16[48,5120]{1,0:T(8,128)(2,1)S(1)}, bf16[48,5120]{1,0:T(8,128)(2,1)S(1)}, u32[]{:S(2)}, u32[]{:S(2)}) collective-permute-start(bf16[48,5120]{1,0:T(8,128)(2,1)S(1)} %collective-permute-done.4.refs_3_), channel_id=1, source_target_pairs={{0,16},{16,0},{1,17},{17,1},{2,18},{18,2},{3,19},{19,3},{4,20},{20... | collective-permute-start | bytes 1474568 | tf_op jit(solution)/shard_map/ppermute | solution.py:196
  97.1 7.2 %collective-permute-start.11 = (bf16[48,5120]{1,0:T(8,128)(2,1)S(1)}, bf16[48,5120]{1,0:T(8,128)(2,1)}, u32[]{:S(2)}, u32[]{:S(2)}) collective-permute-start(bf16[48,5120]{1,0:T(8,128)(2,1)S(1)} %collective-permute-done.5.refs_4_), channel_id=1, source_target_pairs={{0,16},{16,0},{1,17},{17,1},{2,18},{18,2},{3,19},{19,3},{4,20},{20... | collective-permute-start | bytes 1474568 | tf_op jit(solution)/shard_map/ppermute | solution.py:196
  99.5 3.3 %copy-start.9 = (bf16[48,5120]{1,0:T(8,128)(2,1)}, bf16[48,5120]{1,0:T(8,128)(2,1)S(1)}, u32[]{:S(2)}) copy-start(bf16[48,5120]{1,0:T(8,128)(2,1)S(1)} %collective-permute-done.7.refs_6_) | copy-start | bytes 1474564
  99.5 3.3 %collective-permute-start.12 = (bf16[16,5120]{1,0:T(8,128)(2,1)S(1)}, bf16[16,5120]{1,0:T(8,128)(2,1)S(1)}, u32[]{:S(2)}, u32[]{:S(2)}) collective-permute-start(bf16[16,5120]{1,0:T(8,128)(2,1)S(1)} %collective-permute-done.6.refs_5_), channel_id=1, source_target_pairs={{0,16},{16,0},{1,17},{17,1},{2,18},{18,2},{3,19},{19,3},{4,20},{20... | collective-permute-start | bytes 491528 | tf_op jit(solution)/shard_map/ppermute | solution.py:196
  101.5 1.4 copy-start.10
  101.5 1.4 copy-start.11
  102.8 0.7 copy-start.16
  103.5 0.8 copy-start.12
  112.9 14.9 %collective-permute-start.13 = (bf16[400,512]{1,0:T(8,128)(2,1)}, bf16[400,512]{1,0:T(8,128)(2,1)S(1)}, u32[]{:S(2)}, u32[]{:S(2)}) collective-permute-start(bf16[400,512]{1,0:T(8,128)(2,1)} %get-tuple-element.27.own), channel_id=1, source_target_pairs={{0,3},{3,0},{1,2},{2,1},{4,7},{7,4},{5,6},{6,5},{8,11},{11,8},{9,1... | collective-permute-start | bytes 1228808 | tf_op jit(solution)/shard_map/ppermute | solution.py:183
  127.8 0.8 copy-start.14
  137.2 16.3 %all-to-all-start.2 = ((bf16[8,72,640]{2,1,0:T(8,128)(2,1)}), bf16[8,72,640]{2,1,0:T(8,128)(2,1)S(1)}, u32[]{:S(2)}, u32[]{:S(2)}) async-start(bf16[8,72,640]{2,1,0:T(8,128)(2,1)} %get-tuple-element.29), calls=%async_computation.2 | async-start | bytes 1474560 | tf_op jit(solution)/shard_map/all_to_all | solution.py:187
  153.5 1.1 copy-start.1
  154.6 0.9 copy-start.3
  177.0 35.4 %copy-start.2 = (f32[400,512]{1,0:T(8,128)S(1)}, f32[400,512]{1,0:T(8,128)}, u32[]{:S(2)}) copy-start(f32[400,512]{1,0:T(8,128)} %get-tuple-element.30.tail.refs_0_.tail_was) | copy-start | bytes 2457604
  177.0 35.4 %copy-start.4 = (f32[1,64,640]{2,1,0:T(8,128)S(1)}, f32[1,64,640]{2,1,0:T(8,128)}, u32[]{:S(2)}) copy-start(f32[1,64,640]{2,1,0:T(8,128)} %param.13) | copy-start | bytes 491524
  177.0 12.2 %collective-permute-start.14 = (bf16[400,512]{1,0:T(8,128)(2,1)}, bf16[400,512]{1,0:T(8,128)(2,1)S(1)}, u32[]{:S(2)}, u32[]{:S(2)}) collective-permute-start(bf16[400,512]{1,0:T(8,128)(2,1)} %shard_map.90.own), channel_id=1, source_target_pairs={{0,3},{3,0},{1,2},{2,1},{4,7},{7,4},{5,6},{6,5},{8,11},{11,8},{9,1... | collective-permute-start | bytes 1228808 | tf_op jit(solution)/shard_map/ppermute | solution.py:183
  189.3 0.8 copy-start.13
  212.4 0.8 copy-start.5

commit v5 on v4

--- a/solution.py
+++ b/solution.py
@@ -208,10 +208,6 @@
     return jnp.swapaxes(mine, 0, 1).reshape(padded, members * units)
 
 
-def start_blocks(mine):
-    return jnp.concatenate([mine, shifted(mine, 5), shifted(mine, -5)], axis=0)
-
-
 def all_blocks(near):
     rows = near.shape[0] // 3
     up, down = shifted(near, 1), shifted(near, -1)
@@ -221,8 +217,9 @@
     both_ways += [(2 * i + 1, 2 * ((i - 2) % size) + 1) for i in range(size)]
     last = lax.ppermute(far, ("z", "c"), both_ways)
     up2, down2, last = lax.optimization_barrier((shifted(up, 1), shifted(down, -1), last))
-    pieces = [near, up, down, up2, down2, last]
-    return pieces + [other_core(piece) for piece in pieces]
+    early = jnp.concatenate([near, up, down], axis=0)
+    late = jnp.concatenate([up2, down2, last], axis=0)
+    return [early, late, other_core(early), other_core(late)]
 
 
 def shards(support_x, adapter_a, gate_pre, lengths, damping, down_w, grad_b):
@@ -258,8 +255,10 @@
     mine = width_block(down_w)
     mine, packed = lax.optimization_barrier((mine, packed))
     gated = exchanged(packed)
+    below, above = shifted(mine, 5), shifted(mine, -5)
     features = jnp.dot(support_x[0], adapter_a[0], preferred_element_type=F32).astype(BF16)
-    near, features = lax.optimization_barrier((start_blocks(mine), features))
+    near = jnp.concatenate([mine, below, above], axis=0)
+    near, features = lax.optimization_barrier((near, features))
     pieces = all_blocks(near)
     width = sum(piece.shape[0] for piece in pieces)
 

time: 215 us -> 204 us (0.949)
  the two profiles are of different devices: /device:TPU:64 before, /device:TPU:4 now
where the time goes in v5:
time: 204 us; the launch traced here: 203 us
  starting transfers between devices  62.8 us (31%)
  waiting for transfers between devices  59.6 us (29%)
  Pallas kernels  40 us (20%)
  blocking collectives  28.2 us (14%)
  local copies, waits for them, and re-layouts  7.88 us (4%)
  matrix products  2.51 us (1%)
  between operations  2.2 us (1%)
    ppermute x6, starting transfers between devices, shifted(): return lax.ppermute(array, 'z', [(i, (i + by) % size) for i in range(size)])  31.7 us
    all_to_all x2, blocking collectives, exchanged(): return lax.all_to_all(array, HALF, split_axis=0, concat_axis=0, tiled=True)  28.2 us
    ppermute x6, waiting for transfers between devices, shifted(): return lax.ppermute(array, 'z', [(i, (i + by) % size) for i in range(size)])  25.9 us
    ppermute x2, waiting for transfers between devices, swapped(): return lax.ppermute(array, ROW, [(0, 3), (3, 0), (1, 2), (2, 1)])  19.2 us
    pallas_call x2, Pallas kernels, product_shares(): pl.pallas_call(functools.partial(backward, rank, bool(before)), grid=(ste...  17.7 us
    all_to_all x3, starting transfers between devices, exchanged(): return lax.all_to_all(array, HALF, split_axis=0, concat_axis=0, tiled=True)  16.5 us
    pallas_call x2, Pallas kernels, mixed_shares(): pl.pallas_call(functools.partial(forward, rank, len(pieces)), grid=(steps...  15.8 us
    all_to_all x3, waiting for transfers between devices, exchanged(): return lax.all_to_all(array, HALF, split_axis=0, concat_axis=0, tiled=True)  12.7 us
  transfers between devices with their start and end apart: 14, of which 11 were waited for; matrix products, arithmetic and copies ran while one was open for 1% of the time, Pallas kernels for 3%

profile of v5, /device:TPU:4, one launch (start us, length us, event | category | flops | bytes accessed | tf_op | source)
XLA Modules:
  0.0 203.2 jit_solution(16686411105767297679)
XLA Ops:
  0.6 0.0 copy-start
  0.7 1.1 reshape.13
  1.8 0.7 pad.4
  2.5 5.1 %all-to-all-start = ((bf16[8,16,640]{2,1,0:T(8,128)(2,1)}), bf16[8,16,640]{2,1,0:T(8,128)(2,1)S(1)}, u32[]{:S(2)}, u32[]{:S(2)}) async-start(bf16[8,16,640]{2,1,0:T(8,128)(2,1)} %pad.4), calls=%async_computation | async-start | bytes 327680 | tf_op jit(solution)/shard_map/all_to_all | solution.py:187
  8.2 5.3 %shard_map.86 = bf16[8,480,640]{2,1,0:T(8,128)(2,1)} custom-call(s32[1]{0:T(128)S(6)} %copy.21.live, bf16[384,640]{1,0:T(8,128)(2,1)} %bitcast.25, f32[64,640]{1,0:T(8,128)} %bitcast.17), custom_call_target="tpu_custom_call" | custom-call | flops 1966080 | bytes 4915200 | tf_op jit(solution)/shard_map/pallas_call | solution.py:240
  13.5 0.9 all-to-all-done
  14.4 10.5 %collective-permute-start = (bf16[16,5120]{1,0:T(8,128)(2,1)S(1)}, bf16[16,5120]{1,0:T(8,128)(2,1)S(1)}, u32[]{:S(2)}, u32[]{:S(2)}) collective-permute-start(bf16[16,5120]{1,0:T(8,128)(2,1)S(1)} %bitcast.22), channel_id=1, source_target_pairs={{0,160},{32,192},{64,224},{96,256},{128,288},{160,320},{192,352},{... | collective-permute-start | bytes 491528 | tf_op jit(solution)/shard_map/ppermute | solution.py:192
  24.9 5.9 %collective-permute-start.1 = (bf16[16,5120]{1,0:T(8,128)(2,1)S(1)}, bf16[16,5120]{1,0:T(8,128)(2,1)S(1)}, u32[]{:S(2)}, u32[]{:S(2)}) collective-permute-start(bf16[16,5120]{1,0:T(8,128)(2,1)S(1)} %bitcast.23), channel_id=1, source_target_pairs={{0,352},{32,384},{64,416},{96,448},{128,480},{160,0},{192,32},{224... | collective-permute-start | bytes 491528 | tf_op jit(solution)/shard_map/ppermute | solution.py:192
  30.8 2.5 %fusion.2.features = bf16[384,64]{1,0:T(8,128)(2,1)} fusion(bf16[1,384,3584]{2,1,0:T(8,128)(2,1)S(1)} %copy-done, bf16[1,3584,64]{1,2,0:T(8,128)(2,1)} %param.8), kind=kOutput, calls=%fused_computation.2 | convolution fusion | flops 176185344 | bytes 3260416 | tf_op jit(solution)/shard_map/dot_general | solution.py:259
  33.3 4.8 %all-to-all-start.1 = ((bf16[8,480,640]{2,1,0:T(8,128)(2,1)}), bf16[8,480,640]{2,1,0:T(8,128)(2,1)}, u32[]{:S(2)}, u32[]{:S(2)}) async-start(bf16[8,480,640]{2,1,0:T(8,128)(2,1)} %shard_map.86), calls=%async_computation.1 | async-start | bytes 9830400 | tf_op jit(solution)/shard_map/all_to_all | solution.py:187
  38.1 0.0 collective-permute-done
  38.1 10.1 %collective-permute-done.1 = bf16[16,5120]{1,0:T(8,128)(2,1)S(1)} collective-permute-done((bf16[16,5120]{1,0:T(8,128)(2,1)S(1)}, bf16[16,5120]{1,0:T(8,128)(2,1)S(1)}, u32[]{:S(2)}, u32[]{:S(2)}) %collective-permute-start.1) | collective-permute-done | bytes 163872 | tf_op jit(solution)/shard_map/ppermute | solution.py:192
  48.2 1.9 collective-permute-start.2
  50.1 6.4 %collective-permute-start.3 = (bf16[48,5120]{1,0:T(8,128)(2,1)S(1)}, bf16[48,5120]{1,0:T(8,128)(2,1)S(1)}, u32[]{:S(2)}, u32[]{:S(2)}) collective-permute-start(bf16[48,5120]{1,0:T(8,128)(2,1)S(1)} %pad_maximum_fusion), channel_id=1, source_target_pairs={{0,480},{32,0},{64,32},{96,64},{128,96},{160,128},{192,160},{224,1... | collective-permute-start | bytes 1474568 | tf_op jit(solution)/shard_map/ppermute | solution.py:192
  56.6 9.0 %collective-permute-done.2 = bf16[48,5120]{1,0:T(8,128)(2,1)S(1)} collective-permute-done((bf16[48,5120]{1,0:T(8,128)(2,1)S(1)}, bf16[48,5120]{1,0:T(8,128)(2,1)S(1)}, u32[]{:S(2)}, u32[]{:S(2)}) %collective-permute-start.2) | collective-permute-done | bytes 491552 | tf_op jit(solution)/shard_map/ppermute | solution.py:192
  65.6 1.2 collective-permute-done.3
  66.8 6.4 %collective-permute-start.6 = (bf16[16,5120]{1,0:T(8,128)(2,1)S(1)}, bf16[16,5120]{1,0:T(8,128)(2,1)S(1)}, u32[]{:S(2)}, u32[]{:S(2)}) collective-permute-start(bf16[16,5120]{1,0:T(8,128)(2,1)S(1)} %slice_select_fusion), channel_id=1, source_target_pairs={{0,64},{32,96},{64,128},{96,160},{128,192},{160,224},{192,256},{22... | collective-permute-start | bytes 491528 | tf_op jit(solution)/shard_map/ppermute | solution.py:218
  73.2 4.9 %collective-permute-start.4 = (bf16[48,5120]{1,0:T(8,128)(2,1)S(1)}, bf16[48,5120]{1,0:T(8,128)(2,1)S(1)}, u32[]{:S(2)}, u32[]{:S(2)}) collective-permute-start(bf16[48,5120]{1,0:T(8,128)(2,1)S(1)} %collective-permute-done.2), channel_id=1, source_target_pairs={{0,32},{32,64},{64,96},{96,128},{128,160},{160,192},{192,224},{224... | collective-permute-start | bytes 1474568 | tf_op jit(solution)/shard_map/ppermute | solution.py:192
  78.1 2.2 %collective-permute-start.5 = (bf16[48,5120]{1,0:T(8,128)(2,1)S(1)}, bf16[48,5120]{1,0:T(8,128)(2,1)S(1)}, u32[]{:S(2)}, u32[]{:S(2)}) collective-permute-start(bf16[48,5120]{1,0:T(8,128)(2,1)S(1)} %collective-permute-done.3), channel_id=1, source_target_pairs={{0,480},{32,0},{64,32},{96,64},{128,96},{160,128},{192,160},{224,1... | collective-permute-start | bytes 1474568 | tf_op jit(solution)/shard_map/ppermute | solution.py:192
  80.4 1.1 copy-done.6
  81.5 1.9 collective-permute-start.7
  83.4 0.0 collective-permute-done.6
  83.4 4.6 %collective-permute-done.4 = bf16[48,5120]{1,0:T(8,128)(2,1)S(1)} collective-permute-done((bf16[48,5120]{1,0:T(8,128)(2,1)S(1)}, bf16[48,5120]{1,0:T(8,128)(2,1)S(1)}, u32[]{:S(2)}, u32[]{:S(2)}) %collective-permute-start.4) | collective-permute-done | bytes 491552 | tf_op jit(solution)/shard_map/ppermute | solution.py:192
  88.0 1.1 collective-permute-done.5
  89.2 1.9 collective-permute-start.8
  91.1 0.0 collective-permute-done.7.refs_2_
  91.1 1.2 copy-done.8
  92.3 1.7 collective-permute-done.8.refs_3_
  94.0 0.5 all-to-all-done.1.gated.vectors
  94.5 8.6 %shard_map.87 = (bf16[400,512]{1,0:T(8,128)(2,1)}, bf16[512,5120]{1,0:T(8,128)(2,1)}) custom-call(bf16[384,64]{1,0:T(8,128)(2,1)} %fusion.2.features, bf16[8,480,640]{2,1,0:T(8,128)(2,1)} %all-to-all-done.1.gated.vectors, bf16[8,480,640]{2,1,0:T(8,128)(2,1)} %all-to-all-done.1.gated.vectors, bf16[144,5120]{1,0:T(8,128)(2,1)} %copy-done.6, ...), custom_call_target="tpu_custom_call" | custom-call | flops 2264924160 | bytes 9912320 | tf_op jit(solution)/shard_map/pallas_call | solution.py:282
  103.1 2.5 %collective-permute-start.9 = (bf16[400,512]{1,0:T(8,128)(2,1)}, bf16[400,512]{1,0:T(8,128)(2,1)S(1)}, u32[]{:S(2)}, u32[]{:S(2)}) collective-permute-start(bf16[400,512]{1,0:T(8,128)(2,1)} %get-tuple-element.27.own), channel_id=1, source_target_pairs={{0,3},{3,0},{1,2},{2,1},{4,7},{7,4},{5,6},{6,5},{8,11},{11,8},{9,1... | collective-permute-start | bytes 1228808 | tf_op jit(solution)/shard_map/ppermute | solution.py:183
  105.6 10.6 %collective-permute-done.9.other = bf16[400,512]{1,0:T(8,128)(2,1)S(1)} collective-permute-done((bf16[400,512]{1,0:T(8,128)(2,1)}, bf16[400,512]{1,0:T(8,128)(2,1)S(1)}, u32[]{:S(2)}, u32[]{:S(2)}) %collective-permute-start.9) | collective-permute-done | bytes 409632 | tf_op jit(solution)/shard_map/ppermute | solution.py:183
  116.2 0.7 copy-done.10
  117.0 8.6 %shard_map.88 = (bf16[8,72,640]{2,1,0:T(8,128)(2,1)}, f32[400,512]{1,0:T(8,128)}) custom-call(bf16[384,64]{1,0:T(8,128)(2,1)} %fusion.2.features, bf16[8,480,640]{2,1,0:T(8,128)(2,1)} %all-to-all-done.1.gated.vectors, bf16[400,512]{1,0:T(8,128)(2,1)} %get-tuple-element.27.own, bf16[400,512]{1,0:T(8,128)(2,1)} %copy-done.10, ...), custom_call_target="tpu_custom_call" | custom-call | flops 2264924160 | bytes 9912320 | tf_op jit(solution)/shard_map/pallas_call | solution.py:305
  125.6 6.6 %all-to-all-start.2 = ((bf16[8,72,640]{2,1,0:T(8,128)(2,1)}), bf16[8,72,640]{2,1,0:T(8,128)(2,1)S(1)}, u32[]{:S(2)}, u32[]{:S(2)}) async-start(bf16[8,72,640]{2,1,0:T(8,128)(2,1)} %get-tuple-element.29), calls=%async_computation.2 | async-start | bytes 1474560 | tf_op jit(solution)/shard_map/all_to_all | solution.py:187
  132.8 11.3 %all-to-all-done.2.arrived = bf16[8,72,640]{2,1,0:T(8,128)(2,1)S(1)} async-done(((bf16[8,72,640]{2,1,0:T(8,128)(2,1)}), bf16[8,72,640]{2,1,0:T(8,128)(2,1)S(1)}, u32[]{:S(2)}, u32[]{:S(2)}) %all-to-all-start.2) | async-done | bytes 737312 | tf_op jit(solution)/shard_map/all_to_all | solution.py:187
  144.1 1.1 copy-done.1
  145.3 0.9 copy-done.3
  146.2 0.3 shard_map.89
  146.5 14.1 %all_to_all.25.vectors = bf16[8,72,640]{2,1,0:T(8,128)(2,1)} all-to-all(bf16[8,72,640]{2,1,0:T(8,128)(2,1)S(1)} %get-tuple-element.31), channel_id=1, replica_groups=mesh['z'=16,'c'=2,'y'=4,'xa'=2,'xb'=2] {'y','xb'}, dimensions={0} | all-to-all | bytes 1474560 | tf_op jit(solution)/shard_map/all_to_all | solution.py:187
  160.5 7.2 %shard_map.90.own = bf16[400,512]{1,0:T(8,128)(2,1)} custom-call(bf16[384,64]{1,0:T(8,128)(2,1)} %fusion.2.features, bf16[8,480,640]{2,1,0:T(8,128)(2,1)} %all-to-all-done.1.gated.vectors, bf16[8,72,640]{2,1,0:T(8,128)(2,1)} %all_to_all.25.vectors, bf16[512,5120]{1,0:T(8,128)(2,1)} %get-tuple-element.28.refs_0_.refs_1_), custom_call_target="tpu_custom_call" | custom-call | flops 2264924160 | bytes 9912320 | tf_op jit(solution)/shard_map/pallas_call | solution.py:282
  167.7 1.9 collective-permute-start.10
  169.6 8.6 %collective-permute-done.10.other = bf16[400,512]{1,0:T(8,128)(2,1)S(1)} collective-permute-done((bf16[400,512]{1,0:T(8,128)(2,1)}, bf16[400,512]{1,0:T(8,128)(2,1)S(1)}, u32[]{:S(2)}, u32[]{:S(2)}) %collective-permute-start.10) | collective-permute-done | bytes 409632 | tf_op jit(solution)/shard_map/ppermute | solution.py:183
  178.2 0.8 copy-done.9
  179.0 9.1 %shard_map.91 = (bf16[8,72,640]{2,1,0:T(8,128)(2,1)}, f32[16,512]{1,0:T(8,128)}) custom-call(bf16[384,64]{1,0:T(8,128)(2,1)} %fusion.2.features, bf16[8,480,640]{2,1,0:T(8,128)(2,1)} %all-to-all-done.1.gated.vectors, bf16[400,512]{1,0:T(8,128)(2,1)} %shard_map.90.own, bf16[400,512]{1,0:T(8,128)(2,1)} %copy-done.9, ...), custom_call_target="tpu_custom_call" | custom-call | flops 2264924160 | bytes 9912320 | tf_op jit(solution)/shard_map/pallas_call | solution.py:305
  188.1 0.0 copy-start.5
  188.1 14.2 %all_to_all.26.arrived = bf16[8,72,640]{2,1,0:T(8,128)(2,1)S(1)} all-to-all(bf16[8,72,640]{2,1,0:T(8,128)(2,1)} %get-tuple-element.32), channel_id=1, replica_groups=mesh['z'=16,'c'=2,'y'=4,'xa'=2,'xb'=2] {'y','xb'}, dimensions={0} | all-to-all | bytes 1474560 | tf_op jit(solution)/shard_map/all_to_all | solution.py:187
  202.3 0.9 shard_map.92
  (24 shorter events, 0.3 us)
Async XLA Ops:
  0.6 30.1 %copy-start = (bf16[1,384,3584]{2,1,0:T(8,128)(2,1)S(1)}, bf16[1,384,3584]{2,1,0:T(8,128)(2,1)}, u32[]{:S(2)}) copy-start(bf16[1,384,3584]{2,1,0:T(8,128)(2,1)} %param.7) | copy-start | bytes 8257540
  2.5 11.9 %all-to-all-start = ((bf16[8,16,640]{2,1,0:T(8,128)(2,1)}), bf16[8,16,640]{2,1,0:T(8,128)(2,1)S(1)}, u32[]{:S(2)}, u32[]{:S(2)}) async-start(bf16[8,16,640]{2,1,0:T(8,128)(2,1)} %pad.4), calls=%async_computation | async-start | bytes 327680 | tf_op jit(solution)/shard_map/all_to_all | solution.py:187
  14.4 23.7 %collective-permute-start = (bf16[16,5120]{1,0:T(8,128)(2,1)S(1)}, bf16[16,5120]{1,0:T(8,128)(2,1)S(1)}, u32[]{:S(2)}, u32[]{:S(2)}) collective-permute-start(bf16[16,5120]{1,0:T(8,128)(2,1)S(1)} %bitcast.22), channel_id=1, source_target_pairs={{0,160},{32,192},{64,224},{96,256},{128,288},{160,320},{192,352},{... | collective-permute-start | bytes 491528 | tf_op jit(solution)/shard_map/ppermute | solution.py:192
  24.9 23.3 %collective-permute-start.1 = (bf16[16,5120]{1,0:T(8,128)(2,1)S(1)}, bf16[16,5120]{1,0:T(8,128)(2,1)S(1)}, u32[]{:S(2)}, u32[]{:S(2)}) collective-permute-start(bf16[16,5120]{1,0:T(8,128)(2,1)S(1)} %bitcast.23), channel_id=1, source_target_pairs={{0,352},{32,384},{64,416},{96,448},{128,480},{160,0},{192,32},{224... | collective-permute-start | bytes 491528 | tf_op jit(solution)/shard_map/ppermute | solution.py:192
  33.3 61.2 %all-to-all-start.1 = ((bf16[8,480,640]{2,1,0:T(8,128)(2,1)}), bf16[8,480,640]{2,1,0:T(8,128)(2,1)}, u32[]{:S(2)}, u32[]{:S(2)}) async-start(bf16[8,480,640]{2,1,0:T(8,128)(2,1)} %shard_map.86), calls=%async_computation.1 | async-start | bytes 9830400 | tf_op jit(solution)/shard_map/all_to_all | solution.py:187
  48.2 17.4 %collective-permute-start.2 = (bf16[48,5120]{1,0:T(8,128)(2,1)S(1)}, bf16[48,5120]{1,0:T(8,128)(2,1)S(1)}, u32[]{:S(2)}, u32[]{:S(2)}) collective-permute-start(bf16[48,5120]{1,0:T(8,128)(2,1)S(1)} %pad_maximum_fusion), channel_id=1, source_target_pairs={{0,32},{32,64},{64,96},{96,128},{128,160},{160,192},{192,224},{224... | collective-permute-start | bytes 1474568 | tf_op jit(solution)/shard_map/ppermute | solution.py:192
  50.1 16.7 %collective-permute-start.3 = (bf16[48,5120]{1,0:T(8,128)(2,1)S(1)}, bf16[48,5120]{1,0:T(8,128)(2,1)S(1)}, u32[]{:S(2)}, u32[]{:S(2)}) collective-permute-start(bf16[48,5120]{1,0:T(8,128)(2,1)S(1)} %pad_maximum_fusion), channel_id=1, source_target_pairs={{0,480},{32,0},{64,32},{96,64},{128,96},{160,128},{192,160},{224,1... | collective-permute-start | bytes 1474568 | tf_op jit(solution)/shard_map/ppermute | solution.py:192
  66.8 16.6 %collective-permute-start.6 = (bf16[16,5120]{1,0:T(8,128)(2,1)S(1)}, bf16[16,5120]{1,0:T(8,128)(2,1)S(1)}, u32[]{:S(2)}, u32[]{:S(2)}) collective-permute-start(bf16[16,5120]{1,0:T(8,128)(2,1)S(1)} %slice_select_fusion), channel_id=1, source_target_pairs={{0,64},{32,96},{64,128},{96,160},{128,192},{160,224},{192,256},{22... | collective-permute-start | bytes 491528 | tf_op jit(solution)/shard_map/ppermute | solution.py:218
  73.2 14.8 %collective-permute-start.4 = (bf16[48,5120]{1,0:T(8,128)(2,1)S(1)}, bf16[48,5120]{1,0:T(8,128)(2,1)S(1)}, u32[]{:S(2)}, u32[]{:S(2)}) collective-permute-start(bf16[48,5120]{1,0:T(8,128)(2,1)S(1)} %collective-permute-done.2), channel_id=1, source_target_pairs={{0,32},{32,64},{64,96},{96,128},{128,160},{160,192},{192,224},{224... | collective-permute-start | bytes 1474568 | tf_op jit(solution)/shard_map/ppermute | solution.py:192
  78.1 11.0 %collective-permute-start.5 = (bf16[48,5120]{1,0:T(8,128)(2,1)S(1)}, bf16[48,5120]{1,0:T(8,128)(2,1)S(1)}, u32[]{:S(2)}, u32[]{:S(2)}) collective-permute-start(bf16[48,5120]{1,0:T(8,128)(2,1)S(1)} %collective-permute-done.3), channel_id=1, source_target_pairs={{0,480},{32,0},{64,32},{96,64},{128,96},{160,128},{192,160},{224,1... | collective-permute-start | bytes 1474568 | tf_op jit(solution)/shard_map/ppermute | solution.py:192
  80.3 1.1 copy-start.6
  81.5 9.6 %collective-permute-start.7 = (bf16[144,5120]{1,0:T(8,128)(2,1)S(1)}, bf16[144,5120]{1,0:T(8,128)(2,1)S(1)}, u32[]{:S(2)}, u32[]{:S(2)}) collective-permute-start(bf16[144,5120]{1,0:T(8,128)(2,1)S(1)} %constant_dynamic-update-slice_fusion.refs_0_), channel_id=1, source_target_pairs={{0,16},{16,0},{1,17},{17,1},{2,18},{18,2},{3,19},{19,3},{4,20},{20... | collective-permute-start | bytes 4423688 | tf_op jit(solution)/shard_map/ppermute | solution.py:196
  89.2 2.0 copy-start.7
  89.2 4.8 %collective-permute-start.8 = (bf16[112,5120]{1,0:T(8,128)(2,1)S(1)}, bf16[112,5120]{1,0:T(8,128)(2,1)}, u32[]{:S(2)}, u32[]{:S(2)}) collective-permute-start(bf16[112,5120]{1,0:T(8,128)(2,1)S(1)} %constant_dynamic-update-slice_fusion.3.refs_1_), channel_id=1, source_target_pairs={{0,16},{16,0},{1,17},{17,1},{2,18},{18,2},{3,19},{19,3},{4,20},{20... | collective-permute-start | bytes 3440648 | tf_op jit(solution)/shard_map/ppermute | solution.py:196
  91.1 1.2 copy-start.8
  103.1 13.1 %collective-permute-start.9 = (bf16[400,512]{1,0:T(8,128)(2,1)}, bf16[400,512]{1,0:T(8,128)(2,1)S(1)}, u32[]{:S(2)}, u32[]{:S(2)}) collective-permute-start(bf16[400,512]{1,0:T(8,128)(2,1)} %get-tuple-element.27.own), channel_id=1, source_target_pairs={{0,3},{3,0},{1,2},{2,1},{4,7},{7,4},{5,6},{6,5},{8,11},{11,8},{9,1... | collective-permute-start | bytes 1228808 | tf_op jit(solution)/shard_map/ppermute | solution.py:183
  116.2 0.7 copy-start.10
  125.6 18.5 %all-to-all-start.2 = ((bf16[8,72,640]{2,1,0:T(8,128)(2,1)}), bf16[8,72,640]{2,1,0:T(8,128)(2,1)S(1)}, u32[]{:S(2)}, u32[]{:S(2)}) async-start(bf16[8,72,640]{2,1,0:T(8,128)(2,1)} %get-tuple-element.29), calls=%async_computation.2 | async-start | bytes 1474560 | tf_op jit(solution)/shard_map/all_to_all | solution.py:187
  144.1 1.1 copy-start.1
  145.3 0.9 copy-start.3
  167.7 10.6 %collective-permute-start.10 = (bf16[400,512]{1,0:T(8,128)(2,1)}, bf16[400,512]{1,0:T(8,128)(2,1)S(1)}, u32[]{:S(2)}, u32[]{:S(2)}) collective-permute-start(bf16[400,512]{1,0:T(8,128)(2,1)} %shard_map.90.own), channel_id=1, source_target_pairs={{0,3},{3,0},{1,2},{2,1},{4,7},{7,4},{5,6},{6,5},{8,11},{11,8},{9,1... | collective-permute-start | bytes 1228808 | tf_op jit(solution)/shard_map/ppermute | solution.py:183
  178.2 0.8 copy-start.9
  188.1 14.2 %copy-start.2 = (f32[400,512]{1,0:T(8,128)S(1)}, f32[400,512]{1,0:T(8,128)}, u32[]{:S(2)}) copy-start(f32[400,512]{1,0:T(8,128)} %get-tuple-element.30.tail.refs_0_.tail_was) | copy-start | bytes 2457604
  188.1 14.2 %copy-start.4 = (f32[1,64,640]{2,1,0:T(8,128)S(1)}, f32[1,64,640]{2,1,0:T(8,128)}, u32[]{:S(2)}) copy-start(f32[1,64,640]{2,1,0:T(8,128)} %param.13) | copy-start | bytes 491524
  188.1 14.2 %copy-start.5 = (f32[16,512]{1,0:T(8,128)S(1)}, f32[16,512]{1,0:T(8,128)}, u32[]{:S(2)}) copy-start(f32[16,512]{1,0:T(8,128)} %get-tuple-element.33.tail) | copy-start | bytes 98308

commit v6 on v5

--- a/solution.py
+++ b/solution.py
@@ -14,7 +14,7 @@
 ALL = ("y", "xa", "xb")
 EXTRA = 8
 TAIL = 16
-LATER = 56
+FIRST, LATER = 56, 53
 TOGETHER = 2
 
 
@@ -106,8 +106,9 @@
 
 
 def backward(rank, second_pass, features, gated, own, other, *refs):
-    before, refs = (refs[0], refs[1:]) if second_pass else (None, refs)
-    weights, message, kept, mixed, norm = refs
+    if second_pass:
+        before, rows_before, *refs = refs
+    weights, message, *kept, mixed, norm = refs
     step = pl.program_id(0)
     tokens = features.shape[0]
 
@@ -115,13 +116,12 @@
     def _():
         value = own[:tokens, :].astype(F32) + other[:tokens, :].astype(F32)
         rows = own[tokens:, :].astype(F32) + other[tokens:, :].astype(F32)
+        kept[0][...] = rows
         if second_pass:
-            kept[...] = rows
-            ratio = from_pieces(rows, 0)[:, :1] / from_pieces(before[tokens:, :], 0)[:, :1]
-            value = value + everywhere(ratio, value.shape) * before[:tokens, :]
+            ratio = from_pieces(rows, 0)[:, :1] / from_pieces(rows_before[...], 0)[:, :1]
+            value = value + everywhere(ratio, value.shape) * before[...]
         else:
-            kept[:tokens, :] = value
-            kept[tokens:, :] = rows
+            kept[1][...] = value
         rounded = value.astype(BF16)
         mixed[...] = rounded
         norm[...] = jnp.broadcast_to(total(value * rounded.astype(F32)), norm.shape)
@@ -295,34 +295,35 @@
                 pltpu.VMEM((tokens, width), F32),
                 pltpu.VMEM((EXTRA, width), F32),
             ],
-            compiler_params=params(56 if len(pieces) > 1 else LATER),
+            compiler_params=params(FIRST if len(pieces) > 1 else LATER),
             cost_estimate=cost,
         )(features, gated, vectors, *pieces)
         return (own, swapped(own)), weights
 
     def product_shares(weights, own, other, *before):
-        kept_shape = (TAIL, width) if before else partial_shape
-        message, kept = pl.pallas_call(
+        kept = [(TAIL, width)] if before else [(TAIL, width), (tokens, width)]
+        message, *kept = pl.pallas_call(
             functools.partial(backward, rank, bool(before)),
             grid=(steps,),
             in_specs=[whole((tokens, rank)), block_gated]
-            + [whole(partial_shape)] * (2 + len(before))
+            + [whole(partial_shape)] * 2
+            + [whole(array.shape) for array in before]
             + [block_weights(weights)],
-            out_specs=[block_message, whole(kept_shape)],
-            out_shape=[message_shape, jax.ShapeDtypeStruct(kept_shape, F32)],
+            out_specs=[block_message] + [whole(shape) for shape in kept],
+            out_shape=[message_shape] + [jax.ShapeDtypeStruct(shape, F32) for shape in kept],
             scratch_shapes=[pltpu.VMEM((tokens, width), BF16), pltpu.VMEM((8, 128), F32)],
             compiler_params=params(LATER),
             cost_estimate=cost,
         )(features, gated, own, other, *before, weights)
-        return exchanged(message), kept
-
-    tail = pl.BlockSpec((TAIL, width), lambda i: (tokens // TAIL, 0))
+        return exchanged(message), *kept
+
+    tail = whole((TAIL, width))
     full_message = whole(message_shape.shape)
     full_state = whole(state.shape)
     full_alpha = whole((8, units))
 
     shares, (weights,) = mixed_shares(gated, pieces)
-    arrived, first = product_shares(weights, *shares)
+    arrived, rows_first, first = product_shares(weights, *shares)
     message, residual, alpha = pl.pallas_call(
         functools.partial(update, rank),
         grid=(1,),
@@ -330,18 +331,18 @@
         out_specs=[full_message, full_state, full_alpha],
         out_shape=[message_shape, state, jax.ShapeDtypeStruct((8, units), F32)],
         compiler_params=params(8),
-    )(live, damping, arrived, target, first)
+    )(live, damping, arrived, target, rows_first)
     shares, _ = mixed_shares(exchanged(message), [weights])
-    arrived, second = product_shares(weights, *shares, first)
+    arrived, rows_second = product_shares(weights, *shares, first, rows_first)
     x, left = pl.pallas_call(
         functools.partial(finish, rank),
         grid=(1,),
-        in_specs=[SCALAR, SCALAR, full_message, full_state, whole((TAIL, width)), tail]
+        in_specs=[SCALAR, SCALAR, full_message, full_state, tail, tail]
         + [full_state, full_alpha],
         out_specs=[full_state, full_state],
         out_shape=[state, state],
         compiler_params=params(8),
-    )(live, damping, arrived, target, second, first, residual, alpha)
+    )(live, damping, arrived, target, rows_second, rows_first, residual, alpha)
     return (x[None], left[None])
 
 

time: 204 us -> 201 us (0.985)
  local copies, waits for them, and re-layouts: 7.88 us -> 5.17 us
    unnamed x26 -> x22, local copies, waits for them, and re-layouts: 6.02 us -> 3.32 us
where the time goes in v6:
time: 201 us; the launch traced here: 200 us
  starting transfers between devices  63.1 us (31%)
  waiting for transfers between devices  60.3 us (30%)
  Pallas kernels  38.7 us (19%)
  blocking collectives  28.1 us (14%)
  local copies, waits for them, and re-layouts  5.17 us (3%)
  matrix products  2.51 us (1%)
  between operations  2.21 us (1%)
    ppermute x6, starting transfers between devices, shifted(): return lax.ppermute(array, 'z', [(i, (i + by) % size) for i in range(size)])  31.7 us
    all_to_all x2, blocking collectives, exchanged(): return lax.all_to_all(array, HALF, split_axis=0, concat_axis=0, tiled=True)  28.1 us
    ppermute x6, waiting for transfers between devices, shifted(): return lax.ppermute(array, 'z', [(i, (i + by) % size) for i in range(size)])  27 us
    ppermute x2, waiting for transfers between devices, swapped(): return lax.ppermute(array, ROW, [(0, 3), (3, 0), (1, 2), (2, 1)])  19.1 us
    pallas_call x2, Pallas kernels, product_shares(): pl.pallas_call(functools.partial(backward, rank, bool(before)), grid=(ste...  17.2 us
    all_to_all x3, starting transfers between devices, exchanged(): return lax.all_to_all(array, HALF, split_axis=0, concat_axis=0, tiled=True)  16.4 us
    pallas_call x2, Pallas kernels, mixed_shares(): pl.pallas_call(functools.partial(forward, rank, len(pieces)), grid=(steps...  15 us
    all_to_all x3, waiting for transfers between devices, exchanged(): return lax.all_to_all(array, HALF, split_axis=0, concat_axis=0, tiled=True)  12.5 us
  transfers between devices with their start and end apart: 14, of which 11 were waited for; matrix products, arithmetic and copies ran while one was open for 1% of the time, Pallas kernels for 3%

profile of v6, /device:TPU:4, one launch (start us, length us, event | category | flops | bytes accessed | tf_op | source)
XLA Modules:
  0.0 200.1 jit_solution(3574453996261209194)
XLA Ops:
  0.6 0.0 copy-start
  0.7 1.1 reshape.13
  1.8 0.7 pad.4
  2.5 5.1 %all-to-all-start = ((bf16[8,16,640]{2,1,0:T(8,128)(2,1)}), bf16[8,16,640]{2,1,0:T(8,128)(2,1)S(1)}, u32[]{:S(2)}, u32[]{:S(2)}) async-start(bf16[8,16,640]{2,1,0:T(8,128)(2,1)} %pad.4), calls=%async_computation | async-start | bytes 327680 | tf_op jit(solution)/shard_map/all_to_all | solution.py:187
  8.2 5.3 %shard_map.86 = bf16[8,480,640]{2,1,0:T(8,128)(2,1)} custom-call(s32[1]{0:T(128)S(6)} %copy.21.live, bf16[384,640]{1,0:T(8,128)(2,1)} %bitcast.25, f32[64,640]{1,0:T(8,128)} %bitcast.17), custom_call_target="tpu_custom_call" | custom-call | flops 1966080 | bytes 4915200 | tf_op jit(solution)/shard_map/pallas_call | solution.py:240
  13.5 0.9 all-to-all-done
  14.4 10.5 %collective-permute-start = (bf16[16,5120]{1,0:T(8,128)(2,1)S(1)}, bf16[16,5120]{1,0:T(8,128)(2,1)S(1)}, u32[]{:S(2)}, u32[]{:S(2)}) collective-permute-start(bf16[16,5120]{1,0:T(8,128)(2,1)S(1)} %bitcast.22), channel_id=1, source_target_pairs={{0,160},{32,192},{64,224},{96,256},{128,288},{160,320},{192,352},{... | collective-permute-start | bytes 491528 | tf_op jit(solution)/shard_map/ppermute | solution.py:192
  24.9 5.9 %collective-permute-start.1 = (bf16[16,5120]{1,0:T(8,128)(2,1)S(1)}, bf16[16,5120]{1,0:T(8,128)(2,1)S(1)}, u32[]{:S(2)}, u32[]{:S(2)}) collective-permute-start(bf16[16,5120]{1,0:T(8,128)(2,1)S(1)} %bitcast.23), channel_id=1, source_target_pairs={{0,352},{32,384},{64,416},{96,448},{128,480},{160,0},{192,32},{224... | collective-permute-start | bytes 491528 | tf_op jit(solution)/shard_map/ppermute | solution.py:192
  30.8 2.5 %fusion.2.features = bf16[384,64]{1,0:T(8,128)(2,1)} fusion(bf16[1,384,3584]{2,1,0:T(8,128)(2,1)S(1)} %copy-done, bf16[1,3584,64]{1,2,0:T(8,128)(2,1)} %param.8), kind=kOutput, calls=%fused_computation.2 | convolution fusion | flops 176185344 | bytes 3260416 | tf_op jit(solution)/shard_map/dot_general | solution.py:259
  33.3 4.8 %all-to-all-start.1 = ((bf16[8,480,640]{2,1,0:T(8,128)(2,1)}), bf16[8,480,640]{2,1,0:T(8,128)(2,1)}, u32[]{:S(2)}, u32[]{:S(2)}) async-start(bf16[8,480,640]{2,1,0:T(8,128)(2,1)} %shard_map.86), calls=%async_computation.1 | async-start | bytes 9830400 | tf_op jit(solution)/shard_map/all_to_all | solution.py:187
  38.1 0.0 collective-permute-done
  38.1 10.1 %collective-permute-done.1 = bf16[16,5120]{1,0:T(8,128)(2,1)S(1)} collective-permute-done((bf16[16,5120]{1,0:T(8,128)(2,1)S(1)}, bf16[16,5120]{1,0:T(8,128)(2,1)S(1)}, u32[]{:S(2)}, u32[]{:S(2)}) %collective-permute-start.1) | collective-permute-done | bytes 163872 | tf_op jit(solution)/shard_map/ppermute | solution.py:192
  48.2 1.9 collective-permute-start.2
  50.1 6.4 %collective-permute-start.3 = (bf16[48,5120]{1,0:T(8,128)(2,1)S(1)}, bf16[48,5120]{1,0:T(8,128)(2,1)S(1)}, u32[]{:S(2)}, u32[]{:S(2)}) collective-permute-start(bf16[48,5120]{1,0:T(8,128)(2,1)S(1)} %pad_maximum_fusion), channel_id=1, source_target_pairs={{0,480},{32,0},{64,32},{96,64},{128,96},{160,128},{192,160},{224,1... | collective-permute-start | bytes 1474568 | tf_op jit(solution)/shard_map/ppermute | solution.py:192
  56.6 9.0 %collective-permute-done.2 = bf16[48,5120]{1,0:T(8,128)(2,1)S(1)} collective-permute-done((bf16[48,5120]{1,0:T(8,128)(2,1)S(1)}, bf16[48,5120]{1,0:T(8,128)(2,1)S(1)}, u32[]{:S(2)}, u32[]{:S(2)}) %collective-permute-start.2) | collective-permute-done | bytes 491552 | tf_op jit(solution)/shard_map/ppermute | solution.py:192
  65.6 1.2 collective-permute-done.3
  66.8 6.4 %collective-permute-start.6 = (bf16[16,5120]{1,0:T(8,128)(2,1)S(1)}, bf16[16,5120]{1,0:T(8,128)(2,1)S(1)}, u32[]{:S(2)}, u32[]{:S(2)}) collective-permute-start(bf16[16,5120]{1,0:T(8,128)(2,1)S(1)} %slice_select_fusion), channel_id=1, source_target_pairs={{0,64},{32,96},{64,128},{96,160},{128,192},{160,224},{192,256},{22... | collective-permute-start | bytes 491528 | tf_op jit(solution)/shard_map/ppermute | solution.py:218
  73.2 4.9 %collective-permute-start.4 = (bf16[48,5120]{1,0:T(8,128)(2,1)S(1)}, bf16[48,5120]{1,0:T(8,128)(2,1)S(1)}, u32[]{:S(2)}, u32[]{:S(2)}) collective-permute-start(bf16[48,5120]{1,0:T(8,128)(2,1)S(1)} %collective-permute-done.2), channel_id=1, source_target_pairs={{0,32},{32,64},{64,96},{96,128},{128,160},{160,192},{192,224},{224... | collective-permute-start | bytes 1474568 | tf_op jit(solution)/shard_map/ppermute | solution.py:192
  78.0 2.2 %collective-permute-start.5 = (bf16[48,5120]{1,0:T(8,128)(2,1)S(1)}, bf16[48,5120]{1,0:T(8,128)(2,1)S(1)}, u32[]{:S(2)}, u32[]{:S(2)}) collective-permute-start(bf16[48,5120]{1,0:T(8,128)(2,1)S(1)} %collective-permute-done.3), channel_id=1, source_target_pairs={{0,480},{32,0},{64,32},{96,64},{128,96},{160,128},{192,160},{224,1... | collective-permute-start | bytes 1474568 | tf_op jit(solution)/shard_map/ppermute | solution.py:192
  80.3 0.0 copy-start.6
  80.3 1.9 collective-permute-start.7
  82.3 0.0 collective-permute-done.6
  82.3 5.7 %collective-permute-done.4 = bf16[48,5120]{1,0:T(8,128)(2,1)S(1)} collective-permute-done((bf16[48,5120]{1,0:T(8,128)(2,1)S(1)}, bf16[48,5120]{1,0:T(8,128)(2,1)S(1)}, u32[]{:S(2)}, u32[]{:S(2)}) %collective-permute-start.4) | collective-permute-done | bytes 491552 | tf_op jit(solution)/shard_map/ppermute | solution.py:192
  88.0 1.1 collective-permute-done.5
  89.1 0.0 copy-done.6
  89.2 0.0 copy-start.1
  89.2 2.1 %collective-permute-start.8 = (bf16[112,5120]{1,0:T(8,128)(2,1)S(1)}, bf16[112,5120]{1,0:T(8,128)(2,1)}, u32[]{:S(2)}, u32[]{:S(2)}) collective-permute-start(bf16[112,5120]{1,0:T(8,128)(2,1)S(1)} %constant_dynamic-update-slice_fusion.3.refs_1_), channel_id=1, source_target_pairs={{0,16},{16,0},{1,17},{17,1},{2,18},{18,2},{3,19},{19,3},{4,20},{20... | collective-permute-start | bytes 3440648 | tf_op jit(solution)/shard_map/ppermute | solution.py:196
  91.2 0.0 collective-permute-done.7.refs_2_
  91.3 1.2 copy-done.8
  92.5 1.7 collective-permute-done.8.refs_3_
  94.1 0.4 all-to-all-done.1.gated.vectors
  94.5 8.6 %shard_map.87 = (bf16[400,512]{1,0:T(8,128)(2,1)}, bf16[512,5120]{1,0:T(8,128)(2,1)}) custom-call(bf16[384,64]{1,0:T(8,128)(2,1)} %fusion.2.features, bf16[8,480,640]{2,1,0:T(8,128)(2,1)} %all-to-all-done.1.gated.vectors, bf16[8,480,640]{2,1,0:T(8,128)(2,1)} %all-to-all-done.1.gated.vectors, bf16[144,5120]{1,0:T(8,128)(2,1)} %copy-done.6, ...), custom_call_target="tpu_custom_call" | custom-call | flops 2264924160 | bytes 9912320 | tf_op jit(solution)/shard_map/pallas_call | solution.py:282
  103.1 2.6 %collective-permute-start.9 = (bf16[400,512]{1,0:T(8,128)(2,1)}, bf16[400,512]{1,0:T(8,128)(2,1)S(1)}, u32[]{:S(2)}, u32[]{:S(2)}) collective-permute-start(bf16[400,512]{1,0:T(8,128)(2,1)} %get-tuple-element.28.own), channel_id=1, source_target_pairs={{0,3},{3,0},{1,2},{2,1},{4,7},{7,4},{5,6},{6,5},{8,11},{11,8},{9,1... | collective-permute-start | bytes 1228808 | tf_op jit(solution)/shard_map/ppermute | solution.py:183
  105.8 10.6 %collective-permute-done.9.other = bf16[400,512]{1,0:T(8,128)(2,1)S(1)} collective-permute-done((bf16[400,512]{1,0:T(8,128)(2,1)}, bf16[400,512]{1,0:T(8,128)(2,1)S(1)}, u32[]{:S(2)}, u32[]{:S(2)}) %collective-permute-start.9) | collective-permute-done | bytes 409632 | tf_op jit(solution)/shard_map/ppermute | solution.py:183
  116.4 1.0 copy-done.5
  117.4 8.4 %shard_map.88 = (bf16[8,72,640]{2,1,0:T(8,128)(2,1)}, f32[16,512]{1,0:T(8,128)S(1)}, f32[384,512]{1,0:T(8,128)}) custom-call(bf16[384,64]{1,0:T(8,128)(2,1)S(1)} %copy-done.1, bf16[8,480,640]{2,1,0:T(8,128)(2,1)} %all-to-all-done.1.gated.vectors, bf16[400,512]{1,0:T(8,128)(2,1)S(1)} %copy-done.5, bf16[400,512]{1,0:T(8,128)(2,1)S(1)} %collective-permute-done.9.other, ...), custom_call_target="tpu_custom_call" | custom-call | flops 2264924160 | bytes 9912320 | tf_op jit(solution)/shard_map/pallas_call | solution.py:305
  125.8 6.6 %all-to-all-start.2 = ((bf16[8,72,640]{2,1,0:T(8,128)(2,1)}), bf16[8,72,640]{2,1,0:T(8,128)(2,1)S(1)}, u32[]{:S(2)}, u32[]{:S(2)}) async-start(bf16[8,72,640]{2,1,0:T(8,128)(2,1)} %get-tuple-element.30), calls=%async_computation.2 | async-start | bytes 1474560 | tf_op jit(solution)/shard_map/all_to_all | solution.py:187
  133.0 11.2 %all-to-all-done.2.arrived = bf16[8,72,640]{2,1,0:T(8,128)(2,1)S(1)} async-done(((bf16[8,72,640]{2,1,0:T(8,128)(2,1)}), bf16[8,72,640]{2,1,0:T(8,128)(2,1)S(1)}, u32[]{:S(2)}, u32[]{:S(2)}) %all-to-all-start.2) | async-done | bytes 737312 | tf_op jit(solution)/shard_map/all_to_all | solution.py:187
  144.2 0.9 copy-done.3
  145.1 0.3 shard_map.89
  145.5 14.0 %all_to_all.25.vectors = bf16[8,72,640]{2,1,0:T(8,128)(2,1)} all-to-all(bf16[8,72,640]{2,1,0:T(8,128)(2,1)S(1)} %get-tuple-element.32), channel_id=1, replica_groups=mesh['z'=16,'c'=2,'y'=4,'xa'=2,'xb'=2] {'y','xb'}, dimensions={0} | all-to-all | bytes 1474560 | tf_op jit(solution)/shard_map/all_to_all | solution.py:187
  159.5 6.4 %shard_map.90.own = bf16[400,512]{1,0:T(8,128)(2,1)S(1)} custom-call(bf16[384,64]{1,0:T(8,128)(2,1)S(1)} %copy-done.2, bf16[8,480,640]{2,1,0:T(8,128)(2,1)} %all-to-all-done.1.gated.vectors, bf16[8,72,640]{2,1,0:T(8,128)(2,1)} %all_to_all.25.vectors, bf16[512,5120]{1,0:T(8,128)(2,1)} %get-tuple-element.29.refs_0_.refs_2_), custom_call_target="tpu_custom_call" | custom-call | flops 2264924160 | bytes 9912320 | tf_op jit(solution)/shard_map/pallas_call | solution.py:282
  165.9 1.9 collective-permute-start.10
  167.8 8.5 %collective-permute-done.10.other = bf16[400,512]{1,0:T(8,128)(2,1)S(1)} collective-permute-done((bf16[400,512]{1,0:T(8,128)(2,1)S(1)}, bf16[400,512]{1,0:T(8,128)(2,1)S(1)}, u32[]{:S(2)}, u32[]{:S(2)}) %collective-permute-start.10) | collective-permute-done | bytes 409632 | tf_op jit(solution)/shard_map/ppermute | solution.py:183
  176.3 8.8 %shard_map.91 = (bf16[8,72,640]{2,1,0:T(8,128)(2,1)}, f32[16,512]{1,0:T(8,128)S(1)}) custom-call(bf16[384,64]{1,0:T(8,128)(2,1)S(1)} %copy-done.2, bf16[8,480,640]{2,1,0:T(8,128)(2,1)} %all-to-all-done.1.gated.vectors, bf16[400,512]{1,0:T(8,128)(2,1)S(1)} %shard_map.90.own, bf16[400,512]{1,0:T(8,128)(2,1)S(1)} %collective-permute-done.10.other, ...), custom_call_target="tpu_custom_call" | custom-call | flops 2264924160 | bytes 9912320 | tf_op jit(solution)/shard_map/pallas_call | solution.py:305
  185.0 14.1 %all_to_all.26.arrived = bf16[8,72,640]{2,1,0:T(8,128)(2,1)S(1)} all-to-all(bf16[8,72,640]{2,1,0:T(8,128)(2,1)} %get-tuple-element.34), channel_id=1, replica_groups=mesh['z'=16,'c'=2,'y'=4,'xa'=2,'xb'=2] {'y','xb'}, dimensions={0} | all-to-all | bytes 1474560 | tf_op jit(solution)/shard_map/all_to_all | solution.py:187
  199.2 0.0 copy-done.4
  199.2 0.9 shard_map.92
  (20 shorter events, 0.3 us)
Async XLA Ops:
  0.6 30.1 %copy-start = (bf16[1,384,3584]{2,1,0:T(8,128)(2,1)S(1)}, bf16[1,384,3584]{2,1,0:T(8,128)(2,1)}, u32[]{:S(2)}) copy-start(bf16[1,384,3584]{2,1,0:T(8,128)(2,1)} %param.7) | copy-start | bytes 8257540
  2.5 11.9 %all-to-all-start = ((bf16[8,16,640]{2,1,0:T(8,128)(2,1)}), bf16[8,16,640]{2,1,0:T(8,128)(2,1)S(1)}, u32[]{:S(2)}, u32[]{:S(2)}) async-start(bf16[8,16,640]{2,1,0:T(8,128)(2,1)} %pad.4), calls=%async_computation | async-start | bytes 327680 | tf_op jit(solution)/shard_map/all_to_all | solution.py:187
  14.4 23.6 %collective-permute-start = (bf16[16,5120]{1,0:T(8,128)(2,1)S(1)}, bf16[16,5120]{1,0:T(8,128)(2,1)S(1)}, u32[]{:S(2)}, u32[]{:S(2)}) collective-permute-start(bf16[16,5120]{1,0:T(8,128)(2,1)S(1)} %bitcast.22), channel_id=1, source_target_pairs={{0,160},{32,192},{64,224},{96,256},{128,288},{160,320},{192,352},{... | collective-permute-start | bytes 491528 | tf_op jit(solution)/shard_map/ppermute | solution.py:192
  24.9 23.3 %collective-permute-start.1 = (bf16[16,5120]{1,0:T(8,128)(2,1)S(1)}, bf16[16,5120]{1,0:T(8,128)(2,1)S(1)}, u32[]{:S(2)}, u32[]{:S(2)}) collective-permute-start(bf16[16,5120]{1,0:T(8,128)(2,1)S(1)} %bitcast.23), channel_id=1, source_target_pairs={{0,352},{32,384},{64,416},{96,448},{128,480},{160,0},{192,32},{224... | collective-permute-start | bytes 491528 | tf_op jit(solution)/shard_map/ppermute | solution.py:192
  33.3 61.2 %all-to-all-start.1 = ((bf16[8,480,640]{2,1,0:T(8,128)(2,1)}), bf16[8,480,640]{2,1,0:T(8,128)(2,1)}, u32[]{:S(2)}, u32[]{:S(2)}) async-start(bf16[8,480,640]{2,1,0:T(8,128)(2,1)} %shard_map.86), calls=%async_computation.1 | async-start | bytes 9830400 | tf_op jit(solution)/shard_map/all_to_all | solution.py:187
  48.2 17.4 %collective-permute-start.2 = (bf16[48,5120]{1,0:T(8,128)(2,1)S(1)}, bf16[48,5120]{1,0:T(8,128)(2,1)S(1)}, u32[]{:S(2)}, u32[]{:S(2)}) collective-permute-start(bf16[48,5120]{1,0:T(8,128)(2,1)S(1)} %pad_maximum_fusion), channel_id=1, source_target_pairs={{0,32},{32,64},{64,96},{96,128},{128,160},{160,192},{192,224},{224... | collective-permute-start | bytes 1474568 | tf_op jit(solution)/shard_map/ppermute | solution.py:192
  50.1 16.7 %collective-permute-start.3 = (bf16[48,5120]{1,0:T(8,128)(2,1)S(1)}, bf16[48,5120]{1,0:T(8,128)(2,1)S(1)}, u32[]{:S(2)}, u32[]{:S(2)}) collective-permute-start(bf16[48,5120]{1,0:T(8,128)(2,1)S(1)} %pad_maximum_fusion), channel_id=1, source_target_pairs={{0,480},{32,0},{64,32},{96,64},{128,96},{160,128},{192,160},{224,1... | collective-permute-start | bytes 1474568 | tf_op jit(solution)/shard_map/ppermute | solution.py:192
  66.8 15.5 %collective-permute-start.6 = (bf16[16,5120]{1,0:T(8,128)(2,1)S(1)}, bf16[16,5120]{1,0:T(8,128)(2,1)S(1)}, u32[]{:S(2)}, u32[]{:S(2)}) collective-permute-start(bf16[16,5120]{1,0:T(8,128)(2,1)S(1)} %slice_select_fusion), channel_id=1, source_target_pairs={{0,64},{32,96},{64,128},{96,160},{128,192},{160,224},{192,256},{22... | collective-permute-start | bytes 491528 | tf_op jit(solution)/shard_map/ppermute | solution.py:218
  73.2 14.8 %collective-permute-start.4 = (bf16[48,5120]{1,0:T(8,128)(2,1)S(1)}, bf16[48,5120]{1,0:T(8,128)(2,1)S(1)}, u32[]{:S(2)}, u32[]{:S(2)}) collective-permute-start(bf16[48,5120]{1,0:T(8,128)(2,1)S(1)} %collective-permute-done.2), channel_id=1, source_target_pairs={{0,32},{32,64},{64,96},{96,128},{128,160},{160,192},{192,224},{224... | collective-permute-start | bytes 1474568 | tf_op jit(solution)/shard_map/ppermute | solution.py:192
  78.0 11.0 %collective-permute-start.5 = (bf16[48,5120]{1,0:T(8,128)(2,1)S(1)}, bf16[48,5120]{1,0:T(8,128)(2,1)S(1)}, u32[]{:S(2)}, u32[]{:S(2)}) collective-permute-start(bf16[48,5120]{1,0:T(8,128)(2,1)S(1)} %collective-permute-done.3), channel_id=1, source_target_pairs={{0,480},{32,0},{64,32},{96,64},{128,96},{160,128},{192,160},{224,1... | collective-permute-start | bytes 1474568 | tf_op jit(solution)/shard_map/ppermute | solution.py:192
  80.3 8.8 %copy-start.6 = (bf16[144,5120]{1,0:T(8,128)(2,1)}, bf16[144,5120]{1,0:T(8,128)(2,1)S(1)}, u32[]{:S(2)}) copy-start(bf16[144,5120]{1,0:T(8,128)(2,1)S(1)} %constant_dynamic-update-slice_fusion.refs_0_) | copy-start | bytes 4423684
  80.3 10.9 %collective-permute-start.7 = (bf16[144,5120]{1,0:T(8,128)(2,1)S(1)}, bf16[144,5120]{1,0:T(8,128)(2,1)S(1)}, u32[]{:S(2)}, u32[]{:S(2)}) collective-permute-start(bf16[144,5120]{1,0:T(8,128)(2,1)S(1)} %constant_dynamic-update-slice_fusion.refs_0_), channel_id=1, source_target_pairs={{0,16},{16,0},{1,17},{17,1},{2,18},{18,2},{3,19},{19,3},{4,20},{20... | collective-permute-start | bytes 4423688 | tf_op jit(solution)/shard_map/ppermute | solution.py:196
  89.2 2.1 %copy-start.7 = (bf16[112,5120]{1,0:T(8,128)(2,1)}, bf16[112,5120]{1,0:T(8,128)(2,1)S(1)}, u32[]{:S(2)}) copy-start(bf16[112,5120]{1,0:T(8,128)(2,1)S(1)} %constant_dynamic-update-slice_fusion.3.refs_1_) | copy-start | bytes 3440644
  89.2 27.2 %copy-start.1 = (bf16[384,64]{1,0:T(8,128)(2,1)S(1)}, bf16[384,64]{1,0:T(8,128)(2,1)}, u32[]{:S(2)}) copy-start(bf16[384,64]{1,0:T(8,128)(2,1)} %fusion.2.features) | copy-start | bytes 147460
  89.2 5.0 %collective-permute-start.8 = (bf16[112,5120]{1,0:T(8,128)(2,1)S(1)}, bf16[112,5120]{1,0:T(8,128)(2,1)}, u32[]{:S(2)}, u32[]{:S(2)}) collective-permute-start(bf16[112,5120]{1,0:T(8,128)(2,1)S(1)} %constant_dynamic-update-slice_fusion.3.refs_1_), channel_id=1, source_target_pairs={{0,16},{16,0},{1,17},{17,1},{2,18},{18,2},{3,19},{19,3},{4,20},{20... | collective-permute-start | bytes 3440648 | tf_op jit(solution)/shard_map/ppermute | solution.py:196
  91.3 1.2 copy-start.8
  103.1 13.2 %collective-permute-start.9 = (bf16[400,512]{1,0:T(8,128)(2,1)}, bf16[400,512]{1,0:T(8,128)(2,1)S(1)}, u32[]{:S(2)}, u32[]{:S(2)}) collective-permute-start(bf16[400,512]{1,0:T(8,128)(2,1)} %get-tuple-element.28.own), channel_id=1, source_target_pairs={{0,3},{3,0},{1,2},{2,1},{4,7},{7,4},{5,6},{6,5},{8,11},{11,8},{9,1... | collective-permute-start | bytes 1228808 | tf_op jit(solution)/shard_map/ppermute | solution.py:183
  116.4 1.0 copy-start.5
  125.8 18.4 %all-to-all-start.2 = ((bf16[8,72,640]{2,1,0:T(8,128)(2,1)}), bf16[8,72,640]{2,1,0:T(8,128)(2,1)S(1)}, u32[]{:S(2)}, u32[]{:S(2)}) async-start(bf16[8,72,640]{2,1,0:T(8,128)(2,1)} %get-tuple-element.30), calls=%async_computation.2 | async-start | bytes 1474560 | tf_op jit(solution)/shard_map/all_to_all | solution.py:187
  144.2 15.3 %copy-start.2 = (bf16[384,64]{1,0:T(8,128)(2,1)S(1)}, bf16[384,64]{1,0:T(8,128)(2,1)}, u32[]{:S(2)}) copy-start(bf16[384,64]{1,0:T(8,128)(2,1)} %fusion.2.features) | copy-start | bytes 147460
  144.2 1.0 copy-start.3
  165.9 10.4 %collective-permute-start.10 = (bf16[400,512]{1,0:T(8,128)(2,1)S(1)}, bf16[400,512]{1,0:T(8,128)(2,1)S(1)}, u32[]{:S(2)}, u32[]{:S(2)}) collective-permute-start(bf16[400,512]{1,0:T(8,128)(2,1)S(1)} %shard_map.90.own), channel_id=1, source_target_pairs={{0,3},{3,0},{1,2},{2,1},{4,7},{7,4},{5,6},{6,5},{8,11},{11,8},{9,1... | collective-permute-start | bytes 1228808 | tf_op jit(solution)/shard_map/ppermute | solution.py:183
  185.0 14.1 %copy-start.4 = (f32[1,64,640]{2,1,0:T(8,128)S(1)}, f32[1,64,640]{2,1,0:T(8,128)}, u32[]{:S(2)}) copy-start(f32[1,64,640]{2,1,0:T(8,128)} %param.13) | copy-start | bytes 491524

commit v7 on v6

--- a/solution.py
+++ b/solution.py
@@ -15,7 +15,8 @@
 EXTRA = 8
 TAIL = 16
 FIRST, LATER = 56, 53
-TOGETHER = 2
+WIDER, TOGETHER = 4, 2
+CHUNK = 128
 
 
 def product(a, b, dims):
@@ -108,7 +109,7 @@
 def backward(rank, second_pass, features, gated, own, other, *refs):
     if second_pass:
         before, rows_before, *refs = refs
-    weights, message, *kept, mixed, norm = refs
+    weights, message, *kept, mixed, second, norm = refs
     step = pl.program_id(0)
     tokens = features.shape[0]
 
@@ -129,9 +130,12 @@
     units = gated.shape[2]
     pieces = in_pieces([norm[:1, :1]], (EXTRA, units))
     for j in range(gated.shape[0]):
-        back = product(mixed[...], weights[:, j * units : (j + 1) * units], ((1,), (0,)))
-        second = (gated[j].astype(F32) * back).astype(BF16)
-        message[j, :rank, :] = product(features[...], second, ((0,), (0,))).astype(BF16)
+        at = slice(j * units, (j + 1) * units)
+        for row in range(0, tokens, CHUNK):
+            part = slice(row, row + CHUNK)
+            back = product(mixed[part, :], weights[:, at], ((1,), (0,)))
+            second[part, at] = (gated[j, part, :].astype(F32) * back).astype(BF16)
+        message[j, :rank, :] = product(features[...], second[:, at], ((0,), (0,))).astype(BF16)
         message[j, rank:, :] = pieces
 
 
@@ -228,10 +232,10 @@
     rank = adapter_a.shape[2]
     target = grad_b[0]
     rows = rank + EXTRA
-    block_message = pl.BlockSpec((TOGETHER, rows, units), lambda i: (i, 0, 0))
-    block_gated = pl.BlockSpec((TOGETHER, tokens, units), lambda i: (i, 0, 0))
-    span = TOGETHER * units
-    steps = members // TOGETHER
+
+    def blocks(together, count, at=0):
+        return pl.BlockSpec((together, count, units), lambda i: (i, at, 0))
+
     message_shape = jax.ShapeDtypeStruct((members, rows, units), BF16)
     state = jax.ShapeDtypeStruct((rank, units), F32)
 
@@ -251,7 +255,6 @@
             transcendentals=tokens * units,
         ),
     )(lengths, gate_pre[0], target)
-    block_first = pl.BlockSpec((TOGETHER, first_rows, units), lambda i: (i, tokens // first_rows, 0))
     mine = width_block(down_w)
     mine, packed = lax.optimization_barrier((mine, packed))
     gated = exchanged(packed)
@@ -262,8 +265,8 @@
     pieces = all_blocks(near)
     width = sum(piece.shape[0] for piece in pieces)
 
-    def block_weights(array):
-        return pl.BlockSpec((array.shape[0], span), lambda i: (0, i))
+    def block_weights(array, together):
+        return pl.BlockSpec((array.shape[0], together * units), lambda i: (0, i))
 
     live = lengths.astype(F32)
     flops = 2 * tokens * units * members * (width + rank)
@@ -278,20 +281,22 @@
         specs = [whole(partial_shape)]
         if len(pieces) > 1:
             shapes.append(jax.ShapeDtypeStruct((width, units * members), BF16))
-            specs.append(block_weights(shapes[1]))
+            specs.append(block_weights(shapes[1], WIDER))
         own, *weights = pl.pallas_call(
             functools.partial(forward, rank, len(pieces)),
-            grid=(steps,),
+            grid=(members // WIDER,),
             in_specs=[
                 whole((tokens, rank)),
-                block_gated,
-                block_message if vectors is not gated else block_first,
+                blocks(WIDER, tokens),
+                blocks(WIDER, rows)
+                if vectors is not gated
+                else blocks(WIDER, first_rows, tokens // first_rows),
             ]
-            + [block_weights(piece) for piece in pieces],
+            + [block_weights(piece, WIDER) for piece in pieces],
             out_specs=specs,
             out_shape=shapes,
             scratch_shapes=[
-                pltpu.VMEM((tokens, span), BF16),
+                pltpu.VMEM((tokens, WIDER * units), BF16),
                 pltpu.VMEM((tokens, width), F32),
                 pltpu.VMEM((EXTRA, width), F32),
             ],
@@ -304,14 +309,18 @@
         kept = [(TAIL, width)] if before else [(TAIL, width), (tokens, width)]
         message, *kept = pl.pallas_call(
             functools.partial(backward, rank, bool(before)),
-            grid=(steps,),
-            in_specs=[whole((tokens, rank)), block_gated]
+            grid=(members // TOGETHER,),
+            in_specs=[whole((tokens, rank)), blocks(TOGETHER, tokens)]
             + [whole(partial_shape)] * 2
             + [whole(array.shape) for array in before]
-            + [block_weights(weights)],
-            out_specs=[block_message] + [whole(shape) for shape in kept],
+            + [block_weights(weights, TOGETHER)],
+            out_specs=[blocks(TOGETHER, rows)] + [whole(shape) for shape in kept],
             out_shape=[message_shape] + [jax.ShapeDtypeStruct(shape, F32) for shape in kept],
-            scratch_shapes=[pltpu.VMEM((tokens, width), BF16), pltpu.VMEM((8, 128), F32)],
+            scratch_shapes=[
+                pltpu.VMEM((tokens, width), BF16),
+                pltpu.VMEM((tokens, TOGETHER * units), BF16),
+                pltpu.VMEM((8, 128), F32),
+            ],
             compiler_params=params(LATER),
             cost_estimate=cost,
         )(features, gated, own, other, *before, weights)

time: 201 us -> 199 us (0.990)
  Pallas kernels: 38.7 us -> 36.4 us
    pallas_call x4, Pallas kernels: 32.2 us -> 29.9 us  [the longest x2 16 us: product_shares(): pl.pallas_call(functools.partial(backward, rank, bool(before)), grid=(mem...]
where the time goes in v7:
time: 199 us; the launch traced here: 198 us
  starting transfers between devices  63.1 us (32%)
  waiting for transfers between devices  60.3 us (30%)
  Pallas kernels  36.4 us (18%)
  blocking collectives  28.1 us (14%)
  local copies, waits for them, and re-layouts  5.17 us (3%)
  matrix products  2.51 us (1%)
  between operations  2.21 us (1%)
    ppermute x6, starting transfers between devices, shifted(): return lax.ppermute(array, 'z', [(i, (i + by) % size) for i in range(size)])  31.7 us
    all_to_all x2, blocking collectives, exchanged(): return lax.all_to_all(array, HALF, split_axis=0, concat_axis=0, tiled=True)  28.1 us
    ppermute x6, waiting for transfers between devices, shifted(): return lax.ppermute(array, 'z', [(i, (i + by) % size) for i in range(size)])  27 us
    ppermute x2, waiting for transfers between devices, swapped(): return lax.ppermute(array, ROW, [(0, 3), (3, 0), (1, 2), (2, 1)])  19.1 us
    all_to_all x3, starting transfers between devices, exchanged(): return lax.all_to_all(array, HALF, split_axis=0, concat_axis=0, tiled=True)  16.4 us
    pallas_call x2, Pallas kernels, product_shares(): pl.pallas_call(functools.partial(backward, rank, bool(before)), grid=(mem...  16 us
    pallas_call x2, Pallas kernels, mixed_shares(): pl.pallas_call(functools.partial(forward, rank, len(pieces)), grid=(membe...  13.9 us
    all_to_all x3, waiting for transfers between devices, exchanged(): return lax.all_to_all(array, HALF, split_axis=0, concat_axis=0, tiled=True)  12.5 us
  transfers between devices with their start and end apart: 14, of which 11 were waited for; matrix products, arithmetic and copies ran while one was open for 1% of the time, Pallas kernels for 3%

profile of v7, /device:TPU:4, one launch (start us, length us, event | category | flops | bytes accessed | tf_op | source)
XLA Modules:
  0.0 197.8 jit_solution(436931119802276558)
XLA Ops:
  0.6 0.0 copy-start
  0.7 1.1 reshape.13
  1.8 0.7 pad.4
  2.5 5.1 %all-to-all-start = ((bf16[8,16,640]{2,1,0:T(8,128)(2,1)}), bf16[8,16,640]{2,1,0:T(8,128)(2,1)S(1)}, u32[]{:S(2)}, u32[]{:S(2)}) async-start(bf16[8,16,640]{2,1,0:T(8,128)(2,1)} %pad.4), calls=%async_computation | async-start | bytes 327680 | tf_op jit(solution)/shard_map/all_to_all | solution.py:191
  8.2 5.3 %shard_map.86 = bf16[8,480,640]{2,1,0:T(8,128)(2,1)} custom-call(s32[1]{0:T(128)S(6)} %copy.21.live, bf16[384,640]{1,0:T(8,128)(2,1)} %bitcast.25, f32[64,640]{1,0:T(8,128)} %bitcast.17), custom_call_target="tpu_custom_call" | custom-call | flops 1966080 | bytes 4915200 | tf_op jit(solution)/shard_map/pallas_call | solution.py:244
  13.5 0.9 all-to-all-done
  14.4 10.5 %collective-permute-start = (bf16[16,5120]{1,0:T(8,128)(2,1)S(1)}, bf16[16,5120]{1,0:T(8,128)(2,1)S(1)}, u32[]{:S(2)}, u32[]{:S(2)}) collective-permute-start(bf16[16,5120]{1,0:T(8,128)(2,1)S(1)} %bitcast.22), channel_id=1, source_target_pairs={{0,160},{32,192},{64,224},{96,256},{128,288},{160,320},{192,352},{... | collective-permute-start | bytes 491528 | tf_op jit(solution)/shard_map/ppermute | solution.py:196
  24.9 5.9 %collective-permute-start.1 = (bf16[16,5120]{1,0:T(8,128)(2,1)S(1)}, bf16[16,5120]{1,0:T(8,128)(2,1)S(1)}, u32[]{:S(2)}, u32[]{:S(2)}) collective-permute-start(bf16[16,5120]{1,0:T(8,128)(2,1)S(1)} %bitcast.23), channel_id=1, source_target_pairs={{0,352},{32,384},{64,416},{96,448},{128,480},{160,0},{192,32},{224... | collective-permute-start | bytes 491528 | tf_op jit(solution)/shard_map/ppermute | solution.py:196
  30.8 0.0 copy-done
  30.8 2.5 %fusion.2.features = bf16[384,64]{1,0:T(8,128)(2,1)} fusion(bf16[1,384,3584]{2,1,0:T(8,128)(2,1)S(1)} %copy-done, bf16[1,3584,64]{1,2,0:T(8,128)(2,1)} %param.8), kind=kOutput, calls=%fused_computation.2 | convolution fusion | flops 176185344 | bytes 3260416 | tf_op jit(solution)/shard_map/dot_general | solution.py:262
  33.3 4.8 %all-to-all-start.1 = ((bf16[8,480,640]{2,1,0:T(8,128)(2,1)}), bf16[8,480,640]{2,1,0:T(8,128)(2,1)}, u32[]{:S(2)}, u32[]{:S(2)}) async-start(bf16[8,480,640]{2,1,0:T(8,128)(2,1)} %shard_map.86), calls=%async_computation.1 | async-start | bytes 9830400 | tf_op jit(solution)/shard_map/all_to_all | solution.py:191
  38.1 0.0 collective-permute-done
  38.1 10.1 %collective-permute-done.1 = bf16[16,5120]{1,0:T(8,128)(2,1)S(1)} collective-permute-done((bf16[16,5120]{1,0:T(8,128)(2,1)S(1)}, bf16[16,5120]{1,0:T(8,128)(2,1)S(1)}, u32[]{:S(2)}, u32[]{:S(2)}) %collective-permute-start.1) | collective-permute-done | bytes 163872 | tf_op jit(solution)/shard_map/ppermute | solution.py:196
  48.2 1.9 collective-permute-start.2
  50.1 6.4 %collective-permute-start.3 = (bf16[48,5120]{1,0:T(8,128)(2,1)S(1)}, bf16[48,5120]{1,0:T(8,128)(2,1)S(1)}, u32[]{:S(2)}, u32[]{:S(2)}) collective-permute-start(bf16[48,5120]{1,0:T(8,128)(2,1)S(1)} %pad_maximum_fusion), channel_id=1, source_target_pairs={{0,480},{32,0},{64,32},{96,64},{128,96},{160,128},{192,160},{224,1... | collective-permute-start | bytes 1474568 | tf_op jit(solution)/shard_map/ppermute | solution.py:196
  56.6 9.0 %collective-permute-done.2 = bf16[48,5120]{1,0:T(8,128)(2,1)S(1)} collective-permute-done((bf16[48,5120]{1,0:T(8,128)(2,1)S(1)}, bf16[48,5120]{1,0:T(8,128)(2,1)S(1)}, u32[]{:S(2)}, u32[]{:S(2)}) %collective-permute-start.2) | collective-permute-done | bytes 491552 | tf_op jit(solution)/shard_map/ppermute | solution.py:196
  65.6 1.2 collective-permute-done.3
  66.8 6.4 %collective-permute-start.6 = (bf16[16,5120]{1,0:T(8,128)(2,1)S(1)}, bf16[16,5120]{1,0:T(8,128)(2,1)S(1)}, u32[]{:S(2)}, u32[]{:S(2)}) collective-permute-start(bf16[16,5120]{1,0:T(8,128)(2,1)S(1)} %slice_select_fusion), channel_id=1, source_target_pairs={{0,64},{32,96},{64,128},{96,160},{128,192},{160,224},{192,256},{22... | collective-permute-start | bytes 491528 | tf_op jit(solution)/shard_map/ppermute | solution.py:222
  73.2 4.9 %collective-permute-start.4 = (bf16[48,5120]{1,0:T(8,128)(2,1)S(1)}, bf16[48,5120]{1,0:T(8,128)(2,1)S(1)}, u32[]{:S(2)}, u32[]{:S(2)}) collective-permute-start(bf16[48,5120]{1,0:T(8,128)(2,1)S(1)} %collective-permute-done.2), channel_id=1, source_target_pairs={{0,32},{32,64},{64,96},{96,128},{128,160},{160,192},{192,224},{224... | collective-permute-start | bytes 1474568 | tf_op jit(solution)/shard_map/ppermute | solution.py:196
  78.0 2.2 %collective-permute-start.5 = (bf16[48,5120]{1,0:T(8,128)(2,1)S(1)}, bf16[48,5120]{1,0:T(8,128)(2,1)S(1)}, u32[]{:S(2)}, u32[]{:S(2)}) collective-permute-start(bf16[48,5120]{1,0:T(8,128)(2,1)S(1)} %collective-permute-done.3), channel_id=1, source_target_pairs={{0,480},{32,0},{64,32},{96,64},{128,96},{160,128},{192,160},{224,1... | collective-permute-start | bytes 1474568 | tf_op jit(solution)/shard_map/ppermute | solution.py:196
  80.3 0.0 copy-start.6
  80.3 1.9 collective-permute-start.7
  82.3 0.0 collective-permute-done.6
  82.3 5.7 %collective-permute-done.4 = bf16[48,5120]{1,0:T(8,128)(2,1)S(1)} collective-permute-done((bf16[48,5120]{1,0:T(8,128)(2,1)S(1)}, bf16[48,5120]{1,0:T(8,128)(2,1)S(1)}, u32[]{:S(2)}, u32[]{:S(2)}) %collective-permute-start.4) | collective-permute-done | bytes 491552 | tf_op jit(solution)/shard_map/ppermute | solution.py:196
  88.0 1.1 collective-permute-done.5
  89.2 0.0 copy-start.1
  89.2 2.1 %collective-permute-start.8 = (bf16[112,5120]{1,0:T(8,128)(2,1)S(1)}, bf16[112,5120]{1,0:T(8,128)(2,1)}, u32[]{:S(2)}, u32[]{:S(2)}) collective-permute-start(bf16[112,5120]{1,0:T(8,128)(2,1)S(1)} %constant_dynamic-update-slice_fusion.3.refs_1_), channel_id=1, source_target_pairs={{0,16},{16,0},{1,17},{17,1},{2,18},{18,2},{3,19},{19,3},{4,20},{20... | collective-permute-start | bytes 3440648 | tf_op jit(solution)/shard_map/ppermute | solution.py:200
  91.2 0.0 collective-permute-done.7.refs_2_
  91.3 1.2 copy-done.8
  92.5 1.7 collective-permute-done.8.refs_3_
  94.1 0.4 all-to-all-done.1.gated.vectors
  94.5 7.9 %shard_map.87 = (bf16[400,512]{1,0:T(8,128)(2,1)}, bf16[512,5120]{1,0:T(8,128)(2,1)}) custom-call(bf16[384,64]{1,0:T(8,128)(2,1)} %fusion.2.features, bf16[8,480,640]{2,1,0:T(8,128)(2,1)} %all-to-all-done.1.gated.vectors, bf16[8,480,640]{2,1,0:T(8,128)(2,1)} %all-to-all-done.1.gated.vectors, bf16[144,5120]{1,0:T(8,128)(2,1)} %copy-done.6, ...), custom_call_target="tpu_custom_call" | custom-call | flops 2264924160 | bytes 9912320 | tf_op jit(solution)/shard_map/pallas_call | solution.py:285
  102.4 2.6 %collective-permute-start.9 = (bf16[400,512]{1,0:T(8,128)(2,1)}, bf16[400,512]{1,0:T(8,128)(2,1)S(1)}, u32[]{:S(2)}, u32[]{:S(2)}) collective-permute-start(bf16[400,512]{1,0:T(8,128)(2,1)} %get-tuple-element.28.own), channel_id=1, source_target_pairs={{0,3},{3,0},{1,2},{2,1},{4,7},{7,4},{5,6},{6,5},{8,11},{11,8},{9,1... | collective-permute-start | bytes 1228808 | tf_op jit(solution)/shard_map/ppermute | solution.py:187
  105.1 10.6 %collective-permute-done.9.other = bf16[400,512]{1,0:T(8,128)(2,1)S(1)} collective-permute-done((bf16[400,512]{1,0:T(8,128)(2,1)}, bf16[400,512]{1,0:T(8,128)(2,1)S(1)}, u32[]{:S(2)}, u32[]{:S(2)}) %collective-permute-start.9) | collective-permute-done | bytes 409632 | tf_op jit(solution)/shard_map/ppermute | solution.py:187
  115.7 0.0 copy-done.1
  115.7 1.0 copy-done.5
  116.7 7.8 %shard_map.88 = (bf16[8,72,640]{2,1,0:T(8,128)(2,1)}, f32[16,512]{1,0:T(8,128)S(1)}, f32[384,512]{1,0:T(8,128)}) custom-call(bf16[384,64]{1,0:T(8,128)(2,1)S(1)} %copy-done.1, bf16[8,480,640]{2,1,0:T(8,128)(2,1)} %all-to-all-done.1.gated.vectors, bf16[400,512]{1,0:T(8,128)(2,1)S(1)} %copy-done.5, bf16[400,512]{1,0:T(8,128)(2,1)S(1)} %collective-permute-done.9.other, ...), custom_call_target="tpu_custom_call" | custom-call | flops 2264924160 | bytes 9912320 | tf_op jit(solution)/shard_map/pallas_call | solution.py:310
  124.5 6.5 %all-to-all-start.2 = ((bf16[8,72,640]{2,1,0:T(8,128)(2,1)}), bf16[8,72,640]{2,1,0:T(8,128)(2,1)S(1)}, u32[]{:S(2)}, u32[]{:S(2)}) async-start(bf16[8,72,640]{2,1,0:T(8,128)(2,1)} %get-tuple-element.30), calls=%async_computation.2 | async-start | bytes 1474560 | tf_op jit(solution)/shard_map/all_to_all | solution.py:191
  131.7 11.2 %all-to-all-done.2.arrived = bf16[8,72,640]{2,1,0:T(8,128)(2,1)S(1)} async-done(((bf16[8,72,640]{2,1,0:T(8,128)(2,1)}), bf16[8,72,640]{2,1,0:T(8,128)(2,1)S(1)}, u32[]{:S(2)}, u32[]{:S(2)}) %all-to-all-start.2) | async-done | bytes 737312 | tf_op jit(solution)/shard_map/all_to_all | solution.py:191
  142.9 0.9 copy-done.3
  143.9 0.3 shard_map.89
  144.2 14.0 %all_to_all.25.vectors = bf16[8,72,640]{2,1,0:T(8,128)(2,1)} all-to-all(bf16[8,72,640]{2,1,0:T(8,128)(2,1)S(1)} %get-tuple-element.32), channel_id=1, replica_groups=mesh['z'=16,'c'=2,'y'=4,'xa'=2,'xb'=2] {'y','xb'}, dimensions={0} | all-to-all | bytes 1474560 | tf_op jit(solution)/shard_map/all_to_all | solution.py:191
  158.2 5.9 %shard_map.90.own = bf16[400,512]{1,0:T(8,128)(2,1)S(1)} custom-call(bf16[384,64]{1,0:T(8,128)(2,1)S(1)} %copy-done.2, bf16[8,480,640]{2,1,0:T(8,128)(2,1)} %all-to-all-done.1.gated.vectors, bf16[8,72,640]{2,1,0:T(8,128)(2,1)} %all_to_all.25.vectors, bf16[512,5120]{1,0:T(8,128)(2,1)} %get-tuple-element.29.refs_0_.refs_2_), custom_call_target="tpu_custom_call" | custom-call | flops 2264924160 | bytes 9912320 | tf_op jit(solution)/shard_map/pallas_call | solution.py:285
  164.2 1.9 collective-permute-start.10
  166.1 8.5 %collective-permute-done.10.other = bf16[400,512]{1,0:T(8,128)(2,1)S(1)} collective-permute-done((bf16[400,512]{1,0:T(8,128)(2,1)S(1)}, bf16[400,512]{1,0:T(8,128)(2,1)S(1)}, u32[]{:S(2)}, u32[]{:S(2)}) %collective-permute-start.10) | collective-permute-done | bytes 409632 | tf_op jit(solution)/shard_map/ppermute | solution.py:187
  174.6 8.2 %shard_map.91 = (bf16[8,72,640]{2,1,0:T(8,128)(2,1)}, f32[16,512]{1,0:T(8,128)S(1)}) custom-call(bf16[384,64]{1,0:T(8,128)(2,1)S(1)} %copy-done.2, bf16[8,480,640]{2,1,0:T(8,128)(2,1)} %all-to-all-done.1.gated.vectors, bf16[400,512]{1,0:T(8,128)(2,1)S(1)} %shard_map.90.own, bf16[400,512]{1,0:T(8,128)(2,1)S(1)} %collective-permute-done.10.other, ...), custom_call_target="tpu_custom_call" | custom-call | flops 2264924160 | bytes 9912320 | tf_op jit(solution)/shard_map/pallas_call | solution.py:310
  182.7 14.1 %all_to_all.26.arrived = bf16[8,72,640]{2,1,0:T(8,128)(2,1)S(1)} all-to-all(bf16[8,72,640]{2,1,0:T(8,128)(2,1)} %get-tuple-element.34), channel_id=1, replica_groups=mesh['z'=16,'c'=2,'y'=4,'xa'=2,'xb'=2] {'y','xb'}, dimensions={0} | all-to-all | bytes 1474560 | tf_op jit(solution)/shard_map/all_to_all | solution.py:191
  196.9 0.9 shard_map.92
  (20 shorter events, 0.3 us)
Async XLA Ops:
  0.6 30.1 %copy-start = (bf16[1,384,3584]{2,1,0:T(8,128)(2,1)S(1)}, bf16[1,384,3584]{2,1,0:T(8,128)(2,1)}, u32[]{:S(2)}) copy-start(bf16[1,384,3584]{2,1,0:T(8,128)(2,1)} %param.7) | copy-start | bytes 8257540
  2.5 11.9 %all-to-all-start = ((bf16[8,16,640]{2,1,0:T(8,128)(2,1)}), bf16[8,16,640]{2,1,0:T(8,128)(2,1)S(1)}, u32[]{:S(2)}, u32[]{:S(2)}) async-start(bf16[8,16,640]{2,1,0:T(8,128)(2,1)} %pad.4), calls=%async_computation | async-start | bytes 327680 | tf_op jit(solution)/shard_map/all_to_all | solution.py:191
  14.4 23.6 %collective-permute-start = (bf16[16,5120]{1,0:T(8,128)(2,1)S(1)}, bf16[16,5120]{1,0:T(8,128)(2,1)S(1)}, u32[]{:S(2)}, u32[]{:S(2)}) collective-permute-start(bf16[16,5120]{1,0:T(8,128)(2,1)S(1)} %bitcast.22), channel_id=1, source_target_pairs={{0,160},{32,192},{64,224},{96,256},{128,288},{160,320},{192,352},{... | collective-permute-start | bytes 491528 | tf_op jit(solution)/shard_map/ppermute | solution.py:196
  24.9 23.3 %collective-permute-start.1 = (bf16[16,5120]{1,0:T(8,128)(2,1)S(1)}, bf16[16,5120]{1,0:T(8,128)(2,1)S(1)}, u32[]{:S(2)}, u32[]{:S(2)}) collective-permute-start(bf16[16,5120]{1,0:T(8,128)(2,1)S(1)} %bitcast.23), channel_id=1, source_target_pairs={{0,352},{32,384},{64,416},{96,448},{128,480},{160,0},{192,32},{224... | collective-permute-start | bytes 491528 | tf_op jit(solution)/shard_map/ppermute | solution.py:196
  33.3 61.2 %all-to-all-start.1 = ((bf16[8,480,640]{2,1,0:T(8,128)(2,1)}), bf16[8,480,640]{2,1,0:T(8,128)(2,1)}, u32[]{:S(2)}, u32[]{:S(2)}) async-start(bf16[8,480,640]{2,1,0:T(8,128)(2,1)} %shard_map.86), calls=%async_computation.1 | async-start | bytes 9830400 | tf_op jit(solution)/shard_map/all_to_all | solution.py:191
  48.2 17.4 %collective-permute-start.2 = (bf16[48,5120]{1,0:T(8,128)(2,1)S(1)}, bf16[48,5120]{1,0:T(8,128)(2,1)S(1)}, u32[]{:S(2)}, u32[]{:S(2)}) collective-permute-start(bf16[48,5120]{1,0:T(8,128)(2,1)S(1)} %pad_maximum_fusion), channel_id=1, source_target_pairs={{0,32},{32,64},{64,96},{96,128},{128,160},{160,192},{192,224},{224... | collective-permute-start | bytes 1474568 | tf_op jit(solution)/shard_map/ppermute | solution.py:196
  50.1 16.7 %collective-permute-start.3 = (bf16[48,5120]{1,0:T(8,128)(2,1)S(1)}, bf16[48,5120]{1,0:T(8,128)(2,1)S(1)}, u32[]{:S(2)}, u32[]{:S(2)}) collective-permute-start(bf16[48,5120]{1,0:T(8,128)(2,1)S(1)} %pad_maximum_fusion), channel_id=1, source_target_pairs={{0,480},{32,0},{64,32},{96,64},{128,96},{160,128},{192,160},{224,1... | collective-permute-start | bytes 1474568 | tf_op jit(solution)/shard_map/ppermute | solution.py:196
  66.8 15.5 %collective-permute-start.6 = (bf16[16,5120]{1,0:T(8,128)(2,1)S(1)}, bf16[16,5120]{1,0:T(8,128)(2,1)S(1)}, u32[]{:S(2)}, u32[]{:S(2)}) collective-permute-start(bf16[16,5120]{1,0:T(8,128)(2,1)S(1)} %slice_select_fusion), channel_id=1, source_target_pairs={{0,64},{32,96},{64,128},{96,160},{128,192},{160,224},{192,256},{22... | collective-permute-start | bytes 491528 | tf_op jit(solution)/shard_map/ppermute | solution.py:222
  73.2 14.8 %collective-permute-start.4 = (bf16[48,5120]{1,0:T(8,128)(2,1)S(1)}, bf16[48,5120]{1,0:T(8,128)(2,1)S(1)}, u32[]{:S(2)}, u32[]{:S(2)}) collective-permute-start(bf16[48,5120]{1,0:T(8,128)(2,1)S(1)} %collective-permute-done.2), channel_id=1, source_target_pairs={{0,32},{32,64},{64,96},{96,128},{128,160},{160,192},{192,224},{224... | collective-permute-start | bytes 1474568 | tf_op jit(solution)/shard_map/ppermute | solution.py:196
  78.0 11.0 %collective-permute-start.5 = (bf16[48,5120]{1,0:T(8,128)(2,1)S(1)}, bf16[48,5120]{1,0:T(8,128)(2,1)S(1)}, u32[]{:S(2)}, u32[]{:S(2)}) collective-permute-start(bf16[48,5120]{1,0:T(8,128)(2,1)S(1)} %collective-permute-done.3), channel_id=1, source_target_pairs={{0,480},{32,0},{64,32},{96,64},{128,96},{160,128},{192,160},{224,1... | collective-permute-start | bytes 1474568 | tf_op jit(solution)/shard_map/ppermute | solution.py:196
  80.3 8.8 %copy-start.6 = (bf16[144,5120]{1,0:T(8,128)(2,1)}, bf16[144,5120]{1,0:T(8,128)(2,1)S(1)}, u32[]{:S(2)}) copy-start(bf16[144,5120]{1,0:T(8,128)(2,1)S(1)} %constant_dynamic-update-slice_fusion.refs_0_) | copy-start | bytes 4423684
  80.3 10.9 %collective-permute-start.7 = (bf16[144,5120]{1,0:T(8,128)(2,1)S(1)}, bf16[144,5120]{1,0:T(8,128)(2,1)S(1)}, u32[]{:S(2)}, u32[]{:S(2)}) collective-permute-start(bf16[144,5120]{1,0:T(8,128)(2,1)S(1)} %constant_dynamic-update-slice_fusion.refs_0_), channel_id=1, source_target_pairs={{0,16},{16,0},{1,17},{17,1},{2,18},{18,2},{3,19},{19,3},{4,20},{20... | collective-permute-start | bytes 4423688 | tf_op jit(solution)/shard_map/ppermute | solution.py:200
  89.2 2.1 %copy-start.7 = (bf16[112,5120]{1,0:T(8,128)(2,1)}, bf16[112,5120]{1,0:T(8,128)(2,1)S(1)}, u32[]{:S(2)}) copy-start(bf16[112,5120]{1,0:T(8,128)(2,1)S(1)} %constant_dynamic-update-slice_fusion.3.refs_1_) | copy-start | bytes 3440644
  89.2 26.5 %copy-start.1 = (bf16[384,64]{1,0:T(8,128)(2,1)S(1)}, bf16[384,64]{1,0:T(8,128)(2,1)}, u32[]{:S(2)}) copy-start(bf16[384,64]{1,0:T(8,128)(2,1)} %fusion.2.features) | copy-start | bytes 147460
  89.2 5.0 %collective-permute-start.8 = (bf16[112,5120]{1,0:T(8,128)(2,1)S(1)}, bf16[112,5120]{1,0:T(8,128)(2,1)}, u32[]{:S(2)}, u32[]{:S(2)}) collective-permute-start(bf16[112,5120]{1,0:T(8,128)(2,1)S(1)} %constant_dynamic-update-slice_fusion.3.refs_1_), channel_id=1, source_target_pairs={{0,16},{16,0},{1,17},{17,1},{2,18},{18,2},{3,19},{19,3},{4,20},{20... | collective-permute-start | bytes 3440648 | tf_op jit(solution)/shard_map/ppermute | solution.py:200
  91.3 1.2 copy-start.8
  102.4 13.2 %collective-permute-start.9 = (bf16[400,512]{1,0:T(8,128)(2,1)}, bf16[400,512]{1,0:T(8,128)(2,1)S(1)}, u32[]{:S(2)}, u32[]{:S(2)}) collective-permute-start(bf16[400,512]{1,0:T(8,128)(2,1)} %get-tuple-element.28.own), channel_id=1, source_target_pairs={{0,3},{3,0},{1,2},{2,1},{4,7},{7,4},{5,6},{6,5},{8,11},{11,8},{9,1... | collective-permute-start | bytes 1228808 | tf_op jit(solution)/shard_map/ppermute | solution.py:187
  115.7 1.0 copy-start.5
  124.5 18.4 %all-to-all-start.2 = ((bf16[8,72,640]{2,1,0:T(8,128)(2,1)}), bf16[8,72,640]{2,1,0:T(8,128)(2,1)S(1)}, u32[]{:S(2)}, u32[]{:S(2)}) async-start(bf16[8,72,640]{2,1,0:T(8,128)(2,1)} %get-tuple-element.30), calls=%async_computation.2 | async-start | bytes 1474560 | tf_op jit(solution)/shard_map/all_to_all | solution.py:191
  142.9 15.3 %copy-start.2 = (bf16[384,64]{1,0:T(8,128)(2,1)S(1)}, bf16[384,64]{1,0:T(8,128)(2,1)}, u32[]{:S(2)}) copy-start(bf16[384,64]{1,0:T(8,128)(2,1)} %fusion.2.features) | copy-start | bytes 147460
  142.9 1.0 copy-start.3
  164.2 10.4 %collective-permute-start.10 = (bf16[400,512]{1,0:T(8,128)(2,1)S(1)}, bf16[400,512]{1,0:T(8,128)(2,1)S(1)}, u32[]{:S(2)}, u32[]{:S(2)}) collective-permute-start(bf16[400,512]{1,0:T(8,128)(2,1)S(1)} %shard_map.90.own), channel_id=1, source_target_pairs={{0,3},{3,0},{1,2},{2,1},{4,7},{7,4},{5,6},{6,5},{8,11},{11,8},{9,1... | collective-permute-start | bytes 1228808 | tf_op jit(solution)/shard_map/ppermute | solution.py:187
  182.7 14.1 %copy-start.4 = (f32[1,64,640]{2,1,0:T(8,128)S(1)}, f32[1,64,640]{2,1,0:T(8,128)}, u32[]{:S(2)}) copy-start(f32[1,64,640]{2,1,0:T(8,128)} %param.13) | copy-start | bytes 491524

commit v8 on v7

--- a/solution.py
+++ b/solution.py
@@ -139,22 +139,22 @@
         message[j, rank:, :] = pieces
 
 
-def update(rank, live, rate, arrived, grad, tail, message, residual, alpha):
+def update(rank, given, arrived, grad, tail, message, residual, alpha):
     rows = arrived[0].astype(F32)
     for j in range(1, arrived.shape[0]):
         rows = rows + arrived[j].astype(F32)
     g = grad[...]
     shape = (1, g.shape[1])
     norm = everywhere(from_pieces(tail[...], 0), shape)
-    step = norm / (from_pieces(rows[rank:], 0) / live[0] + rate[0] * norm)
-    h = rows[:rank] / live[0] + rate[0] * g
+    step = norm / (from_pieces(rows[rank:], 0) / given[0] + given[1] * norm)
+    h = rows[:rank] / given[0] + given[1] * g
     r = g - step * h
     residual[...] = r
     alpha[...] = jnp.broadcast_to(step, alpha.shape)
     post(message, r.astype(BF16), [total(r * r), total(r * g)], rank)
 
 
-def finish(rank, live, rate, arrived, grad, tail, tail_was, residual, alpha, x, left):
+def finish(rank, given, arrived, grad, tail, tail_was, residual, alpha, x, left):
     rows = arrived[0].astype(F32)
     for j in range(1, arrived.shape[0]):
         rows = rows + arrived[j].astype(F32)
@@ -165,9 +165,9 @@
     norm_was = everywhere(from_pieces(tail_was[...], 0), shape)
     ratio = norm / norm_was
     length = norm + ratio * (2.0 * cross + ratio * norm_was)
-    step = norm / (from_pieces(rows[rank:], 0) / live[0] + rate[0] * length)
+    step = norm / (from_pieces(rows[rank:], 0) / given[0] + given[1] * length)
     d = r + ratio * g
-    h = rows[:rank] / live[0] + rate[0] * d
+    h = rows[:rank] / given[0] + given[1] * d
     x[...] = alpha[:1, :] * g + step * d
     left[...] = r - step * h
 
@@ -261,14 +261,14 @@
     below, above = shifted(mine, 5), shifted(mine, -5)
     features = jnp.dot(support_x[0], adapter_a[0], preferred_element_type=F32).astype(BF16)
     near = jnp.concatenate([mine, below, above], axis=0)
-    near, features = lax.optimization_barrier((near, features))
+    scalars = jnp.concatenate([lengths.astype(F32), damping])
+    near, features, scalars = lax.optimization_barrier((near, features, scalars))
     pieces = all_blocks(near)
     width = sum(piece.shape[0] for piece in pieces)
 
     def block_weights(array, together):
         return pl.BlockSpec((array.shape[0], together * units), lambda i: (0, i))
 
-    live = lengths.astype(F32)
     flops = 2 * tokens * units * members * (width + rank)
     moved = 2 * units * members * (tokens + width + rows)
 
@@ -336,22 +336,22 @@
     message, residual, alpha = pl.pallas_call(
         functools.partial(update, rank),
         grid=(1,),
-        in_specs=[SCALAR, SCALAR, full_message, full_state, tail],
+        in_specs=[SCALAR, full_message, full_state, tail],
         out_specs=[full_message, full_state, full_alpha],
         out_shape=[message_shape, state, jax.ShapeDtypeStruct((8, units), F32)],
         compiler_params=params(8),
-    )(live, damping, arrived, target, rows_first)
+    )(scalars, arrived, target, rows_first)
     shares, _ = mixed_shares(exchanged(message), [weights])
     arrived, rows_second = product_shares(weights, *shares, first, rows_first)
     x, left = pl.pallas_call(
         functools.partial(finish, rank),
         grid=(1,),
-        in_specs=[SCALAR, SCALAR, full_message, full_state, tail, tail]
+        in_specs=[SCALAR, full_message, full_state, tail, tail]
         + [full_state, full_alpha],
         out_specs=[full_state, full_state],
         out_shape=[state, state],
         compiler_params=params(8),
-    )(live, damping, arrived, target, rows_second, rows_first, residual, alpha)
+    )(scalars, arrived, target, rows_second, rows_first, residual, alpha)
     return (x[None], left[None])
 
 

time: 199 us -> 201 us (1.010)
  blocking collectives: 28.1 us -> 46.9 us
  starting transfers between devices: 63.1 us -> 50 us
  waiting for transfers between devices: 60.3 us -> 56.4 us
    all_to_all x2 -> x3, blocking collectives: 28.1 us -> 46.9 us  [exchanged(): return lax.all_to_all(array, HALF, split_axis=0, concat_axis=0, tiled=True)]
    all_to_all x3 -> x2, waiting for transfers between devices: 12.5 us -> 0.9 us  [exchanged(): return lax.all_to_all(array, HALF, split_axis=0, concat_axis=0, tiled=True)]
    ppermute x6, waiting for transfers between devices: 27 us -> 34.4 us  [shifted(): return lax.ppermute(array, 'z', [(i, (i + by) % size) for i in range(size)])]
    all_to_all x3 -> x2, starting transfers between devices: 16.4 us -> 9.92 us  [exchanged(): return lax.all_to_all(array, HALF, split_axis=0, concat_axis=0, tiled=True)]
    ppermute x1, starting transfers between devices: 6.37 us -> 2.16 us  [all_blocks(): last = lax.ppermute(far, ('z', 'c'), both_ways)]
    ppermute x6, starting transfers between devices: 31.7 us -> 28.9 us  [shifted(): return lax.ppermute(array, 'z', [(i, (i + by) % size) for i in range(size)])]
  transfers between devices with their start and end apart: 14 -> 13, of which waited for: 11 -> 11; matrix products, arithmetic and copies ran while one was open for 1% -> 1% of each run, Pallas kernels for 3% -> 3%
where the time goes in v8:
time: 201 us; the launch traced here: 200 us
  waiting for transfers between devices  56.4 us (28%)
  starting transfers between devices  50 us (25%)
  blocking collectives  46.9 us (23%)
  Pallas kernels  37.5 us (19%)
  local copies, waits for them, and re-layouts  4.2 us (2%)
  matrix products  2.51 us (1%)
  between operations  2.19 us (1%)
    all_to_all x3, blocking collectives, exchanged(): return lax.all_to_all(array, HALF, split_axis=0, concat_axis=0, tiled=True)  46.9 us
    ppermute x6, waiting for transfers between devices, shifted(): return lax.ppermute(array, 'z', [(i, (i + by) % size) for i in range(size)])  34.4 us
    ppermute x6, starting transfers between devices, shifted(): return lax.ppermute(array, 'z', [(i, (i + by) % size) for i in range(size)])  28.9 us
    ppermute x2, waiting for transfers between devices, swapped(): return lax.ppermute(array, ROW, [(0, 3), (3, 0), (1, 2), (2, 1)])  18.9 us
    pallas_call x2, Pallas kernels, product_shares(): pl.pallas_call(functools.partial(backward, rank, bool(before)), grid=(mem...  16 us
    pallas_call x2, Pallas kernels, mixed_shares(): pl.pallas_call(functools.partial(forward, rank, len(pieces)), grid=(membe...  13.9 us
    all_to_all x2, starting transfers between devices, exchanged(): return lax.all_to_all(array, HALF, split_axis=0, concat_axis=0, tiled=True)  9.92 us
    pallas_call x1, Pallas kernels, shards(): pl.pallas_call(pack, grid=(members,), in_specs=[SCALAR, whole((tokens, un...  5.28 us
  transfers between devices with their start and end apart: 13, of which 11 were waited for; matrix products, arithmetic and copies ran while one was open for 1% of the time, Pallas kernels for 3%

profile of v8, /device:TPU:4, one launch (start us, length us, event | category | flops | bytes accessed | tf_op | source)
XLA Modules:
  0.0 199.9 jit_solution(18430875197157328317)
XLA Ops:
  0.6 0.0 copy-start
  0.7 1.1 reshape.13
  1.8 0.7 pad.4
  2.5 5.1 %all-to-all-start = ((bf16[8,16,640]{2,1,0:T(8,128)(2,1)}), bf16[8,16,640]{2,1,0:T(8,128)(2,1)S(1)}, u32[]{:S(2)}, u32[]{:S(2)}) async-start(bf16[8,16,640]{2,1,0:T(8,128)(2,1)} %pad.4), calls=%async_computation | async-start | bytes 327680 | tf_op jit(solution)/shard_map/all_to_all | solution.py:191
  8.2 5.3 %shard_map.86 = bf16[8,480,640]{2,1,0:T(8,128)(2,1)} custom-call(s32[1]{0:T(128)S(6)} %copy.21.live, bf16[384,640]{1,0:T(8,128)(2,1)} %bitcast.25, f32[64,640]{1,0:T(8,128)} %bitcast.17), custom_call_target="tpu_custom_call" | custom-call | flops 1966080 | bytes 4915200 | tf_op jit(solution)/shard_map/pallas_call | solution.py:244
  13.5 0.9 all-to-all-done
  14.4 14.4 %collective-permute-start.1 = (bf16[16,5120]{1,0:T(8,128)(2,1)S(1)}, bf16[16,5120]{1,0:T(8,128)(2,1)S(1)}, u32[]{:S(2)}, u32[]{:S(2)}) collective-permute-start(bf16[16,5120]{1,0:T(8,128)(2,1)S(1)} %bitcast.22), channel_id=1, source_target_pairs={{0,352},{32,384},{64,416},{96,448},{128,480},{160,0},{192,32},{224... | collective-permute-start | bytes 491528 | tf_op jit(solution)/shard_map/ppermute | solution.py:196
  28.8 1.9 collective-permute-start
  30.8 0.0 copy-done
  30.8 2.5 %fusion.2.features = bf16[384,64]{1,0:T(8,128)(2,1)} fusion(bf16[1,384,3584]{2,1,0:T(8,128)(2,1)S(1)} %copy-done, bf16[1,3584,64]{1,2,0:T(8,128)(2,1)} %param.8), kind=kOutput, calls=%fused_computation.2 | convolution fusion | flops 176185344 | bytes 3260416 | tf_op jit(solution)/shard_map/dot_general | solution.py:262
  33.9 0.1 pad_maximum_fusion.1.given
  34.0 4.8 %all-to-all-start.1 = ((bf16[8,480,640]{2,1,0:T(8,128)(2,1)}), bf16[8,480,640]{2,1,0:T(8,128)(2,1)}, u32[]{:S(2)}, u32[]{:S(2)}) async-start(bf16[8,480,640]{2,1,0:T(8,128)(2,1)} %shard_map.86), calls=%async_computation.1 | async-start | bytes 9830400 | tf_op jit(solution)/shard_map/all_to_all | solution.py:191
  38.8 5.8 %collective-permute-done.1 = bf16[16,5120]{1,0:T(8,128)(2,1)S(1)} collective-permute-done((bf16[16,5120]{1,0:T(8,128)(2,1)S(1)}, bf16[16,5120]{1,0:T(8,128)(2,1)S(1)}, u32[]{:S(2)}, u32[]{:S(2)}) %collective-permute-start.1) | collective-permute-done | bytes 163872 | tf_op jit(solution)/shard_map/ppermute | solution.py:196
  44.6 10.0 %collective-permute-done = bf16[16,5120]{1,0:T(8,128)(2,1)S(1)} collective-permute-done((bf16[16,5120]{1,0:T(8,128)(2,1)S(1)}, bf16[16,5120]{1,0:T(8,128)(2,1)S(1)}, u32[]{:S(2)}, u32[]{:S(2)}) %collective-permute-start) | collective-permute-done | bytes 163872 | tf_op jit(solution)/shard_map/ppermute | solution.py:196
  54.6 2.4 %collective-permute-start.3 = (bf16[48,5120]{1,0:T(8,128)(2,1)S(1)}, bf16[48,5120]{1,0:T(8,128)(2,1)S(1)}, u32[]{:S(2)}, u32[]{:S(2)}) collective-permute-start(bf16[48,5120]{1,0:T(8,128)(2,1)S(1)} %pad_maximum_fusion), channel_id=1, source_target_pairs={{0,480},{32,0},{64,32},{96,64},{128,96},{160,128},{192,160},{224,1... | collective-permute-start | bytes 1474568 | tf_op jit(solution)/shard_map/ppermute | solution.py:196
  57.0 3.4 %collective-permute-start.2 = (bf16[48,5120]{1,0:T(8,128)(2,1)S(1)}, bf16[48,5120]{1,0:T(8,128)(2,1)S(1)}, u32[]{:S(2)}, u32[]{:S(2)}) collective-permute-start(bf16[48,5120]{1,0:T(8,128)(2,1)S(1)} %pad_maximum_fusion), channel_id=1, source_target_pairs={{0,32},{32,64},{64,96},{96,128},{128,160},{160,192},{192,224},{224... | collective-permute-start | bytes 1474568 | tf_op jit(solution)/shard_map/ppermute | solution.py:196
  60.5 4.8 %collective-permute-done.3 = bf16[48,5120]{1,0:T(8,128)(2,1)S(1)} collective-permute-done((bf16[48,5120]{1,0:T(8,128)(2,1)S(1)}, bf16[48,5120]{1,0:T(8,128)(2,1)S(1)}, u32[]{:S(2)}, u32[]{:S(2)}) %collective-permute-start.3) | collective-permute-done | bytes 491552 | tf_op jit(solution)/shard_map/ppermute | solution.py:196
  65.3 3.6 %collective-permute-done.2 = bf16[48,5120]{1,0:T(8,128)(2,1)S(1)} collective-permute-done((bf16[48,5120]{1,0:T(8,128)(2,1)S(1)}, bf16[48,5120]{1,0:T(8,128)(2,1)S(1)}, u32[]{:S(2)}, u32[]{:S(2)}) %collective-permute-start.2) | collective-permute-done | bytes 491552 | tf_op jit(solution)/shard_map/ppermute | solution.py:196
  69.0 2.2 %collective-permute-start.6 = (bf16[16,5120]{1,0:T(8,128)(2,1)S(1)}, bf16[16,5120]{1,0:T(8,128)(2,1)S(1)}, u32[]{:S(2)}, u32[]{:S(2)}) collective-permute-start(bf16[16,5120]{1,0:T(8,128)(2,1)S(1)} %slice_select_fusion), channel_id=1, source_target_pairs={{0,64},{32,96},{64,128},{96,160},{128,192},{160,224},{192,256},{22... | collective-permute-start | bytes 491528 | tf_op jit(solution)/shard_map/ppermute | solution.py:222
  71.2 4.6 %collective-permute-start.5 = (bf16[48,5120]{1,0:T(8,128)(2,1)S(1)}, bf16[48,5120]{1,0:T(8,128)(2,1)S(1)}, u32[]{:S(2)}, u32[]{:S(2)}) collective-permute-start(bf16[48,5120]{1,0:T(8,128)(2,1)S(1)} %collective-permute-done.3), channel_id=1, source_target_pairs={{0,480},{32,0},{64,32},{96,64},{128,96},{160,128},{192,160},{224,1... | collective-permute-start | bytes 1474568 | tf_op jit(solution)/shard_map/ppermute | solution.py:196
  75.8 2.1 %collective-permute-start.4 = (bf16[48,5120]{1,0:T(8,128)(2,1)S(1)}, bf16[48,5120]{1,0:T(8,128)(2,1)S(1)}, u32[]{:S(2)}, u32[]{:S(2)}) collective-permute-start(bf16[48,5120]{1,0:T(8,128)(2,1)S(1)} %collective-permute-done.2), channel_id=1, source_target_pairs={{0,32},{32,64},{64,96},{96,128},{128,160},{160,192},{192,224},{224... | collective-permute-start | bytes 1474568 | tf_op jit(solution)/shard_map/ppermute | solution.py:196
  78.0 0.0 copy-start.4
  78.0 1.9 collective-permute-start.7
  80.0 0.5 collective-permute-done.6
  80.5 6.6 %collective-permute-done.5 = bf16[48,5120]{1,0:T(8,128)(2,1)S(1)} collective-permute-done((bf16[48,5120]{1,0:T(8,128)(2,1)S(1)}, bf16[48,5120]{1,0:T(8,128)(2,1)S(1)}, u32[]{:S(2)}, u32[]{:S(2)}) %collective-permute-start.5) | collective-permute-done | bytes 491552 | tf_op jit(solution)/shard_map/ppermute | solution.py:196
  87.0 3.6 %collective-permute-done.4 = bf16[48,5120]{1,0:T(8,128)(2,1)S(1)} collective-permute-done((bf16[48,5120]{1,0:T(8,128)(2,1)S(1)}, bf16[48,5120]{1,0:T(8,128)(2,1)S(1)}, u32[]{:S(2)}, u32[]{:S(2)}) %collective-permute-start.4) | collective-permute-done | bytes 491552 | tf_op jit(solution)/shard_map/ppermute | solution.py:196
  90.7 0.0 copy-done.4
  90.7 0.0 copy-start.5
  90.8 0.0 copy-start.1
  90.8 2.1 %collective-permute-start.8 = (bf16[112,5120]{1,0:T(8,128)(2,1)S(1)}, bf16[112,5120]{1,0:T(8,128)(2,1)}, u32[]{:S(2)}, u32[]{:S(2)}) collective-permute-start(bf16[112,5120]{1,0:T(8,128)(2,1)S(1)} %constant_dynamic-update-slice_fusion.3.refs_1_), channel_id=1, source_target_pairs={{0,16},{16,0},{1,17},{17,1},{2,18},{18,2},{3,19},{19,3},{4,20},{20... | collective-permute-start | bytes 3440648 | tf_op jit(solution)/shard_map/ppermute | solution.py:200
  92.8 0.0 collective-permute-done.7.refs_2_
  92.9 1.2 copy-done.6
  94.0 1.7 collective-permute-done.8.refs_3_
  95.7 0.0 all-to-all-done.1.gated.vectors
  95.7 7.9 %shard_map.87 = (bf16[400,512]{1,0:T(8,128)(2,1)}, bf16[512,5120]{1,0:T(8,128)(2,1)}) custom-call(bf16[384,64]{1,0:T(8,128)(2,1)} %fusion.2.features, bf16[8,480,640]{2,1,0:T(8,128)(2,1)} %all-to-all-done.1.gated.vectors, bf16[8,480,640]{2,1,0:T(8,128)(2,1)} %all-to-all-done.1.gated.vectors, bf16[144,5120]{1,0:T(8,128)(2,1)} %copy-done.4, ...), custom_call_target="tpu_custom_call" | custom-call | flops 2264924160 | bytes 9912320 | tf_op jit(solution)/shard_map/pallas_call | solution.py:285
  103.7 3.1 %collective-permute-start.9 = (bf16[400,512]{1,0:T(8,128)(2,1)}, bf16[400,512]{1,0:T(8,128)(2,1)S(1)}, u32[]{:S(2)}, u32[]{:S(2)}) collective-permute-start(bf16[400,512]{1,0:T(8,128)(2,1)} %get-tuple-element.30.own), channel_id=1, source_target_pairs={{0,3},{3,0},{1,2},{2,1},{4,7},{7,4},{5,6},{6,5},{8,11},{11,8},{9,1... | collective-permute-start | bytes 1228808 | tf_op jit(solution)/shard_map/ppermute | solution.py:187
  106.8 10.4 %collective-permute-done.9.other = bf16[400,512]{1,0:T(8,128)(2,1)S(1)} collective-permute-done((bf16[400,512]{1,0:T(8,128)(2,1)}, bf16[400,512]{1,0:T(8,128)(2,1)S(1)}, u32[]{:S(2)}, u32[]{:S(2)}) %collective-permute-start.9) | collective-permute-done | bytes 409632 | tf_op jit(solution)/shard_map/ppermute | solution.py:187
  117.3 1.0 copy-done.3
  118.3 7.9 %shard_map.88 = (bf16[8,72,640]{2,1,0:T(8,128)(2,1)}, f32[16,512]{1,0:T(8,128)S(1)}, f32[384,512]{1,0:T(8,128)}) custom-call(bf16[384,64]{1,0:T(8,128)(2,1)S(1)} %copy-done.1, bf16[8,480,640]{2,1,0:T(8,128)(2,1)} %all-to-all-done.1.gated.vectors, bf16[400,512]{1,0:T(8,128)(2,1)S(1)} %copy-done.3, bf16[400,512]{1,0:T(8,128)(2,1)S(1)} %collective-permute-done.9.other, ...), custom_call_target="tpu_custom_call" | custom-call | flops 2264924160 | bytes 9912320 | tf_op jit(solution)/shard_map/pallas_call | solution.py:310
  126.1 18.8 %all_to_all.25.arrived = bf16[8,72,640]{2,1,0:T(8,128)(2,1)S(1)} all-to-all(bf16[8,72,640]{2,1,0:T(8,128)(2,1)} %get-tuple-element.32), channel_id=1, replica_groups=mesh['z'=16,'c'=2,'y'=4,'xa'=2,'xb'=2] {'y','xb'}, dimensions={0} | all-to-all | bytes 1474560 | tf_op jit(solution)/shard_map/all_to_all | solution.py:191
  145.0 0.8 shard_map.89
  145.8 14.0 %all_to_all.26.vectors = bf16[8,72,640]{2,1,0:T(8,128)(2,1)} all-to-all(bf16[8,72,640]{2,1,0:T(8,128)(2,1)S(1)} %get-tuple-element.34), channel_id=1, replica_groups=mesh['z'=16,'c'=2,'y'=4,'xa'=2,'xb'=2] {'y','xb'}, dimensions={0} | all-to-all | bytes 1474560 | tf_op jit(solution)/shard_map/all_to_all | solution.py:191
  159.8 6.0 %shard_map.90.own = bf16[400,512]{1,0:T(8,128)(2,1)S(1)} custom-call(bf16[384,64]{1,0:T(8,128)(2,1)S(1)} %copy-done.1, bf16[8,480,640]{2,1,0:T(8,128)(2,1)} %all-to-all-done.1.gated.vectors, bf16[8,72,640]{2,1,0:T(8,128)(2,1)} %all_to_all.26.vectors, bf16[512,5120]{1,0:T(8,128)(2,1)} %get-tuple-element.31.refs_0_.refs_2_), custom_call_target="tpu_custom_call" | custom-call | flops 2264924160 | bytes 9912320 | tf_op jit(solution)/shard_map/pallas_call | solution.py:285
  165.8 1.9 collective-permute-start.10
  167.7 8.5 %collective-permute-done.10.other = bf16[400,512]{1,0:T(8,128)(2,1)S(1)} collective-permute-done((bf16[400,512]{1,0:T(8,128)(2,1)S(1)}, bf16[400,512]{1,0:T(8,128)(2,1)S(1)}, u32[]{:S(2)}, u32[]{:S(2)}) %collective-permute-start.10) | collective-permute-done | bytes 409632 | tf_op jit(solution)/shard_map/ppermute | solution.py:187
  176.2 8.2 %shard_map.91 = (bf16[8,72,640]{2,1,0:T(8,128)(2,1)}, f32[16,512]{1,0:T(8,128)S(1)}) custom-call(bf16[384,64]{1,0:T(8,128)(2,1)S(1)} %copy-done.1, bf16[8,480,640]{2,1,0:T(8,128)(2,1)} %all-to-all-done.1.gated.vectors, bf16[400,512]{1,0:T(8,128)(2,1)S(1)} %shard_map.90.own, bf16[400,512]{1,0:T(8,128)(2,1)S(1)} %collective-permute-done.10.other, ...), custom_call_target="tpu_custom_call" | custom-call | flops 2264924160 | bytes 9912320 | tf_op jit(solution)/shard_map/pallas_call | solution.py:310
  184.4 14.0 %all_to_all.27.arrived = bf16[8,72,640]{2,1,0:T(8,128)(2,1)S(1)} all-to-all(bf16[8,72,640]{2,1,0:T(8,128)(2,1)} %get-tuple-element.36), channel_id=1, replica_groups=mesh['z'=16,'c'=2,'y'=4,'xa'=2,'xb'=2] {'y','xb'}, dimensions={0} | all-to-all | bytes 1474560 | tf_op jit(solution)/shard_map/all_to_all | solution.py:191
  198.4 1.5 shard_map.92
  (16 shorter events, 0.3 us)
Async XLA Ops:
  0.6 30.1 %copy-start = (bf16[1,384,3584]{2,1,0:T(8,128)(2,1)S(1)}, bf16[1,384,3584]{2,1,0:T(8,128)(2,1)}, u32[]{:S(2)}) copy-start(bf16[1,384,3584]{2,1,0:T(8,128)(2,1)} %param.7) | copy-start | bytes 8257540
  2.5 11.9 %all-to-all-start = ((bf16[8,16,640]{2,1,0:T(8,128)(2,1)}), bf16[8,16,640]{2,1,0:T(8,128)(2,1)S(1)}, u32[]{:S(2)}, u32[]{:S(2)}) async-start(bf16[8,16,640]{2,1,0:T(8,128)(2,1)} %pad.4), calls=%async_computation | async-start | bytes 327680 | tf_op jit(solution)/shard_map/all_to_all | solution.py:191
  14.4 30.2 %collective-permute-start.1 = (bf16[16,5120]{1,0:T(8,128)(2,1)S(1)}, bf16[16,5120]{1,0:T(8,128)(2,1)S(1)}, u32[]{:S(2)}, u32[]{:S(2)}) collective-permute-start(bf16[16,5120]{1,0:T(8,128)(2,1)S(1)} %bitcast.22), channel_id=1, source_target_pairs={{0,352},{32,384},{64,416},{96,448},{128,480},{160,0},{192,32},{224... | collective-permute-start | bytes 491528 | tf_op jit(solution)/shard_map/ppermute | solution.py:196
  28.8 25.7 %collective-permute-start = (bf16[16,5120]{1,0:T(8,128)(2,1)S(1)}, bf16[16,5120]{1,0:T(8,128)(2,1)S(1)}, u32[]{:S(2)}, u32[]{:S(2)}) collective-permute-start(bf16[16,5120]{1,0:T(8,128)(2,1)S(1)} %bitcast.23), channel_id=1, source_target_pairs={{0,160},{32,192},{64,224},{96,256},{128,288},{160,320},{192,352},{... | collective-permute-start | bytes 491528 | tf_op jit(solution)/shard_map/ppermute | solution.py:196
  34.0 61.7 %all-to-all-start.1 = ((bf16[8,480,640]{2,1,0:T(8,128)(2,1)}), bf16[8,480,640]{2,1,0:T(8,128)(2,1)}, u32[]{:S(2)}, u32[]{:S(2)}) async-start(bf16[8,480,640]{2,1,0:T(8,128)(2,1)} %shard_map.86), calls=%async_computation.1 | async-start | bytes 9830400 | tf_op jit(solution)/shard_map/all_to_all | solution.py:191
  54.6 10.7 %collective-permute-start.3 = (bf16[48,5120]{1,0:T(8,128)(2,1)S(1)}, bf16[48,5120]{1,0:T(8,128)(2,1)S(1)}, u32[]{:S(2)}, u32[]{:S(2)}) collective-permute-start(bf16[48,5120]{1,0:T(8,128)(2,1)S(1)} %pad_maximum_fusion), channel_id=1, source_target_pairs={{0,480},{32,0},{64,32},{96,64},{128,96},{160,128},{192,160},{224,1... | collective-permute-start | bytes 1474568 | tf_op jit(solution)/shard_map/ppermute | solution.py:196
  57.0 11.9 %collective-permute-start.2 = (bf16[48,5120]{1,0:T(8,128)(2,1)S(1)}, bf16[48,5120]{1,0:T(8,128)(2,1)S(1)}, u32[]{:S(2)}, u32[]{:S(2)}) collective-permute-start(bf16[48,5120]{1,0:T(8,128)(2,1)S(1)} %pad_maximum_fusion), channel_id=1, source_target_pairs={{0,32},{32,64},{64,96},{96,128},{128,160},{160,192},{192,224},{224... | collective-permute-start | bytes 1474568 | tf_op jit(solution)/shard_map/ppermute | solution.py:196
  69.0 11.5 %collective-permute-start.6 = (bf16[16,5120]{1,0:T(8,128)(2,1)S(1)}, bf16[16,5120]{1,0:T(8,128)(2,1)S(1)}, u32[]{:S(2)}, u32[]{:S(2)}) collective-permute-start(bf16[16,5120]{1,0:T(8,128)(2,1)S(1)} %slice_select_fusion), channel_id=1, source_target_pairs={{0,64},{32,96},{64,128},{96,160},{128,192},{160,224},{192,256},{22... | collective-permute-start | bytes 491528 | tf_op jit(solution)/shard_map/ppermute | solution.py:222
  71.2 15.9 %collective-permute-start.5 = (bf16[48,5120]{1,0:T(8,128)(2,1)S(1)}, bf16[48,5120]{1,0:T(8,128)(2,1)S(1)}, u32[]{:S(2)}, u32[]{:S(2)}) collective-permute-start(bf16[48,5120]{1,0:T(8,128)(2,1)S(1)} %collective-permute-done.3), channel_id=1, source_target_pairs={{0,480},{32,0},{64,32},{96,64},{128,96},{160,128},{192,160},{224,1... | collective-permute-start | bytes 1474568 | tf_op jit(solution)/shard_map/ppermute | solution.py:196
  75.8 14.8 %collective-permute-start.4 = (bf16[48,5120]{1,0:T(8,128)(2,1)S(1)}, bf16[48,5120]{1,0:T(8,128)(2,1)S(1)}, u32[]{:S(2)}, u32[]{:S(2)}) collective-permute-start(bf16[48,5120]{1,0:T(8,128)(2,1)S(1)} %collective-permute-done.2), channel_id=1, source_target_pairs={{0,32},{32,64},{64,96},{96,128},{128,160},{160,192},{192,224},{224... | collective-permute-start | bytes 1474568 | tf_op jit(solution)/shard_map/ppermute | solution.py:196
  78.0 12.7 %copy-start.4 = (bf16[144,5120]{1,0:T(8,128)(2,1)}, bf16[144,5120]{1,0:T(8,128)(2,1)S(1)}, u32[]{:S(2)}) copy-start(bf16[144,5120]{1,0:T(8,128)(2,1)S(1)} %constant_dynamic-update-slice_fusion.refs_0_) | copy-start | bytes 4423684
  78.0 14.8 %collective-permute-start.7 = (bf16[144,5120]{1,0:T(8,128)(2,1)S(1)}, bf16[144,5120]{1,0:T(8,128)(2,1)S(1)}, u32[]{:S(2)}, u32[]{:S(2)}) collective-permute-start(bf16[144,5120]{1,0:T(8,128)(2,1)S(1)} %constant_dynamic-update-slice_fusion.refs_0_), channel_id=1, source_target_pairs={{0,16},{16,0},{1,17},{17,1},{2,18},{18,2},{3,19},{19,3},{4,20},{20... | collective-permute-start | bytes 4423688 | tf_op jit(solution)/shard_map/ppermute | solution.py:200
  90.7 2.1 %copy-start.5 = (bf16[112,5120]{1,0:T(8,128)(2,1)}, bf16[112,5120]{1,0:T(8,128)(2,1)S(1)}, u32[]{:S(2)}) copy-start(bf16[112,5120]{1,0:T(8,128)(2,1)S(1)} %constant_dynamic-update-slice_fusion.3.refs_1_) | copy-start | bytes 3440644
  90.8 26.5 %copy-start.1 = (bf16[384,64]{1,0:T(8,128)(2,1)S(1)}, bf16[384,64]{1,0:T(8,128)(2,1)}, u32[]{:S(2)}) copy-start(bf16[384,64]{1,0:T(8,128)(2,1)} %fusion.2.features) | copy-start | bytes 147460
  90.8 5.0 %collective-permute-start.8 = (bf16[112,5120]{1,0:T(8,128)(2,1)S(1)}, bf16[112,5120]{1,0:T(8,128)(2,1)}, u32[]{:S(2)}, u32[]{:S(2)}) collective-permute-start(bf16[112,5120]{1,0:T(8,128)(2,1)S(1)} %constant_dynamic-update-slice_fusion.3.refs_1_), channel_id=1, source_target_pairs={{0,16},{16,0},{1,17},{17,1},{2,18},{18,2},{3,19},{19,3},{4,20},{20... | collective-permute-start | bytes 3440648 | tf_op jit(solution)/shard_map/ppermute | solution.py:200
  92.8 1.2 copy-start.6
  103.7 13.6 %collective-permute-start.9 = (bf16[400,512]{1,0:T(8,128)(2,1)}, bf16[400,512]{1,0:T(8,128)(2,1)S(1)}, u32[]{:S(2)}, u32[]{:S(2)}) collective-permute-start(bf16[400,512]{1,0:T(8,128)(2,1)} %get-tuple-element.30.own), channel_id=1, source_target_pairs={{0,3},{3,0},{1,2},{2,1},{4,7},{7,4},{5,6},{6,5},{8,11},{11,8},{9,1... | collective-permute-start | bytes 1228808 | tf_op jit(solution)/shard_map/ppermute | solution.py:187
  117.3 1.0 copy-start.3
  126.1 18.9 %copy-start.2 = (f32[1,64,640]{2,1,0:T(8,128)S(1)}, f32[1,64,640]{2,1,0:T(8,128)}, u32[]{:S(2)}) copy-start(f32[1,64,640]{2,1,0:T(8,128)} %param.13) | copy-start | bytes 491524
  165.8 10.4 %collective-permute-start.10 = (bf16[400,512]{1,0:T(8,128)(2,1)S(1)}, bf16[400,512]{1,0:T(8,128)(2,1)S(1)}, u32[]{:S(2)}, u32[]{:S(2)}) collective-permute-start(bf16[400,512]{1,0:T(8,128)(2,1)S(1)} %shard_map.90.own), channel_id=1, source_target_pairs={{0,3},{3,0},{1,2},{2,1},{4,7},{7,4},{5,6},{6,5},{8,11},{11,8},{9,1... | collective-permute-start | bytes 1228808 | tf_op jit(solution)/shard_map/ppermute | solution.py:187
